TPU v7x, 32 devices: a whole 2x2x4 slice. The times are simulated.
32 devices in a mesh: stripe: 2 (over x), row: 8 (over z, y), col: 2 (over core).
Axes of the slice: x: 2, y: 2, z: 4, core: 2. Of those that a mesh axis runs over, the one named last changes fastest.
Arguments:
- coverage: int32 [4096, 4096], P(('stripe', 'row'), 'col'), parts along dimension 0, may hold values from 0 to 255
- fog_rows: float32 [8, 8], replicated, may hold values from 0.02 to 50
- fog_cols: float32 [16, 16], replicated, may hold values from 0.02 to 50
Outputs:
- dose: float32 [4096, 4096], P(('stripe', 'row'), 'col'), parts along dimension 0
There are 2 independent parts, one for each index of `stripe`. A program takes and returns all parts, laid end to end along the dimension named above; an argument that names none is the same for every part. Nothing has to cross between parts.
All inputs are finite; a program needn't handle non-finite values.
Results may differ from a plain program's by a relative error of at most 0.0001.
Values sent between devices are 32-bit elements; how exact they have to be, the bound alone decides.
No kernel may reach another device: no remote copies, remote signals or barrier semaphores. Data moves between devices by JAX's collectives and lax.ppermute only.
A program may use at most 64 MiB of HBM per device.

v0:
```python
import math

import jax
import jax.numpy as jnp
from jax import lax
from jax.sharding import PartitionSpec as P

BS = 32
FB = 256
HALO = 4
BSIG = 16
REACH = 40
PASSES = 2


def extended(value, sides, width):
    for axis, dim in sides:
        count, length = (lax.axis_size(axis), value.shape[dim])
        up = [(i, (i + 1) % count) for i in range(count - 1)]
        down = [(j, i) for i, j in up]
        last = lax.slice_in_dim(value, length - width, length, axis=dim)
        initial = lax.slice_in_dim(value, 0, width, axis=dim)
        before = lax.ppermute(last, axis, up)
        after = lax.ppermute(initial, axis, down)
        value = jnp.concatenate([before, value, after], axis=dim)
    return value


def fine_taps():
    offsets = jnp.arange(-HALO, HALO + 1).astype(jnp.float32)
    raw = jnp.exp(-0.5 * (offsets / 1.25) ** 2)
    return raw / jnp.sum(raw)


def blur_padded(padded, rows, cols):
    taps = fine_taps()
    across = taps[0] * padded[0:rows, :]
    for index in range(1, 2 * HALO + 1):
        across = across + taps[index] * padded[index : index + rows, :]
    result = taps[0] * across[:, 0:cols]
    for index in range(1, 2 * HALO + 1):
        result = result + taps[index] * across[:, index : index + cols]
    return result


def block_mean(field, size):
    rows, cols = field.shape
    return field.reshape(rows // size, size, cols // size, size).sum(axis=(1, 3)) / (size * size)


def spread_add(field, small, size, weight):
    rows, cols = field.shape
    return (
        field.reshape(rows // size, size, cols // size, size) + weight * small[:, None, :, None]
    ).reshape(rows, cols)


def gauss_matrix(first, second):
    offsets = (first[:, None] - second[None, :]).astype(jnp.float32)
    values = jnp.exp(-0.5 * (offsets / BSIG) ** 2) / (BSIG * math.sqrt(2.0 * math.pi))
    return jnp.where(jnp.abs(offsets) <= REACH, values, jnp.zeros_like(values))


def shards(coverage, fog_rows, fog_cols):
    high = lax.Precision.HIGHEST
    cover = coverage.astype(jnp.float32) / 255.0
    rows, cols = cover.shape
    dose = jnp.ones((rows, cols), jnp.float32)
    row_place = lax.axis_index("row")
    col_place = lax.axis_index("col")
    row_count = lax.axis_size("row")
    col_count = lax.axis_size("col")
    back_rows = rows // BS
    back_cols = cols // BS
    fog_here_rows = rows // FB
    fog_here_cols = cols // FB
    row_norm = fog_rows / jnp.sum(fog_rows, axis=1, keepdims=True)
    col_norm = fog_cols / jnp.sum(fog_cols, axis=1, keepdims=True)
    row_norm_own = lax.dynamic_slice_in_dim(row_norm, row_place * fog_here_rows, fog_here_rows, 0)
    col_norm_own = lax.dynamic_slice_in_dim(col_norm, col_place * fog_here_cols, fog_here_cols, 0)
    all_back_cols = back_cols * col_count
    all_back_rows = back_rows * row_count
    own_back_cols = col_place * back_cols + jnp.arange(back_cols, dtype=jnp.int32)
    own_back_rows = row_place * back_rows + jnp.arange(back_rows, dtype=jnp.int32)
    across_gauss = gauss_matrix(jnp.arange(all_back_cols, dtype=jnp.int32), own_back_cols)
    for step in range(PASSES):
        charge = dose * cover
        padded = extended(charge, (("row", 0), ("col", 1)), HALO)
        fine = blur_padded(padded, rows, cols)
        back = block_mean(charge, BS)
        stacked = lax.all_gather(back, ("row", "col"), axis=0, tiled=True)
        back_all = (
            stacked.reshape(row_count, col_count, back_rows, back_cols)
            .transpose(0, 2, 1, 3)
            .reshape(all_back_rows, all_back_cols)
        )
        back_h_all = jnp.dot(back_all, across_gauss, precision=high)
        down_own = gauss_matrix(own_back_rows, jnp.arange(all_back_rows, dtype=jnp.int32))
        back_v = jnp.dot(down_own, back_h_all, precision=high)
        fogmean = block_mean(back_all, FB // BS)
        fog = jnp.dot(
            jnp.dot(row_norm_own, fogmean, precision=high), col_norm_own.T, precision=high
        )
        energy = spread_add(fine, back_v, BS, 0.6)
        energy = spread_add(energy, fog, FB, 0.4) / 2.0
        dose = dose + (0.5 - energy)
    return dose


def solution(mesh):
    in_specs = (P(("stripe", "row"), "col"), P(), P())
    out_specs = P(("stripe", "row"), "col")
    return jax.shard_map(shards, mesh=mesh, in_specs=in_specs, out_specs=out_specs, check_vma=False)
```

profile of v0, /device:TPU:0, one launch (start us, length us, event | category | flops | bytes accessed | tf_op | source)
XLA Modules:
  0.0 155.1 jit_solution(1370925216682589065)
XLA Ops:
  0.0 1.8 %convert_multiply_fusion = f32[256,2048]{1,0:T(8,128)S(1)} fusion(s32[256,2048]{1,0:T(8,128)} %param.3), kind=kLoop, calls=%fused_computation.79 | loop fusion | flops 1048576 | bytes 4194304 | tf_op jit(solution)/shard_map/div | solution.py:66
  1.8 1.3 collective-permute-start.1
  3.1 5.5 %collective-permute-start = (f32[4,2048]{1,0:T(4,128)S(1)}, f32[4,2048]{1,0:T(4,128)S(1)}, u32[]{:S(2)}, u32[]{:S(2)}) collective-permute-start(f32[4,2048]{1,0:T(4,128)S(1)} %get-tuple-element.13), channel_id=1, source_target_pairs={{0,2},{2,4},{4,6},{6,8},{8,10},{10,12},{12,14},{1,3},{3,5},{5,7},{... | collective-permute-start | bytes 98312 | tf_op jit(solution)/shard_map/ppermute | solution.py:23
  8.7 4.8 %reshape.76 = f32[8,32,64,32]{3,2,1,0:T(8,128)} reshape(f32[256,2048]{1,0:T(8,128)S(1)} %convert_multiply_fusion) | data formatting | bytes 4194304 | tf_op jit(solution)/shard_map/reshape | solution.py:48
  13.5 0.6 fusion.75
  14.1 4.2 %reduce_sum.82 = f32[8,64]{1,0:T(8,128)S(1)} reduce(f32[8,32,64,32]{3,2,1,0:T(8,128)} %reshape.76, f32[]{:T(128)} %constant.24.clone.1), dimensions={1,3}, to_apply=%region_1.0 | reduce | flops 523776 | bytes 2099204 | tf_op jit(solution)/shard_map/reduce_sum | solution.py:48
  18.3 20.4 %all_gather.6 = f32[128,64]{1,0:T(8,128)S(1)} all-gather(f32[8,64]{1,0:T(8,128)S(1)} %broadcast_multiply_fusion.1), channel_id=1, replica_groups=mesh['stripe'=2,'row'=8,'col'=2] {'row','col'}, dimensions={0}, use_global_device_ids=true | all-gather | bytes 34816 | tf_op jit(solution)/shard_map/all_gather | solution.py:91
  38.7 0.1 reduce_sum.85
  38.8 0.1 reduce_sum.86
  38.9 0.1 reduce_sum.83
  39.0 0.1 broadcast_divide_fusion
  39.1 0.1 reduce_sum.87
  39.2 0.1 dynamic-slice
  39.3 0.1 convolution_bitcast_fusion.3
  39.4 0.2 fusion.41
  39.6 0.1 broadcast_bitcast_fusion.1
  39.8 0.1 reshape.78
  39.9 0.2 fusion.44
  40.1 0.2 convolution_multiply_fusion.1
  40.3 0.7 broadcast_divide_fusion.1
  41.0 0.0 collective-permute-done.1
  41.0 0.0 collective-permute-done
  41.0 0.2 pad_maximum_fusion
  41.2 1.4 copy-done
  42.6 0.1 fusion.101
  42.7 2.3 %collective-permute-start.2 = (f32[264,4]{1,0:T(8,128)S(1)}, f32[264,4]{1,0:T(8,128)S(1)}, u32[]{:S(2)}, u32[]{:S(2)}) collective-permute-start(f32[264,4]{1,0:T(8,128)S(1)} %get-tuple-element.10), channel_id=1, source_target_pairs={{0,1},{2,3},{4,5},{6,7},{8,9},{10,11},{12,13},{14,15},{16,17},{18,... | collective-permute-start | bytes 12680 | tf_op jit(solution)/shard_map/ppermute | solution.py:23
  45.0 1.3 collective-permute-start.3
  46.3 0.7 fusion.104
  46.9 4.4 %add.209 = f32[8,32,64,32]{3,2,1,0:T(8,128)} broadcast(f32[8,64]{1,0:T(8,128)S(1)} %convolution_multiply_fusion.1), dimensions={0,2} | broadcast | bytes 2099200 | tf_op jit(solution)/shard_map/add | solution.py:54
  51.3 7.5 %add.210 = f32[256,2048]{1,0:T(8,128)} reshape(f32[8,32,64,32]{3,2,1,0:T(8,128)} %add.209) | data formatting | bytes 4194304 | tf_op jit(solution)/shard_map/add | solution.py:54
  58.8 0.0 collective-permute-done.2
  58.8 0.0 collective-permute-done.3
  58.8 3.0 %concatenate.13 = f32[264,2056]{1,0:T(8,128)S(1)} concatenate(f32[264,4]{1,0:T(8,128)S(1)} %collective-permute-done.2, f32[264,2048]{1,0:T(8,128)} %copy-done, f32[264,4]{1,0:T(8,128)S(1)} %collective-permute-done.3), dimensions={1} | concatenate | bytes 4342272 | tf_op jit(solution)/shard_map/concatenate | solution.py:25
  61.8 0.0 copy-start.2
  61.8 0.0 copy-start.3
  61.8 8.3 %fusion.8 = f32[256,2056]{1,0:T(8,128)S(1)} fusion(f32[264,2056]{1,0:T(8,128)S(1)} %concatenate.13, f32[]{:T(128)} %bitcast.8, f32[]{:T(128)} %bitcast.7, f32[]{:T(128)} %bitcast.6, f32[]{:T(128)} %bitcast.5, f32[]{:T(128)} %bitcast.4, f32[]{:T(128)} %bitcast.3, f32[]{:T(128)} %bitcast.2, f32[]{:T(128)} %bitcast.1, f32[]{:T(128)} %bitcast), kind=kLoop, calls=%fused_computation.18 | loop fusion | flops 8947712 | bytes 21053476 | tf_op jit(solution)/shard_map/add | solution.py:39
  70.2 10.9 %fusion.98 = (f32[256,2048]{1,0:T(8,128)S(1)}, f32[256,2048]{1,0:T(8,128)}) fusion(s32[256,2048]{1,0:T(8,128)S(1)} %copy-done.3, f32[2048]{0:T(1024)S(1)} %bitcast.57, f32[256,2048]{1,0:T(8,128)S(1)} %copy-done.2, f32[256,2056]{1,0:T(8,128)S(1)} %fusion.8, f32[]{:T(128)} %bitcast.8, f32[]{:T(128)} %bitcast.7, f32[]{:T(128)} %bitcast.6, f32[]{:T(128)} %bitcast.5, ...), kind=kLoop, calls=%fused_computation.160 | loop fusion | flops 12582912 | bytes 27271204 | tf_op jit(solution)/shard_map/mul | solution.py:87
  81.1 4.8 %reshape.80 = f32[8,32,64,32]{3,2,1,0:T(8,128)} reshape(f32[256,2048]{1,0:T(8,128)S(1)} %get-tuple-element.5) | data formatting | bytes 4194304 | tf_op jit(solution)/shard_map/reshape | solution.py:48
  85.9 4.2 %reduce_sum.88 = f32[8,64]{1,0:T(8,128)S(1)} reduce(f32[8,32,64,32]{3,2,1,0:T(8,128)} %reshape.80, f32[]{:T(128)} %constant.24.clone.1), dimensions={1,3}, to_apply=%region_6.7 | reduce | flops 523776 | bytes 2099204 | tf_op jit(solution)/shard_map/reduce_sum | solution.py:48
  90.0 18.4 %all_gather.7 = f32[128,64]{1,0:T(8,128)S(1)} all-gather(f32[8,64]{1,0:T(8,128)S(1)} %broadcast_multiply_fusion), channel_id=1, replica_groups=mesh['stripe'=2,'row'=8,'col'=2] {'row','col'}, dimensions={0}, use_global_device_ids=true | all-gather | bytes 34816 | tf_op jit(solution)/shard_map/all_gather | solution.py:91
  108.5 0.1 reshape.82
  108.6 0.2 fusion.43
  108.8 0.2 convolution_multiply_fusion
  109.0 1.3 collective-permute-start.5
  110.3 4.5 %collective-permute-start.4 = (f32[4,2048]{1,0:T(4,128)S(1)}, f32[4,2048]{1,0:T(4,128)S(1)}, u32[]{:S(2)}, u32[]{:S(2)}) collective-permute-start(f32[4,2048]{1,0:T(4,128)S(1)} %get-tuple-element.11), channel_id=1, source_target_pairs={{0,2},{2,4},{4,6},{6,8},{8,10},{10,12},{12,14},{1,3},{3,5},{5,7},{... | collective-permute-start | bytes 98312 | tf_op jit(solution)/shard_map/ppermute | solution.py:23
  114.9 0.1 reduce_sum.90
  115.0 0.1 reduce_sum.91
  115.1 0.1 convolution_bitcast_fusion.1
  115.2 0.2 fusion.42
  115.4 0.0 collective-permute-done.5
  115.4 1.0 collective-permute-done.4
  116.5 0.2 pad_maximum_fusion.1
  116.7 1.4 copy-done.1
  118.1 0.1 fusion.100
  118.2 1.3 collective-permute-start.6
  119.5 1.5 collective-permute-start.7
  121.0 0.1 broadcast_bitcast_fusion
  121.0 4.3 %add.234 = f32[8,32,64,32]{3,2,1,0:T(8,128)} broadcast(f32[8,64]{1,0:T(8,128)S(1)} %convolution_multiply_fusion), dimensions={0,2} | broadcast | bytes 2099200 | tf_op jit(solution)/shard_map/add | solution.py:54
  125.4 7.5 %add.235 = f32[256,2048]{1,0:T(8,128)} reshape(f32[8,32,64,32]{3,2,1,0:T(8,128)} %add.234) | data formatting | bytes 4194304 | tf_op jit(solution)/shard_map/add | solution.py:54
  132.9 0.0 collective-permute-done.7
  132.9 3.0 %concatenate.15 = f32[264,2056]{1,0:T(8,128)S(1)} concatenate(f32[264,4]{1,0:T(8,128)S(1)} %collective-permute-done.6, f32[264,2048]{1,0:T(8,128)} %copy-done.1, f32[264,4]{1,0:T(8,128)S(1)} %collective-permute-done.7), dimensions={1} | concatenate | bytes 4342272 | tf_op jit(solution)/shard_map/concatenate | solution.py:25
  135.9 0.0 copy-start.4
  135.9 8.3 %fusion = f32[256,2056]{1,0:T(8,128)S(1)} fusion(f32[264,2056]{1,0:T(8,128)S(1)} %concatenate.15, f32[]{:T(128)} %bitcast.8, f32[]{:T(128)} %bitcast.7, f32[]{:T(128)} %bitcast.6, f32[]{:T(128)} %bitcast.5, f32[]{:T(128)} %bitcast.4, f32[]{:T(128)} %bitcast.3, f32[]{:T(128)} %bitcast.2, f32[]{:T(128)} %bitcast.1, f32[]{:T(128)} %bitcast), kind=kLoop, calls=%fused_computation.1 | loop fusion | flops 8947712 | bytes 21053476 | tf_op jit(solution)/shard_map/add | solution.py:39
  144.2 10.9 %fusion.21 = f32[256,2048]{1,0:T(8,128)} fusion(f32[256,2048]{1,0:T(8,128)S(1)} %copy-done.4, f32[256,2048]{1,0:T(8,128)S(1)} %copy-done.5, f32[256,2056]{1,0:T(8,128)S(1)} %fusion, f32[2048]{0:T(1024)S(1)} %bitcast.56, f32[]{:T(128)} %bitcast.8, f32[]{:T(128)} %bitcast.7, f32[]{:T(128)} %bitcast.6, f32[]{:T(128)} %bitcast.5, f32[]{:T(128)} %bitcast.4, ...), kind=kLoop, calls=%fused_computation.42 | loop fusion | flops 11534336 | bytes 25174052 | tf_op jit(solution)/shard_map/add | solution.py:106
  (24 shorter events, 0.2 us)
Async XLA Ops:
  1.8 39.1 %collective-permute-start.1 = (f32[4,2048]{1,0:T(4,128)S(1)}, f32[4,2048]{1,0:T(4,128)S(1)}, u32[]{:S(2)}, u32[]{:S(2)}) collective-permute-start(f32[4,2048]{1,0:T(4,128)S(1)} %get-tuple-element.14), channel_id=1, source_target_pairs={{2,0},{4,2},{6,4},{8,6},{10,8},{12,10},{14,12},{3,1},{5,3},{7,5},{... | collective-permute-start | bytes 98312 | tf_op jit(solution)/shard_map/ppermute | solution.py:24
  3.1 37.9 %collective-permute-start = (f32[4,2048]{1,0:T(4,128)S(1)}, f32[4,2048]{1,0:T(4,128)S(1)}, u32[]{:S(2)}, u32[]{:S(2)}) collective-permute-start(f32[4,2048]{1,0:T(4,128)S(1)} %get-tuple-element.13), channel_id=1, source_target_pairs={{0,2},{2,4},{4,6},{6,8},{8,10},{10,12},{12,14},{1,3},{3,5},{5,7},{... | collective-permute-start | bytes 98312 | tf_op jit(solution)/shard_map/ppermute | solution.py:23
  14.1 24.8 %copy-start.6 = (f32[8,8]{1,0:T(8,128)S(1)}, f32[8,8]{1,0:T(8,128)}, u32[]{:S(2)}) copy-start(f32[8,8]{1,0:T(8,128)} %param.4) | copy-start | bytes 772
  14.1 25.0 %copy-start.7 = (f32[16,16]{1,0:T(8,128)S(1)}, f32[16,16]{1,0:T(8,128)}, u32[]{:S(2)}) copy-start(f32[16,16]{1,0:T(8,128)} %param.5) | copy-start | bytes 3076
  41.2 1.4 copy-start
  42.7 16.1 %collective-permute-start.2 = (f32[264,4]{1,0:T(8,128)S(1)}, f32[264,4]{1,0:T(8,128)S(1)}, u32[]{:S(2)}, u32[]{:S(2)}) collective-permute-start(f32[264,4]{1,0:T(8,128)S(1)} %get-tuple-element.10), channel_id=1, source_target_pairs={{0,1},{2,3},{4,5},{6,7},{8,9},{10,11},{12,13},{14,15},{16,17},{18,... | collective-permute-start | bytes 12680 | tf_op jit(solution)/shard_map/ppermute | solution.py:23
  45.0 13.8 %collective-permute-start.3 = (f32[264,4]{1,0:T(8,128)S(1)}, f32[264,4]{1,0:T(8,128)S(1)}, u32[]{:S(2)}, u32[]{:S(2)}) collective-permute-start(f32[264,4]{1,0:T(8,128)S(1)} %get-tuple-element.9), channel_id=1, source_target_pairs={{1,0},{3,2},{5,4},{7,6},{9,8},{11,10},{13,12},{15,14},{17,16},{19,... | collective-permute-start | bytes 12680 | tf_op jit(solution)/shard_map/ppermute | solution.py:24
  61.8 8.3 %copy-start.2 = (f32[256,2048]{1,0:T(8,128)S(1)}, f32[256,2048]{1,0:T(8,128)}, u32[]{:S(2)}) copy-start(f32[256,2048]{1,0:T(8,128)} %add.210) | copy-start | bytes 6291460
  61.8 8.3 %copy-start.3 = (s32[256,2048]{1,0:T(8,128)S(1)}, s32[256,2048]{1,0:T(8,128)}, u32[]{:S(2)}) copy-start(s32[256,2048]{1,0:T(8,128)} %param.3) | copy-start | bytes 6291460
  109.0 6.4 %collective-permute-start.5 = (f32[4,2048]{1,0:T(4,128)S(1)}, f32[4,2048]{1,0:T(4,128)S(1)}, u32[]{:S(2)}, u32[]{:S(2)}) collective-permute-start(f32[4,2048]{1,0:T(4,128)S(1)} %get-tuple-element.12), channel_id=1, source_target_pairs={{2,0},{4,2},{6,4},{8,6},{10,8},{12,10},{14,12},{3,1},{5,3},{7,5},{... | collective-permute-start | bytes 98312 | tf_op jit(solution)/shard_map/ppermute | solution.py:24
  110.3 6.1 %collective-permute-start.4 = (f32[4,2048]{1,0:T(4,128)S(1)}, f32[4,2048]{1,0:T(4,128)S(1)}, u32[]{:S(2)}, u32[]{:S(2)}) collective-permute-start(f32[4,2048]{1,0:T(4,128)S(1)} %get-tuple-element.11), channel_id=1, source_target_pairs={{0,2},{2,4},{4,6},{6,8},{8,10},{10,12},{12,14},{1,3},{3,5},{5,7},{... | collective-permute-start | bytes 98312 | tf_op jit(solution)/shard_map/ppermute | solution.py:23
  116.7 1.4 copy-start.1
  118.2 14.7 %collective-permute-start.6 = (f32[264,4]{1,0:T(8,128)S(1)}, f32[264,4]{1,0:T(8,128)S(1)}, u32[]{:S(2)}, u32[]{:S(2)}) collective-permute-start(f32[264,4]{1,0:T(8,128)S(1)} %get-tuple-element.8), channel_id=1, source_target_pairs={{0,1},{2,3},{4,5},{6,7},{8,9},{10,11},{12,13},{14,15},{16,17},{18,... | collective-permute-start | bytes 12680 | tf_op jit(solution)/shard_map/ppermute | solution.py:23
  119.5 13.4 %collective-permute-start.7 = (f32[264,4]{1,0:T(8,128)S(1)}, f32[264,4]{1,0:T(8,128)S(1)}, u32[]{:S(2)}, u32[]{:S(2)}) collective-permute-start(f32[264,4]{1,0:T(8,128)S(1)} %get-tuple-element.7), channel_id=1, source_target_pairs={{1,0},{3,2},{5,4},{7,6},{9,8},{11,10},{13,12},{15,14},{17,16},{19,... | collective-permute-start | bytes 12680 | tf_op jit(solution)/shard_map/ppermute | solution.py:24
  135.9 8.3 %copy-start.4 = (f32[256,2048]{1,0:T(8,128)S(1)}, f32[256,2048]{1,0:T(8,128)}, u32[]{:S(2)}) copy-start(f32[256,2048]{1,0:T(8,128)} %get-tuple-element.6) | copy-start | bytes 6291460
  135.9 8.3 %copy-start.5 = (f32[256,2048]{1,0:T(8,128)S(1)}, f32[256,2048]{1,0:T(8,128)}, u32[]{:S(2)}) copy-start(f32[256,2048]{1,0:T(8,128)} %add.235) | copy-start | bytes 6291460
where the time goes:
time: 158 us; the launch traced here: 155 us
  other arithmetic  50.8 us (32%)
  local copies, waits for them, and re-layouts  43.6 us (28%)
  blocking collectives  38.8 us (25%)
  starting transfers between devices  19 us (12%)
    all_gather x2, blocking collectives, shards(): stacked = lax.all_gather(back, ('row', 'col'), axis=0, tiled=True)  38.8 us
    add x4, local copies, waits for them, and re-layouts, spread_add(): field.reshape(rows // size, size, cols // size, size)  23.7 us
    add x2, other arithmetic, blur_padded(): across = across + taps[index] * padded[index:index + rows, :]  16.5 us
    ppermute x4, starting transfers between devices, extended(): before = lax.ppermute(last, axis, up)  13.6 us
    mul x1, other arithmetic, shards(): charge = dose * cover  10.9 us
    add x1, other arithmetic, shards(): dose = dose + (0.5 - energy)  10.9 us
    reshape x2, local copies, waits for them, and re-layouts, block_mean(): field.reshape(rows // size, size, cols // size, size).sum(axis=(1, 3))  9.57 us
    reduce_sum x6, other arithmetic, block_mean(): field.reshape(rows // size, size, cols // size, size).sum(axis=(1, 3))  8.62 us
  transfers between devices with their start and end apart: 8, of which 1 were waited for; matrix products, arithmetic and copies ran while one was open for 24% of the time, Pallas kernels for 0%

commit v1 on v0

v1 whole, which is shorter than its diff:
```python
import math

import jax
import jax.numpy as jnp
import numpy as np
from jax import lax
from jax.experimental import pallas as pl
from jax.experimental.pallas import tpu as pltpu
from jax.sharding import PartitionSpec as P

BS = 32
FB = 256
HALO = 4
BSIG = 16
REACH = 40
LANES = 128
HALF = LANES // 2
EDGE = 2 * HALO
PAD = 8
HIGH = lax.Precision.HIGHEST
F32 = jnp.float32
BF16 = jnp.bfloat16
VMEM = pl.BlockSpec(memory_space=pltpu.VMEM)


def fine_taps():
    offsets = np.arange(-HALO, HALO + 1).astype(np.float32)
    raw = np.exp(np.float32(-0.5) * (offsets / np.float32(1.25)) ** 2).astype(np.float32)
    taps = (raw / raw.sum(dtype=np.float32)).astype(np.float32)
    return [float(taps[HALO + k]) for k in range(HALO + 1)]


TAPS = fine_taps()


def iota(shape, dim):
    return lax.broadcasted_iota(jnp.int32, shape, dim)


def tap_of(distance):
    value = jnp.zeros(distance.shape, F32)
    for k in range(HALO + 1):
        value = jnp.where(distance == k, F32(TAPS[k]), value)
    return value


def gauss(offsets):
    off = offsets.astype(F32)
    values = jnp.exp(-0.5 * (off / BSIG) ** 2) / (BSIG * math.sqrt(2.0 * math.pi))
    return jnp.where(jnp.abs(off) <= REACH, values, jnp.zeros_like(values))


def dot(a, b, precision=HIGH):
    return jnp.dot(a, b, precision=precision, preferred_element_type=F32)


def prep_kernel(cells, fog_rows_ref, fog_cols_ref, band_ref, left_ref, own_ref, right_ref):
    back_rows, n_rows, n_cols = cells
    place = lax.axis_index("row") * back_rows
    side = FB // BS
    row = iota((2 * LANES, LANES), 0)
    lane = iota((2 * LANES, LANES), 1)
    tap = tap_of(jnp.abs(row - HALF - lane))
    upper = tap.astype(BF16)
    band_ref[:, :LANES] = upper
    band_ref[:, LANES:] = (tap - upper.astype(F32)).astype(BF16)
    fog_rows = fog_rows_ref[...]
    fog_cols = fog_cols_ref[...]
    kr = fog_rows / jnp.sum(fog_rows, axis=1, keepdims=True)
    kc = fog_cols / jnp.sum(fog_cols, axis=1, keepdims=True)
    fr, fc = kr.shape[0], kc.shape[0]
    spread_r = (iota((fr, n_rows), 1) // side == iota((fr, n_rows), 0)).astype(F32)
    spread_c = (iota((fc, n_cols), 1) // side == iota((fc, n_cols), 0)).astype(F32)
    kr_cols = dot(kr, spread_r)

    def left(count, first):
        here = iota((count, n_rows), 0) + first
        weight = 0.3 * gauss(here - iota((count, n_rows), 1))
        pick = (jnp.clip(iota((count, fr), 0) + first, 0, n_rows - 1) // side == iota((count, fr), 1)).astype(F32)
        fog = dot(pick, kr_cols) * F32(0.2 / (side * side))
        return weight, fog

    left_ref[:, :n_rows], left_ref[:, n_rows:] = left(n_rows, 0)
    ring = own_ref.shape[0]
    own_ref[:, :n_rows], own_ref[:, n_rows:] = left(ring, place - 1)
    right_ref[:, :n_cols] = gauss(iota((n_cols, n_cols), 0) - iota((n_cols, n_cols), 1))
    cols = lax.dot_general(kc, spread_c, (((0,), (0,)), ((), ())), precision=HIGH, preferred_element_type=F32)
    right_ref[:, n_cols:] = lax.dot_general(
        spread_c, cols, (((0,), (0,)), ((), ())), precision=HIGH, preferred_element_type=F32
    )


def row_blur(load):
    acc = F32(TAPS[0]) * load(0)
    for k in range(1, HALO + 1):
        acc = acc + F32(TAPS[k]) * (load(-k) + load(k))
    return acc


def first_kernel(cov_ref, first_ref, second_ref, side_ref, band_ref, cover_ref, fine_ref, sums_ref, shifted, across):
    rows, cols = cov_ref.shape
    tiles = cols // LANES
    ext = rows + 2 * EDGE
    even = lax.rem(lax.axis_index("row"), 2) == 0
    lane = iota((1, LANES), 1)

    def gather(at, span, own):
        top = jnp.where(even, second_ref[:, span], first_ref[:, span])
        low = jnp.where(even, first_ref[:, span], second_ref[:, span])
        cover_ref[at, 0:EDGE, :] = top.astype(F32)
        cover_ref[at, EDGE : EDGE + rows, :] = own.astype(F32)
        cover_ref[at, EDGE + rows :, :] = low.astype(F32)

    for t in range(tiles):
        span = slice(t * LANES, (t + 1) * LANES)
        gather(t, span, cov_ref[:, span])
    gather(tiles, slice(cols, cols + LANES), side_ref[...])
    for t in range(tiles + 1):
        before = pltpu.roll(cover_ref[(t - 1) % (tiles + 1)], HALF, 1)
        here = pltpu.roll(cover_ref[t], HALF, 1)
        tile = jnp.where(lane < HALF, before, here).astype(BF16)
        shifted[t] = tile
        if t == 0:
            shifted[tiles + 1] = tile
    across[:, 0:PAD, :] = jnp.zeros((tiles + 1, PAD, LANES), F32)
    across[:, PAD + ext :, :] = jnp.zeros((tiles + 1, PAD, LANES), F32)

    def columns(t):
        window = jnp.concatenate([shifted[t], shifted[t + 1]], axis=1)
        both = jnp.dot(window, band_ref[...], preferred_element_type=F32)
        across[t, PAD : PAD + ext, :] = both[:, :LANES] + both[:, LANES:]

    cells = rows // BS
    per = LANES // BS
    spot = iota((cells, LANES), 1)
    pick = (spot % per) * BS

    def lanes(x):
        step = BS // 2
        while step:
            x = x + pltpu.roll(x, LANES - step, 1)
            step //= 2
        return jnp.take_along_axis(x, pick, axis=1)

    def down(t):
        fine = row_blur(lambda k: across[t, PAD + k : PAD + k + ext, :])
        fine_ref[t] = fine
        return fine

    sums_ref[...] = jnp.zeros((cells, LANES), F32)
    columns(0)
    for t in range(tiles + 1):
        if t < tiles:
            columns(t + 1)
        fine = down(t)
        if t < tiles:
            cover = cover_ref[t, EDGE : EDGE + rows, :]
            energy = cover * fine[EDGE : EDGE + rows, :]
            c = lanes(cover.reshape(cells, BS, LANES).sum(axis=1))
            f = lanes(energy.reshape(cells, BS, LANES).sum(axis=1))
            where_c = spot // per == t
            where_f = spot // per == t + tiles
            sums_ref[...] = jnp.where(where_c, c, jnp.where(where_f, f, sums_ref[...]))


def second_kernel(order, gathered_ref, left_ref, own_ref, right_ref, band_ref, cover_ref, fine_ref, out_ref, c_all, f_all, ring_ref, last_ref, charge, upper, lower):
    rows, cols = out_ref.shape
    tiles = cols // LANES
    ext = rows + 2 * EDGE
    n_rows, n_cols = c_all.shape
    back_rows = rows // BS
    col = lax.axis_index("col")
    row = lax.axis_index("row")
    lane8 = iota((back_rows, LANES), 1)
    lane = iota((1, LANES), 1)
    for j in range(n_rows // back_rows):
        a = gathered_ref[(2 * j) * back_rows : (2 * j + 1) * back_rows, :]
        b = gathered_ref[(2 * j + 1) * back_rows : (2 * j + 2) * back_rows, :]
        low = jnp.where(col == 0, a, b)
        high = jnp.where(col == 0, b, a)
        at = pl.ds(pl.multiple_of(order(row, j) * back_rows, back_rows), back_rows)
        c_all[at, :] = jnp.where(lane8 < HALF, low, pltpu.roll(high, HALF, 1)) * F32(1.0 / (255.0 * BS * BS))
        f_all[at, :] = jnp.where(lane8 < HALF, pltpu.roll(low, HALF, 1), high) * F32(1.0 / (255.0 * 255.0 * BS * BS))
    right = right_ref[...]

    def both(x):
        part = dot(x, right)
        return jnp.concatenate([part[:, :n_cols], part[:, n_cols:]], axis=0)

    c = c_all[...]
    spread = both(c)
    ring_ref[...] = dot(own_ref[...], spread)
    coarse = dot(left_ref[...], spread)
    back = (1.5 - coarse) * c - 0.5 * f_all[...]
    last_ref[...] = dot(own_ref[...], both(back))

    count = ring_ref.shape[0]
    scale = F32(-0.5 / 255.0)

    def expand(ref, t):
        if t < tiles:
            pick = iota((count, LANES), 1) // BS + (col * (cols // BS) + t * (LANES // BS))
        else:
            pick = jnp.where(iota((count, LANES), 1) < HALF, (col + 1) * (cols // BS), col * (cols // BS) - 1)
        pick = jnp.clip(pick, 0, n_cols - 1)
        parts = [
            jnp.take_along_axis(ref[i : i + 8, :], pick[i : i + 8], axis=1) for i in range(0, count, 8)
        ]
        return jnp.concatenate(parts, axis=0)

    def rows_of(value, first, length):
        return jnp.broadcast_to(value[first : first + 1, :], (length, LANES))

    def dose_of(t):
        ring = expand(ring_ref, t)
        spread = jnp.concatenate(
            [rows_of(ring, 0, EDGE)]
            + [rows_of(ring, 1 + i, BS) for i in range(back_rows)]
            + [rows_of(ring, 1 + back_rows, EDGE)],
            axis=0,
        )
        return 1.5 + scale * fine_ref[t] - spread

    for t in range(tiles + 1):
        charge[t] = dose_of(t) * (cover_ref[t] * F32(1.0 / 255.0))

    def down(t):
        blurred = row_blur(lambda k: charge[t, EDGE + k : EDGE + k + rows, :])
        return pltpu.roll(blurred, HALF, 1)

    before = down(tiles)
    for t in range(tiles + 1):
        here = down(t)
        tile = jnp.where(lane < HALF, before, here)
        top = tile.astype(BF16)
        upper[t] = top
        lower[t] = (tile - top.astype(F32)).astype(BF16)
        before = here
    for t in range(tiles):
        window = jnp.concatenate([upper[t], upper[t + 1]], axis=1)
        rest = jnp.concatenate([lower[t], lower[t + 1]], axis=1)
        twice = jnp.dot(window, band_ref[...], preferred_element_type=F32)
        once = jnp.dot(rest, band_ref[:, :LANES], preferred_element_type=F32)
        fine = twice[:, :LANES] + twice[:, LANES:] + once
        last = expand(last_ref, t)
        spread = jnp.concatenate([rows_of(last, 1 + i, BS) for i in range(back_rows)], axis=0)
        dose = dose_of(t)[EDGE : EDGE + rows, :]
        out_ref[:, t * LANES : (t + 1) * LANES] = dose + (0.5 - 0.5 * fine) - spread


def pairs(count):
    even = [(i, i + 1) for i in range(0, count - 1, 2)]
    odd = [(i, i + 1) for i in range(1, count - 1, 2)]
    return [[p for i, j in some for p in ((i, j), (j, i))] for some in (even, odd)]


def swap(value, axis, some):
    return lax.ppermute(value, axis, some) if some else jnp.zeros_like(value)


def shards(coverage, fog_rows, fog_cols):
    rows, cols = coverage.shape
    row = lax.axis_index("row")
    col = lax.axis_index("col")
    row_count = lax.axis_size("row")
    col_count = lax.axis_size("col")
    tiles = cols // LANES
    back_rows, back_cols = rows // BS, cols // BS
    n_rows, n_cols = back_rows * row_count, back_cols * col_count
    ext = rows + 2 * EDGE
    if col_count != 2 or n_cols != LANES or row_count & (row_count - 1):
        raise ValueError("unsupported mesh")

    band, left, own, right = pl.pallas_call(
        lambda *refs: prep_kernel((back_rows, n_rows, n_cols), *refs),
        out_shape=(
            jax.ShapeDtypeStruct((2 * LANES, 2 * LANES), BF16),
            jax.ShapeDtypeStruct((n_rows, 2 * n_rows), F32),
            jax.ShapeDtypeStruct((16, 2 * n_rows), F32),
            jax.ShapeDtypeStruct((n_cols, 2 * n_cols), F32),
        ),
        in_specs=[VMEM] * 2,
        out_specs=(VMEM,) * 4,
        name="prep",
    )(fog_rows, fog_cols)

    edge = lax.dynamic_slice(coverage, (0, (1 - col) * (cols - LANES)), (rows, LANES)).astype(F32)
    side = swap(edge, "col", pairs(col_count)[0])
    lane = jnp.arange(LANES, dtype=jnp.int32)[None, :]
    side = jnp.where((lane < HALF) == (col == 0), side, 0.0)
    wide = lambda first: jnp.concatenate(
        [
            lax.dynamic_slice(coverage, (first, 0), (EDGE, cols)).astype(F32),
            lax.dynamic_slice(side, (first, 0), (EDGE, LANES)),
        ],
        axis=1,
    )
    odd = row % 2
    even_pairs, odd_pairs = pairs(row_count)
    first = swap(wide((1 - odd) * (rows - EDGE)), "row", even_pairs)
    second = swap(wide(odd * (rows - EDGE)), "row", odd_pairs)

    cover, fine, sums = pl.pallas_call(
        first_kernel,
        out_shape=(
            jax.ShapeDtypeStruct((tiles + 1, ext, LANES), F32),
            jax.ShapeDtypeStruct((tiles + 1, ext, LANES), F32),
            jax.ShapeDtypeStruct((back_rows, LANES), F32),
        ),
        in_specs=[VMEM] * 5,
        out_specs=(VMEM,) * 3,
        scratch_shapes=[
            pltpu.VMEM((tiles + 2, ext, LANES), BF16),
            pltpu.VMEM((tiles + 1, ext + 2 * PAD, LANES), F32),
        ],
        name="first",
    )(coverage, first, second, side, band)

    gathered = jnp.concatenate([sums, lax.ppermute(sums, "col", [(0, 1), (1, 0)])], axis=0)
    bit = 1
    while bit < row_count:
        other = lax.ppermute(gathered, "row", [(i, i ^ bit) for i in range(row_count)])
        gathered = jnp.concatenate([gathered, other], axis=0)
        bit *= 2

    return pl.pallas_call(
        lambda *refs: second_kernel(lambda r, j: r ^ j, *refs),
        out_shape=jax.ShapeDtypeStruct((rows, cols), F32),
        in_specs=[VMEM] * 7,
        out_specs=VMEM,
        scratch_shapes=[
            pltpu.VMEM((n_rows, n_cols), F32),
            pltpu.VMEM((n_rows, n_cols), F32),
            pltpu.VMEM((16, n_cols), F32),
            pltpu.VMEM((16, n_cols), F32),
            pltpu.VMEM((tiles + 1, ext, LANES), F32),
            pltpu.VMEM((tiles + 1, rows, LANES), BF16),
            pltpu.VMEM((tiles + 1, rows, LANES), BF16),
        ],
        name="second",
    )(gathered, left, own, right, band, cover, fine)


def solution(mesh):
    in_specs = (P(("stripe", "row"), "col"), P(), P())
    out_specs = P(("stripe", "row"), "col")
    return jax.shard_map(shards, mesh=mesh, in_specs=in_specs, out_specs=out_specs, check_vma=False)
```

time: 158 us -> 43.1 us (0.27); the launches traced: 155 us -> 42.7 us
  other arithmetic: 50.8 us -> 3.87 us
  local copies, waits for them, and re-layouts: 43.6 us -> 1.96 us
  blocking collectives: 38.8 us -> 0 us
  Pallas kernels: 0 us -> 15.6 us
  waiting for transfers between devices: 1.07 us -> 6.01 us
  starting transfers between devices: 19 us -> 15.2 us
    all_gather x2 -> x0, blocking collectives: 38.8 us -> none  [shards(): stacked = lax.all_gather(back, ('row', 'col'), axis=0, tiled=True)]
    add x5 -> x0, other arithmetic: 27.5 us -> none  [the longest x2 16.5 us: blur_padded(): across = across + taps[index] * padded[index:index + rows, :]]
    add x4 -> x0, local copies, waits for them, and re-layouts: 23.7 us -> none  [spread_add(): field.reshape(rows // size, size, cols // size, size)]
    pallas_call x0 -> x3, Pallas kernels: none -> 15.6 us  [the longest x1 7.73 us: shards(): pl.pallas_call(lambda *refs: second_kernel(lambda r, j: r ^ j, *refs), ou...]
    mul x1 -> x0, other arithmetic: 10.9 us -> none  [shards(): charge = dose * cover]
    reshape x4 -> x0, local copies, waits for them, and re-layouts: 9.77 us -> none  [the longest x2 9.57 us: block_mean(): field.reshape(rows // size, size, cols // size, size).sum(axis=(1, 3))]
    reduce_sum x9 -> x0, other arithmetic: 9.46 us -> none  [the longest x6 8.62 us: block_mean(): field.reshape(rows // size, size, cols // size, size).sum(axis=(1, 3))]
    concatenate x2 -> x1, local copies, waits for them, and re-layouts: 6.06 us -> 0.01 us  [shards(): gathered = jnp.concatenate([gathered, other], axis=0)]
  transfers between devices with their start and end apart: 8 -> 7, of which waited for: 1 -> 5; matrix products, arithmetic and copies ran while one was open for 24% -> 4% of each run, Pallas kernels for 0% -> 5%
where the time goes in v1:
time: 43.1 us; the launch traced here: 42.7 us
  Pallas kernels  15.6 us (36%)
  starting transfers between devices  15.2 us (35%)
  waiting for transfers between devices  6.01 us (14%)
  other arithmetic  3.87 us (9%)
  local copies, waits for them, and re-layouts  1.96 us (5%)
    ppermute x3, starting transfers between devices, shards(): lax.ppermute(gathered, 'row', [(i, i ^ bit) for i in range(row_count)])  11.1 us
    pallas_call x1, Pallas kernels, shards(): pl.pallas_call(lambda *refs: second_kernel(lambda r, j: r ^ j, *refs), ou...  7.73 us
    pallas_call x1, Pallas kernels, shards(): pl.pallas_call(first_kernel, out_shape=(jax.ShapeDtypeStruct((tiles + 1,...  5.87 us
    ppermute x3, waiting for transfers between devices, shards(): lax.ppermute(gathered, 'row', [(i, i ^ bit) for i in range(row_count)])  5.23 us
    ppermute x3, starting transfers between devices, swap(): return lax.ppermute(value, axis, some) if some else jnp.zeros_like(value)  4.14 us
    pallas_call x1, Pallas kernels, shards(): pl.pallas_call(lambda *refs: prep_kernel((back_rows, n_rows, n_cols), *re...  1.97 us
    unnamed x12, local copies, waits for them, and re-layouts  1.95 us
    concatenate x2, other arithmetic, shards(): gathered = jnp.concatenate([gathered, other], axis=0)  1.36 us
  transfers between devices with their start and end apart: 7, of which 5 were waited for; matrix products, arithmetic and copies ran while one was open for 4% of the time, Pallas kernels for 5%

profile of v1, /device:TPU:0, one launch (start us, length us, event | category | flops | bytes accessed | tf_op | source)
XLA Modules:
  0.0 42.7 jit_solution(2153810101050904525)
XLA Ops:
  0.0 0.9 %dynamic-slice_convert_fusion = f32[256,128]{1,0:T(8,128)S(1)} fusion(s32[256,2048]{1,0:T(8,128)} %cov_ref.1, s32[]{:T(128)S(6)} %select_n.24), kind=kLoop, calls=%fused_computation | loop fusion | flops 32768 | bytes 262148 | tf_op jit(solution)/shard_map/convert_element_type | solution.py:287
  0.9 0.6 %collective-permute-start = (f32[256,128]{1,0:T(8,128)S(1)}, f32[256,128]{1,0:T(8,128)S(1)}, u32[]{:S(2)}, u32[]{:S(2)}) collective-permute-start(f32[256,128]{1,0:T(8,128)S(1)} %dynamic-slice_convert_fusion), channel_id=1, source_target_pairs={{0,1},{1,0},{2,3},{3,2},{4,5},{5,4},{6,7},{7,6},{8,9},{9,8},{10,11... | collective-permute-start | bytes 393224 | tf_op jit(solution)/shard_map/ppermute | solution.py:258
  1.5 0.9 %dynamic-slice_convert_fusion.1 = (f32[8,2048]{1,0:T(8,128)S(1)}, f32[8,2048]{1,0:T(8,128)S(1)}) fusion(s32[256,2048]{1,0:T(8,128)} %cov_ref.1, s32[]{:T(128)S(6)} %select_n.26, s32[]{:T(128)S(6)} %select_n.23), kind=kLoop, calls=%fused_computation.3 | loop fusion | flops 32768 | bytes 262152 | tf_op jit(solution)/shard_map/convert_element_type | solution.py:293
  2.4 0.1 collective-permute-done
  2.5 0.0 copy-start
  2.5 2.9 %collective-permute-start.1 = (f32[8,2176]{1,0:T(8,128)S(1)}, f32[8,2176]{1,0:T(8,128)S(1)}, u32[]{:S(2)}, u32[]{:S(2)}) collective-permute-start(f32[8,2176]{1,0:T(8,128)S(1)} %pad_maximum_fusion), channel_id=1, source_target_pairs={{0,2},{2,0},{4,6},{6,4},{8,10},{10,8},{12,14},{14,12},{1,3},{3,1},... | collective-permute-start | bytes 208904 | tf_op jit(solution)/shard_map/ppermute | solution.py:258
  5.5 0.7 %collective-permute-start.2 = (f32[8,2176]{1,0:T(8,128)S(1)}, f32[8,2176]{1,0:T(8,128)S(1)}, u32[]{:S(2)}, u32[]{:S(2)}) collective-permute-start(f32[8,2176]{1,0:T(8,128)S(1)} %pad_maximum_fusion.1), channel_id=1, source_target_pairs={{2,4},{4,2},{6,8},{8,6},{10,12},{12,10},{3,5},{5,3},{7,9},{9,7},{1... | collective-permute-start | bytes 208904 | tf_op jit(solution)/shard_map/ppermute | solution.py:258
  6.1 2.0 %prep.1 = (bf16[256,256]{1,0:T(8,128)(2,1)}, f32[64,128]{1,0:T(8,128)}, f32[16,128]{1,0:T(8,128)}, f32[128,256]{1,0:T(8,128)}) custom-call(f32[8,8]{1,0:T(8,128)} %refs_0_.1, f32[16,16]{1,0:T(8,128)} %refs_1_.1), custom_call_target="tpu_custom_call" | custom-call | tf_op jit(solution)/shard_map/prep/pallas_call | solution.py:274
  8.1 0.0 collective-permute-done.1.first_ref
  8.1 0.0 copy-start.2
  8.1 0.0 collective-permute-done.2.second_ref
  8.1 0.0 copy-start.3
  8.1 0.0 copy-done
  8.1 0.6 %copy-done.2 = f32[8,2176]{1,0:T(8,128)} copy-done((f32[8,2176]{1,0:T(8,128)}, f32[8,2176]{1,0:T(8,128)S(1)}, u32[]{:S(2)}) %copy-start.2) | copy-done | bytes 69656
  8.7 0.0 copy-done.3
  8.8 5.9 %first.1 = (f32[17,272,128]{2,1,0:T(8,128)}, f32[17,272,128]{2,1,0:T(8,128)}, f32[8,128]{1,0:T(8,128)}) custom-call(s32[256,2048]{1,0:T(8,128)} %cov_ref.1, f32[8,2176]{1,0:T(8,128)} %copy-done.2, f32[8,2176]{1,0:T(8,128)} %copy-done.3, f32[256,128]{1,0:T(8,128)} %copy-done, bf16[256,256]{1,0:T(8,128)(2,1)} %get-tuple-element.12.band_ref.refs_4_), custom_call_target="tpu_custom_call" | custom-call | tf_op jit(solution)/shard_map/first/pallas_call | solution.py:303
  14.6 0.0 collective-permute-start.3
  14.6 0.7 %constant_dynamic-update-slice_fusion.4 = f32[128,128]{1,0:T(8,128)S(1)} fusion(f32[8,128]{1,0:T(8,128)} %get-tuple-element.13), kind=kLoop, calls=%fused_computation.12 | loop fusion | bytes 8192
  15.3 0.7 %collective-permute-done.3 = f32[8,128]{1,0:T(8,128)S(1)} collective-permute-done((f32[8,128]{1,0:T(8,128)}, f32[8,128]{1,0:T(8,128)S(1)}, u32[]{:S(2)}, u32[]{:S(2)}) %collective-permute-start.3) | collective-permute-done | bytes 4128 | tf_op jit(solution)/shard_map/ppermute | solution.py:319
  16.0 0.7 %pad_maximum_fusion.4 = f32[16,128]{1,0:T(8,128)S(1)} fusion(f32[8,128]{1,0:T(8,128)S(1)} %collective-permute-done.3, f32[8,128]{1,0:T(8,128)} %get-tuple-element.13), kind=kLoop, calls=%fused_computation.13 | loop fusion | flops 2048 | bytes 16384 | tf_op jit(solution)/shard_map/concatenate | solution.py:319
  16.7 4.6 %collective-permute-start.4 = (f32[16,128]{1,0:T(8,128)S(1)}, f32[16,128]{1,0:T(8,128)S(1)}, u32[]{:S(2)}, u32[]{:S(2)}) collective-permute-start(f32[16,128]{1,0:T(8,128)S(1)} %pad_maximum_fusion.4), channel_id=1, source_target_pairs={{0,2},{2,0},{4,6},{6,4},{8,10},{10,8},{12,14},{14,12},{1,3},{3,1},... | collective-permute-start | bytes 24584 | tf_op jit(solution)/shard_map/ppermute | solution.py:322
  21.2 1.6 %collective-permute-done.4 = f32[16,128]{1,0:T(8,128)S(1)} collective-permute-done((f32[16,128]{1,0:T(8,128)S(1)}, f32[16,128]{1,0:T(8,128)S(1)}, u32[]{:S(2)}, u32[]{:S(2)}) %collective-permute-start.4) | collective-permute-done | bytes 8224 | tf_op jit(solution)/shard_map/ppermute | solution.py:322
  22.9 0.7 %pad_maximum_fusion.3 = f32[32,128]{1,0:T(8,128)S(1)} fusion(f32[16,128]{1,0:T(8,128)S(1)} %collective-permute-done.4, f32[8,128]{1,0:T(8,128)S(1)} %collective-permute-done.3, f32[8,128]{1,0:T(8,128)} %get-tuple-element.13), kind=kLoop, calls=%fused_computation.7 | loop fusion | flops 8192 | bytes 32768 | tf_op jit(solution)/shard_map/concatenate | solution.py:323
  23.6 3.5 %collective-permute-start.5 = (f32[32,128]{1,0:T(8,128)S(1)}, f32[32,128]{1,0:T(8,128)S(1)}, u32[]{:S(2)}, u32[]{:S(2)}) collective-permute-start(f32[32,128]{1,0:T(8,128)S(1)} %pad_maximum_fusion.3), channel_id=1, source_target_pairs={{0,4},{2,6},{4,0},{6,2},{8,12},{10,14},{12,8},{14,10},{1,5},{3,7},... | collective-permute-start | bytes 49160 | tf_op jit(solution)/shard_map/ppermute | solution.py:322
  27.0 1.7 %collective-permute-done.5 = f32[32,128]{1,0:T(8,128)S(1)} collective-permute-done((f32[32,128]{1,0:T(8,128)S(1)}, f32[32,128]{1,0:T(8,128)S(1)}, u32[]{:S(2)}, u32[]{:S(2)}) %collective-permute-start.5) | collective-permute-done | bytes 16416 | tf_op jit(solution)/shard_map/ppermute | solution.py:322
  28.7 0.7 %pad_maximum_fusion.2 = f32[64,128]{1,0:T(8,128)S(1)} fusion(f32[32,128]{1,0:T(8,128)S(1)} %collective-permute-done.5, f32[16,128]{1,0:T(8,128)S(1)} %collective-permute-done.4, f32[8,128]{1,0:T(8,128)S(1)} %collective-permute-done.3, f32[8,128]{1,0:T(8,128)} %get-tuple-element.13), kind=kLoop, calls=%fused_computation.6 | loop fusion | flops 24576 | bytes 65536 | tf_op jit(solution)/shard_map/concatenate | solution.py:323
  29.4 3.0 %collective-permute-start.6 = (f32[64,128]{1,0:T(8,128)S(1)}, f32[64,128]{1,0:T(8,128)S(1)}, u32[]{:S(2)}, u32[]{:S(2)}) collective-permute-start(f32[64,128]{1,0:T(8,128)S(1)} %pad_maximum_fusion.2), channel_id=1, source_target_pairs={{0,8},{2,10},{4,12},{6,14},{8,0},{10,2},{12,4},{14,6},{1,9},{3,11}... | collective-permute-start | bytes 98312 | tf_op jit(solution)/shard_map/ppermute | solution.py:322
  32.5 1.9 %collective-permute-done.6 = f32[64,128]{1,0:T(8,128)S(1)} collective-permute-done((f32[64,128]{1,0:T(8,128)S(1)}, f32[64,128]{1,0:T(8,128)S(1)}, u32[]{:S(2)}, u32[]{:S(2)}) %collective-permute-start.6) | collective-permute-done | bytes 32800 | tf_op jit(solution)/shard_map/ppermute | solution.py:322
  34.4 0.0 copy-start.1
  34.4 0.6 %copy-done.1 = f32[128,128]{1,0:T(8,128)} copy-done((f32[128,128]{1,0:T(8,128)}, f32[128,128]{1,0:T(8,128)S(1)}, u32[]{:S(2)}) %copy-start.1) | copy-done | bytes 65560
  35.0 7.7 %second.1 = f32[256,2048]{1,0:T(8,128)} custom-call(f32[128,128]{1,0:T(8,128)} %copy-done.1, f32[64,128]{1,0:T(8,128)} %get-tuple-element.14.refs_1_, f32[16,128]{1,0:T(8,128)} %get-tuple-element.15.refs_2_, f32[128,256]{1,0:T(8,128)} %get-tuple-element.16.refs_3_, bf16[256,256]{1,0:T(8,128)(2,1)} %get-tuple-element.12.band_ref.refs_4_, ...), custom_call_target="tpu_custom_call" | custom-call | tf_op jit(solution)/shard_map/second/pallas_call | solution.py:326
  (9 shorter events, 0.1 us)
Async XLA Ops:
  0.9 1.5 %collective-permute-start = (f32[256,128]{1,0:T(8,128)S(1)}, f32[256,128]{1,0:T(8,128)S(1)}, u32[]{:S(2)}, u32[]{:S(2)}) collective-permute-start(f32[256,128]{1,0:T(8,128)S(1)} %dynamic-slice_convert_fusion), channel_id=1, source_target_pairs={{0,1},{1,0},{2,3},{3,2},{4,5},{5,4},{6,7},{7,6},{8,9},{9,8},{10,11... | collective-permute-start | bytes 393224 | tf_op jit(solution)/shard_map/ppermute | solution.py:258
  2.5 5.6 %copy-start = (f32[256,128]{1,0:T(8,128)}, f32[256,128]{1,0:T(8,128)S(1)}, u32[]{:S(2)}) copy-start(f32[256,128]{1,0:T(8,128)S(1)} %broadcast_select_fusion.side_ref) | copy-start | bytes 393220
  2.5 5.6 %collective-permute-start.1 = (f32[8,2176]{1,0:T(8,128)S(1)}, f32[8,2176]{1,0:T(8,128)S(1)}, u32[]{:S(2)}, u32[]{:S(2)}) collective-permute-start(f32[8,2176]{1,0:T(8,128)S(1)} %pad_maximum_fusion), channel_id=1, source_target_pairs={{0,2},{2,0},{4,6},{6,4},{8,10},{10,8},{12,14},{14,12},{1,3},{3,1},... | collective-permute-start | bytes 208904 | tf_op jit(solution)/shard_map/ppermute | solution.py:258
  5.5 2.6 %collective-permute-start.2 = (f32[8,2176]{1,0:T(8,128)S(1)}, f32[8,2176]{1,0:T(8,128)S(1)}, u32[]{:S(2)}, u32[]{:S(2)}) collective-permute-start(f32[8,2176]{1,0:T(8,128)S(1)} %pad_maximum_fusion.1), channel_id=1, source_target_pairs={{2,4},{4,2},{6,8},{8,6},{10,12},{12,10},{3,5},{5,3},{7,9},{9,7},{1... | collective-permute-start | bytes 208904 | tf_op jit(solution)/shard_map/ppermute | solution.py:258
  8.1 0.6 %copy-start.2 = (f32[8,2176]{1,0:T(8,128)}, f32[8,2176]{1,0:T(8,128)S(1)}, u32[]{:S(2)}) copy-start(f32[8,2176]{1,0:T(8,128)S(1)} %collective-permute-done.1.first_ref) | copy-start | bytes 208900
  8.1 0.6 %copy-start.3 = (f32[8,2176]{1,0:T(8,128)}, f32[8,2176]{1,0:T(8,128)S(1)}, u32[]{:S(2)}) copy-start(f32[8,2176]{1,0:T(8,128)S(1)} %collective-permute-done.2.second_ref) | copy-start | bytes 208900
  14.6 1.4 %collective-permute-start.3 = (f32[8,128]{1,0:T(8,128)}, f32[8,128]{1,0:T(8,128)S(1)}, u32[]{:S(2)}, u32[]{:S(2)}) collective-permute-start(f32[8,128]{1,0:T(8,128)} %get-tuple-element.13), channel_id=1, source_target_pairs={{0,1},{1,0},{2,3},{3,2},{4,5},{5,4},{6,7},{7,6},{8,9},{9,8},{10,11... | collective-permute-start | bytes 12296 | tf_op jit(solution)/shard_map/ppermute | solution.py:319
  16.7 6.2 %collective-permute-start.4 = (f32[16,128]{1,0:T(8,128)S(1)}, f32[16,128]{1,0:T(8,128)S(1)}, u32[]{:S(2)}, u32[]{:S(2)}) collective-permute-start(f32[16,128]{1,0:T(8,128)S(1)} %pad_maximum_fusion.4), channel_id=1, source_target_pairs={{0,2},{2,0},{4,6},{6,4},{8,10},{10,8},{12,14},{14,12},{1,3},{3,1},... | collective-permute-start | bytes 24584 | tf_op jit(solution)/shard_map/ppermute | solution.py:322
  23.6 5.2 %collective-permute-start.5 = (f32[32,128]{1,0:T(8,128)S(1)}, f32[32,128]{1,0:T(8,128)S(1)}, u32[]{:S(2)}, u32[]{:S(2)}) collective-permute-start(f32[32,128]{1,0:T(8,128)S(1)} %pad_maximum_fusion.3), channel_id=1, source_target_pairs={{0,4},{2,6},{4,0},{6,2},{8,12},{10,14},{12,8},{14,10},{1,5},{3,7},... | collective-permute-start | bytes 49160 | tf_op jit(solution)/shard_map/ppermute | solution.py:322
  29.4 4.9 %collective-permute-start.6 = (f32[64,128]{1,0:T(8,128)S(1)}, f32[64,128]{1,0:T(8,128)S(1)}, u32[]{:S(2)}, u32[]{:S(2)}) collective-permute-start(f32[64,128]{1,0:T(8,128)S(1)} %pad_maximum_fusion.2), channel_id=1, source_target_pairs={{0,8},{2,10},{4,12},{6,14},{8,0},{10,2},{12,4},{14,6},{1,9},{3,11}... | collective-permute-start | bytes 98312 | tf_op jit(solution)/shard_map/ppermute | solution.py:322
  34.4 0.6 %copy-start.1 = (f32[128,128]{1,0:T(8,128)}, f32[128,128]{1,0:T(8,128)S(1)}, u32[]{:S(2)}) copy-start(f32[128,128]{1,0:T(8,128)S(1)} %constant_dynamic-update-slice_fusion.refs_0_) | copy-start | bytes 196612

commit v2 on v0

v2 whole, which is shorter than its diff:
```python
import math

import jax
import jax.numpy as jnp
import numpy as np
from jax import lax
from jax.experimental import pallas as pl
from jax.experimental.pallas import tpu as pltpu
from jax.sharding import PartitionSpec as P

BS = 32
FB = 256
HALO = 4
BSIG = 16
REACH = 40
LANES = 128
HALF = LANES // 2
EDGE = 2 * HALO
PAD = 8
F32 = jnp.float32
BF16 = jnp.bfloat16
VMEM = pl.BlockSpec(memory_space=pltpu.VMEM)


def fine_taps():
    offsets = np.arange(-HALO, HALO + 1).astype(np.float32)
    raw = np.exp(np.float32(-0.5) * (offsets / np.float32(1.25)) ** 2).astype(np.float32)
    taps = (raw / raw.sum(dtype=np.float32)).astype(np.float32)
    return [float(taps[HALO + k]) for k in range(HALO + 1)]


TAPS = fine_taps()


def iota(shape, dim):
    return lax.broadcasted_iota(jnp.int32, shape, dim)


def tap_of(distance):
    value = jnp.zeros(distance.shape, F32)
    for k in range(HALO + 1):
        value = jnp.where(distance == k, F32(TAPS[k]), value)
    return value


def gauss(offsets):
    off = offsets.astype(F32)
    values = jnp.exp(-0.5 * (off / BSIG) ** 2) / (BSIG * math.sqrt(2.0 * math.pi))
    return jnp.where(jnp.abs(off) <= REACH, values, jnp.zeros_like(values))


def halves(x):
    upper = x.astype(BF16)
    return upper, (x - upper.astype(F32)).astype(BF16)


def dot(a, b):
    (ah, al), (bh, bl) = halves(a), halves(b)
    return jnp.dot(
        jnp.concatenate([ah, al, ah], axis=1),
        jnp.concatenate([bh, bh, bl], axis=0),
        preferred_element_type=F32,
    )


def full_dot(a, b, over=1):
    return lax.dot_general(
        a, b, (((over,), (0,)), ((), ())), precision=lax.Precision.HIGHEST, preferred_element_type=F32
    )


def prep(place, fog_rows, fog_cols, left_ref, own_ref, right_ref):
    n_rows = left_ref.shape[0]
    n_cols = right_ref.shape[0]
    side = FB // BS
    kr = fog_rows / jnp.sum(fog_rows, axis=1, keepdims=True)
    kc = fog_cols / jnp.sum(fog_cols, axis=1, keepdims=True)
    fr, fc = kr.shape[0], kc.shape[0]
    spread_r = (iota((fr, n_rows), 1) // side == iota((fr, n_rows), 0)).astype(F32)
    spread_c = (iota((fc, n_cols), 1) // side == iota((fc, n_cols), 0)).astype(F32)
    kr_cols = full_dot(kr, spread_r)

    def left(count, first):
        here = iota((count, n_rows), 0) + first
        weight = 0.3 * gauss(here - iota((count, n_rows), 1))
        cell = jnp.clip(iota((count, fr), 0) + first, 0, n_rows - 1) // side
        pick = (cell == iota((count, fr), 1)).astype(F32)
        return weight, full_dot(pick, kr_cols) * F32(0.2 / (side * side))

    left_ref[:, :n_rows], left_ref[:, n_rows:] = left(n_rows, 0)
    own_ref[:, :n_rows], own_ref[:, n_rows:] = left(own_ref.shape[0], place - 1)
    right_ref[:, :n_cols] = gauss(iota((n_cols, n_cols), 0) - iota((n_cols, n_cols), 1))
    right_ref[:, n_cols:] = full_dot(spread_c, full_dot(kc, spread_c, 0), 0)


def row_blur(load, scale=1.0):
    acc = F32(TAPS[0] * scale) * load(0)
    for k in range(1, HALO + 1):
        acc = acc + F32(TAPS[k] * scale) * (load(-k) + load(k))
    return acc


def fold(parts, pick):
    row = iota((8, LANES), 0)
    step = 4
    while step:
        keep = row % (2 * step) < step
        half = len(parts) // 2
        parts = [
            jnp.where(keep, a + pltpu.roll(a, 8 - step, 0), b + pltpu.roll(b, step, 0))
            for a, b in zip(parts[:half], parts[half:])
        ]
        step //= 2
    x = parts[0]
    step = BS // 2
    while step:
        x = x + pltpu.roll(x, LANES - step, 1)
        step //= 2
    return jnp.take_along_axis(x, pick, axis=1)


def chunks(start, stop, size=64):
    return [(a, min(size, stop - a)) for a in range(start, stop, size)]


def load_kernel(cov_ref, fog_rows_ref, fog_cols_ref, cover_ref, shifted, sums_ref, edge_ref, first_ref, second_ref, band_ref, left_ref, own_ref, right_ref, loaded, cells_of, fog_r, fog_c, sems):
    rows, cols = cov_ref.shape
    tiles = cols // LANES
    pieces = sems.shape[0] - 2
    part = rows // pieces
    copies = [
        pltpu.make_async_copy(
            cov_ref.at[p * part : (p + 1) * part], loaded.at[p * part : (p + 1) * part], sems.at[p]
        )
        for p in range(pieces)
    ]
    fogs = [
        pltpu.make_async_copy(fog_rows_ref, fog_r, sems.at[pieces]),
        pltpu.make_async_copy(fog_cols_ref, fog_c, sems.at[pieces + 1]),
    ]
    for copy in fogs + copies[:2]:
        copy.start()
    tap = tap_of(jnp.abs(iota((2 * LANES, LANES), 0) - HALF - iota((2 * LANES, LANES), 1)))
    band_ref[:, :LANES], band_ref[:, LANES:] = halves(tap)
    for copy in fogs:
        copy.wait()
    place = lax.axis_index("row") * (rows // BS)
    prep(place, fog_r[...], fog_c[...], left_ref, own_ref, right_ref)
    lane = iota((1, LANES), 1)
    per = LANES // BS
    for p, copy in enumerate(copies):
        copy.wait()
        if p + 2 < pieces:
            copies[p + 2].start()
        at = slice(EDGE + p * part, EDGE + (p + 1) * part)
        before = None
        for t in range(tiles):
            value = loaded[p * part : (p + 1) * part, t * LANES : (t + 1) * LANES].astype(F32)
            cover_ref[t, at, :] = value
            here = pltpu.roll(value, HALF, 1)
            if t:
                shifted[t, p * part : (p + 1) * part, :] = jnp.where(lane < HALF, before, here).astype(BF16)
            before = here
            for i in range(part // BS):
                cell = value[i * BS : (i + 1) * BS]
                cells_of[t, p * (part // BS) + i] = sum(cell[b : b + 8] for b in range(8, BS, 8)) + cell[:8]
    edge_ref[...] = cover_ref[(1 - lax.axis_index("col")) * (tiles - 1), EDGE : EDGE + rows, :]
    even = lax.rem(lax.axis_index("row"), 2) == 0
    spot = iota((8, LANES), 1)
    sums = jnp.zeros((8, LANES), F32)
    for t in range(tiles):
        top = cover_ref[t, EDGE : 2 * EDGE, :]
        low = cover_ref[t, rows : rows + EDGE, :]
        first_ref[t] = jnp.where(even, low, top)
        second_ref[t] = jnp.where(even, top, low)
        cell = fold([cells_of[t, i] for i in range(rows // BS)], (spot % per) * BS)
        sums = jnp.where(spot // per == t, cell, sums)
    sums_ref[...] = sums


def inner_kernel(side_ref, band_ref, c_ref, cover_in, shifted, cover_ref, fine_ref, across, sums_ref, ends):
    tiles = cover_ref.shape[0] - 1
    rows = side_ref.shape[0]
    lane = iota((1, LANES), 1)
    cells = rows // BS
    per = LANES // BS
    spot = iota((cells, LANES), 1)
    pick = (spot % per) * BS
    own = slice(EDGE, EDGE + rows)
    value = jnp.where((lane < HALF) == (lax.axis_index("col") == 0), side_ref[...], 0.0)
    cover_ref[tiles, own, :] = value
    side = pltpu.roll(value, HALF, 1)
    ends[0] = jnp.where(lane < HALF, side, pltpu.roll(cover_in[0, own, :], HALF, 1)).astype(BF16)
    ends[1] = jnp.where(lane < HALF, pltpu.roll(cover_in[tiles - 1, own, :], HALF, 1), side).astype(BF16)

    def tile(t):
        return ends.at[0] if t in (0, tiles + 1) else ends.at[1] if t == tiles else shifted.at[t]

    def columns(t):
        left, right = tile(t), tile(t + 1)
        for a, n in chunks(0, rows, 128):
            window = jnp.concatenate([left[a : a + n, :], right[a : a + n, :]], axis=1)
            both = jnp.dot(window, band_ref[...], preferred_element_type=F32)
            across[t, PAD + EDGE + a : PAD + EDGE + a + n, :] = both[:, :LANES] + both[:, LANES:]

    def down(t):
        parts = []
        for a, n in chunks(0, rows, BS):
            low, high = max(a, 8), min(a + n, rows - 8)
            base = PAD + EDGE + low
            fine = row_blur(lambda k: across[t, base + k : base + k + high - low, :])
            fine_ref[t, EDGE + low : EDGE + high, :] = fine
            energy = cover_in[t, EDGE + low : EDGE + high, :] * fine
            parts.append(sum(energy[b : b + 8] for b in range(8, high - low, 8)) + energy[:8])
        if t < tiles:
            f = fold(parts, pick)
            sums_ref[...] = jnp.where(spot // per == t + tiles, f, sums_ref[...])

    sums_ref[...] = c_ref[...]
    columns(0)
    for t in range(tiles + 1):
        if t < tiles:
            columns(t + 1)
        down(t)


def outer_kernel(first_ref, second_ref, band_ref, across_ref, part_ref, cover_in, fine_in, cover_ref, fine_ref, sums_ref, across, window):
    tiles = cover_ref.shape[0] - 1
    ext = cover_ref.shape[1]
    rows = ext - 2 * EDGE
    even = lax.rem(lax.axis_index("row"), 2) == 0
    lane = iota((1, LANES), 1)
    cells = rows // BS
    per = LANES // BS
    spot = iota((cells, LANES), 1)
    pick = (spot % per) * BS
    both = 2 * EDGE
    touches = (lane < HALF) == (lax.axis_index("col") == 0)
    place = lax.axis_index("row")
    alone = (place == 0) | (place == lax.axis_size("row") - 1)

    def halo(t):
        if t < tiles:
            a, b = first_ref[t], second_ref[t]
        else:
            a = jnp.where(even, first_ref[t], first_ref[t + 1])
            b = jnp.where(even, second_ref[t + 1], second_ref[t])
            a, b = jnp.where(touches, a, 0.0), jnp.where(touches, b, 0.0)
        b = jnp.where(alone, 0.0, b)
        top = jnp.where(even, b, a)
        low = jnp.where(even, a, b)
        cover_ref[t, 0:EDGE, :] = top
        cover_ref[t, EDGE + rows :, :] = low
        return pltpu.roll(jnp.concatenate([top, low], axis=0), HALF, 1)

    before = halo(tiles)
    first = before
    for t in range(tiles + 1):
        here = halo(t) if t < tiles else first
        tile = jnp.where(lane < HALF, before, here).astype(BF16)
        window[t * both : (t + 1) * both, :LANES] = tile
        at = t - 1 if t else tiles
        window[at * both : (at + 1) * both, LANES:] = tile
        before = here
    twice = jnp.dot(window[...], band_ref[...], preferred_element_type=F32)
    once = twice[:, :LANES] + twice[:, LANES:]
    reach = 2 * PAD + 2 * EDGE
    total = jnp.zeros((cells, LANES), F32)
    for t in range(tiles + 1):
        across[t, 0:PAD, :] = jnp.zeros((PAD, LANES), F32)
        across[t, PAD : PAD + EDGE, :] = once[t * both : t * both + EDGE]
        across[t, PAD + EDGE : reach, :] = across_ref[t, PAD + EDGE : reach, :]
        low = reach
        across[t, low : low + PAD + EDGE, :] = across_ref[t, ext - PAD - EDGE : ext, :]
        across[t, low + PAD + EDGE : low + PAD + 2 * EDGE, :] = once[t * both + EDGE : (t + 1) * both]
        across[t, low + PAD + 2 * EDGE :, :] = jnp.zeros((PAD, LANES), F32)
        top = row_blur(lambda k: across[t, PAD + k : PAD + k + EDGE + 8, :])
        base = low + 8
        bot = row_blur(lambda k: across[t, base + k : base + k + EDGE + 8, :])
        fine_ref[t, 0 : EDGE + 8, :] = top
        fine_ref[t, EDGE + rows - 8 :, :] = bot
        if t < tiles:
            zero = jnp.zeros((8, LANES), F32)
            a = top[EDGE:] * cover_ref[t, EDGE : EDGE + 8, :]
            b = bot[:8] * cover_ref[t, EDGE + rows - 8 : EDGE + rows, :]
            total = jnp.where(spot // per == t + tiles, fold([a] + [zero] * (cells - 2) + [b], pick), total)
    sums_ref[...] = part_ref[...] + total


def spread_kernel(cover_ref, blurred_ref, above_ref, below_ref):
    tiles, ext = cover_ref.shape[0] - 1, cover_ref.shape[1]
    rows = ext - 2 * EDGE
    scale = 0.5 / 255.0
    row = iota((8, LANES), 0)
    for t in range(tiles + 1):
        for a, n in chunks(0, rows):
            blurred_ref[t, a : a + n, :] = row_blur(lambda k: cover_ref[t, EDGE + a + k : EDGE + a + k + n, :], scale)
        for i in range(rows // BS):
            top = EDGE + i * BS
            low = top + BS - 8
            above = jnp.zeros((8, LANES), F32)
            below = jnp.zeros((8, LANES), F32)
            for k in range(1, HALO + 1):
                tap = F32(TAPS[k] * scale)
                above = above + jnp.where(row < k, tap * cover_ref[t, top - k : top - k + 8, :], 0.0)
                below = below + jnp.where(row >= 8 - k, tap * cover_ref[t, low + k : low + k + 8, :], 0.0)
            above_ref[t, i] = above
            below_ref[t, i] = below


def first_dose_kernel(cover_ref, fine_ref, after_ref, dose_ref, blurred_ref, charge):
    del after_ref
    tiles, ext = cover_ref.shape[0] - 1, cover_ref.shape[1]
    rows = ext - 2 * EDGE
    for t in range(tiles + 1):
        for a, n in [(0, EDGE)] + [(EDGE + a, n) for a, n in chunks(0, rows)] + [(EDGE + rows, EDGE)]:
            dose = 2.0 - F32(0.5 / 255.0) * fine_ref[t, a : a + n, :]
            if t < tiles and EDGE <= a < EDGE + rows:
                dose_ref[t, a - EDGE : a - EDGE + n, :] = dose
            charge[t, a : a + n, :] = (dose - 0.5) * cover_ref[t, a : a + n, :]
        for a, n in chunks(0, rows):
            blurred_ref[t, a : a + n, :] = row_blur(
                lambda k: charge[t, EDGE + a + k : EDGE + a + k + n, :], 0.5 / 255.0
            )


def last_kernel(gathered_ref, left_ref, own_ref, right_ref, band_ref, dose_ref, charge_ref, blurred_ref, above_ref, below_ref, out_ref, c_all, f_all, ring_ref, last_ref, upper, lower, turned, ends, staged, sems):
    rows, cols = out_ref.shape
    tiles = cols // LANES
    n_rows, n_cols = c_all.shape
    cells = rows // BS
    col = lax.axis_index("col")
    row = lax.axis_index("row")
    lane8 = iota((cells, LANES), 1)
    lane = iota((1, LANES), 1)
    count = n_rows // cells
    for j in range(count):
        mine = gathered_ref[j * cells : (j + 1) * cells, :]
        other = gathered_ref[(count + j) * cells : (count + j + 1) * cells, :]
        here = col == bin(j).count("1") % 2
        low = jnp.where(here, mine, other)
        high = jnp.where(here, other, mine)
        at = pl.ds(pl.multiple_of((row ^ j) * cells, cells), cells)
        c_all[at, :] = jnp.where(lane8 < HALF, low, pltpu.roll(high, HALF, 1)) * F32(1.0 / (255.0 * BS * BS))
        f_all[at, :] = jnp.where(lane8 < HALF, pltpu.roll(low, HALF, 1), high) * F32(1.0 / (255.0 * 255.0 * BS * BS))
    right = right_ref[...]

    def both(x):
        part = dot(x, right)
        return jnp.concatenate([part[:, :n_cols], part[:, n_cols:]], axis=0)

    c = c_all[...]
    spread = both(c)
    ring_ref[...] = dot(own_ref[...], spread)
    coarse = dot(left_ref[...], spread)
    back = (1.5 - coarse) * c - 0.5 * f_all[...]
    last_ref[...] = dot(own_ref[...], both(back))
    ring = ring_ref.shape[0]

    def expand(ref, t):
        if t < tiles:
            pick = iota((ring, LANES), 1) // BS + (col * (cols // BS) + t * (LANES // BS))
        else:
            pick = jnp.where(iota((ring, LANES), 1) < HALF, (col + 1) * (cols // BS), col * (cols // BS) - 1)
        pick = jnp.clip(pick, 0, n_cols - 1)
        parts = [jnp.take_along_axis(ref[i : i + 8, :], pick[i : i + 8], axis=1) for i in range(0, ring, 8)]
        return jnp.concatenate(parts, axis=0)

    def charge(t):
        value = expand(ring_ref, t)
        for i in range(cells):
            here = value[1 + i : 2 + i, :]
            up = value[i : 1 + i, :] - here
            down = value[2 + i : 3 + i, :] - here
            at = i * BS
            some = charge_ref[t, at : at + BS, :] - here * blurred_ref[t, at : at + BS, :]
            some = jnp.concatenate(
                [some[:8] - up * above_ref[t, i], some[8 : BS - 8], some[BS - 8 :] - down * below_ref[t, i]], axis=0
            )
            turned[t % 2, at : at + BS, :] = pltpu.roll(some, HALF, 1)

    def copy(g):
        span = slice(2 * g * LANES, 2 * (g + 1) * LANES)
        return pltpu.make_async_copy(staged.at[:, span], out_ref.at[:, span], sems.at[g])

    def finish(t):
        coarse = expand(ring_ref, t)[1 : 1 + cells] + expand(last_ref, t)[1 : 1 + cells]
        for a, n in chunks(0, rows, 128):
            at = slice(a, a + n)
            window = jnp.concatenate([upper[t, at, :], upper[t + 1, at, :]], axis=1)
            rest = jnp.concatenate([lower[t, at, :], lower[t + 1, at, :]], axis=1)
            twice = jnp.dot(window, band_ref[...], preferred_element_type=F32)
            once = jnp.dot(rest, band_ref[:, :LANES], preferred_element_type=F32)
            fine = twice[:, :LANES] + twice[:, LANES:] + once
            for i in range(n // BS):
                cell = slice(a + i * BS, a + (i + 1) * BS)
                value = dose_ref[t, cell, :] - fine[i * BS : (i + 1) * BS] - coarse[a // BS + i : a // BS + i + 1, :]
                staged[cell, t * LANES : (t + 1) * LANES] = value
        if t % 2:
            copy(t // 2).start()

    charge(tiles)
    first = tiles % 2
    for t in range(tiles + 1):
        if t == 0:
            ends[...] = turned[first]
        if t < tiles:
            charge(t)
        for a, n in chunks(0, rows):
            at = slice(a, a + n)
            before = turned[(t - 1) % 2, at, :] if t else ends[at, :]
            here = turned[t % 2, at, :] if t < tiles else ends[at, :]
            upper[t, at, :], lower[t, at, :] = halves(jnp.where(lane < HALF, before, here))
        if t:
            finish(t - 1)
    for g in range(tiles // 2):
        copy(g).wait()


def shards(coverage, fog_rows, fog_cols):
    rows, cols = coverage.shape
    row_count = lax.axis_size("row")
    col_count = lax.axis_size("col")
    tiles = cols // LANES
    back_rows, back_cols = rows // BS, cols // BS
    n_rows, n_cols = back_rows * row_count, back_cols * col_count
    ext = rows + 2 * EDGE
    if col_count != 2 or n_cols != LANES or row_count & (row_count - 1):
        raise ValueError("unsupported mesh")

    def move(value, target):
        both = [(r, c) for r in range(row_count) for c in range(col_count)]
        flat = [(r * col_count + c, target(r, c)) for r, c in both]
        return lax.ppermute(value, ("row", "col"), [(i, r * col_count + c) for i, (r, c) in flat])

    def shape(*dims, dtype=F32):
        return jax.ShapeDtypeStruct(dims, dtype)

    def call(kernel, outs, ins, *args, scratch=(), mib=16, name=None, aliases={}, ops=1):
        return pl.pallas_call(
            kernel,
            out_shape=outs,
            in_specs=ins,
            out_specs=(VMEM,) * len(outs),
            scratch_shapes=list(scratch),
            input_output_aliases=aliases,
            compiler_params=pltpu.CompilerParams(vmem_limit_bytes=mib << 20),
            cost_estimate=pl.CostEstimate(flops=ops * rows * cols, bytes_accessed=ops * rows * cols, transcendentals=0),
            name=name,
        )(*args)

    wide = shape(tiles + 1, ext, LANES)
    own_tiles = shape(tiles + 1, rows, LANES)
    hbm = pl.BlockSpec(memory_space=pltpu.HBM)
    in_hbm = [pltpu.with_memory_space_constraint(x, pltpu.HBM) for x in (coverage, fog_rows, fog_cols)]
    cover, shifted, c_sums, edge, first_rows, second_rows, band, left, own, right = call(
        load_kernel,
        (
            wide,
            shape(tiles, rows, LANES, dtype=BF16),
            shape(back_rows, LANES),
            shape(rows, LANES),
            shape(tiles, EDGE, LANES),
            shape(tiles, EDGE, LANES),
            shape(2 * LANES, 2 * LANES, dtype=BF16),
            shape(n_rows, 2 * n_rows),
            shape(16, 2 * n_rows),
            shape(n_cols, 2 * n_cols),
        ),
        [hbm] * 3,
        *in_hbm,
        scratch=[
            pltpu.VMEM((rows, cols), jnp.int32),
            pltpu.VMEM((tiles, back_rows, 8, LANES), F32),
            pltpu.VMEM(fog_rows.shape, F32),
            pltpu.VMEM(fog_cols.shape, F32),
            pltpu.SemaphoreType.DMA((4 + 2,)),
        ],
        name="load",
    )

    side = move(edge, lambda r, c: (r, 1 - c))
    corners = [side[None, :EDGE], side[None, rows - EDGE :]]

    first = move(jnp.concatenate([first_rows] + corners, axis=0), lambda r, c: (r ^ 1, c))
    second = move(
        jnp.concatenate([second_rows] + corners, axis=0),
        lambda r, c: (r, 1 - c) if r in (0, row_count - 1) else ((r + 1, c) if r % 2 else (r - 1, c)),
    )
    cover, fine, across, part = call(
        inner_kernel,
        (wide, wide, shape(tiles + 1, ext + 2 * PAD, LANES), shape(back_rows, LANES)),
        [VMEM] * 5,
        side,
        band,
        c_sums,
        cover,
        shifted,
        scratch=[pltpu.VMEM((2, rows, LANES), BF16)],
        aliases={3: 0},
        ops=64,
        name="inner",
    )
    cover, fine, sums = call(
        outer_kernel,
        (wide, wide, shape(back_rows, LANES)),
        [VMEM] * 7,
        first,
        second,
        band,
        across,
        part,
        cover,
        fine,
        scratch=[
            pltpu.VMEM((tiles + 1, 4 * PAD + 4 * EDGE, LANES), F32),
            pltpu.VMEM(((tiles + 1) * 2 * EDGE, 2 * LANES), BF16),
        ],
        aliases={5: 0, 6: 1},
        name="outer",
    )

    few = shape(tiles + 1, back_rows, 8, LANES)
    blurred, above, below = call(
        spread_kernel, (own_tiles, few, few), [VMEM], cover, mib=4, ops=32, name="spread"
    )
    gathered = sums
    bit = 1
    while bit < row_count:
        other = move(gathered, lambda r, c: (r ^ bit, 1 - c))
        gathered = jnp.concatenate([gathered, other], axis=0)
        if bit == 1:
            dose, charge = call(
                first_dose_kernel,
                (shape(tiles, rows, LANES), own_tiles),
                [VMEM] * 3,
                cover,
                fine,
                gathered,
                scratch=[pltpu.VMEM((tiles + 1, ext, LANES), F32)],
                mib=8,
                ops=32,
                name="dose",
            )
        bit *= 2
    gathered = jnp.concatenate([gathered, move(gathered, lambda r, c: (r, 1 - c))], axis=0)

    return pl.pallas_call(
        last_kernel,
        out_shape=shape(rows, cols),
        in_specs=[VMEM] * 10,
        out_specs=pl.BlockSpec(memory_space=pltpu.HBM),
        scratch_shapes=[
            pltpu.VMEM((n_rows, n_cols), F32),
            pltpu.VMEM((n_rows, n_cols), F32),
            pltpu.VMEM((16, n_cols), F32),
            pltpu.VMEM((16, n_cols), F32),
            pltpu.VMEM((tiles + 1, rows, LANES), BF16),
            pltpu.VMEM((tiles + 1, rows, LANES), BF16),
            pltpu.VMEM((2, rows, LANES), F32),
            pltpu.VMEM((rows, LANES), F32),
            pltpu.VMEM((rows, cols), F32),
            pltpu.SemaphoreType.DMA((tiles // 2,)),
        ],
        compiler_params=pltpu.CompilerParams(vmem_limit_bytes=16 << 20),
        name="last",
    )(gathered, left, own, right, band, dose, charge, blurred, above, below)


def solution(mesh):
    in_specs = (P(("stripe", "row"), "col"), P(), P())
    out_specs = P(("stripe", "row"), "col")
    return jax.shard_map(shards, mesh=mesh, in_specs=in_specs, out_specs=out_specs, check_vma=False)
```

time: 158 us -> 30.8 us (0.19); the launches traced: 155 us -> 30.6 us
  other arithmetic: 50.8 us -> 0.02 us
  local copies, waits for them, and re-layouts: 43.6 us -> 0.01 us
  blocking collectives: 38.8 us -> 0 us
  Pallas kernels: 0 us -> 13.3 us
  starting transfers between devices: 19 us -> 11.9 us
  waiting for transfers between devices: 1.07 us -> 5.33 us
    all_gather x2 -> x0, blocking collectives: 38.8 us -> none  [shards(): stacked = lax.all_gather(back, ('row', 'col'), axis=0, tiled=True)]
    add x5 -> x0, other arithmetic: 27.5 us -> none  [the longest x2 16.5 us: blur_padded(): across = across + taps[index] * padded[index:index + rows, :]]
    add x4 -> x0, local copies, waits for them, and re-layouts: 23.7 us -> none  [spread_add(): field.reshape(rows // size, size, cols // size, size)]
    pallas_call x0 -> x6, Pallas kernels: none -> 13.3 us  [the longest x5 9.3 us: call(): pl.pallas_call(kernel, out_shape=outs, in_specs=ins, out_specs=(VMEM,) *...]
    mul x1 -> x0, other arithmetic: 10.9 us -> none  [shards(): charge = dose * cover]
    reshape x4 -> x0, local copies, waits for them, and re-layouts: 9.77 us -> none  [the longest x2 9.57 us: block_mean(): field.reshape(rows // size, size, cols // size, size).sum(axis=(1, 3))]
    reduce_sum x9 -> x0, other arithmetic: 9.46 us -> none  [the longest x6 8.62 us: block_mean(): field.reshape(rows // size, size, cols // size, size).sum(axis=(1, 3))]
    ppermute x8 -> x7, starting transfers between devices: 19 us -> 11.9 us  [move(): lax.ppermute(value, ('row', 'col'), [(i, r * col_count + c) for i, (r, c)...]
  transfers between devices with their start and end apart: 8 -> 7, of which waited for: 1 -> 5; matrix products, arithmetic and copies ran while one was open for 24% -> 0% of each run, Pallas kernels for 0% -> 17%
where the time goes in v2:
time: 30.8 us; the launch traced here: 30.6 us
  Pallas kernels  13.3 us (43%)
  starting transfers between devices  11.9 us (39%)
  waiting for transfers between devices  5.33 us (17%)
    ppermute x7, starting transfers between devices, move(): lax.ppermute(value, ('row', 'col'), [(i, r * col_count + c) for i, (r, c)...  11.9 us
    pallas_call x5, Pallas kernels, call(): pl.pallas_call(kernel, out_shape=outs, in_specs=ins, out_specs=(VMEM,) *...  9.3 us
    ppermute x7, waiting for transfers between devices, move(): lax.ppermute(value, ('row', 'col'), [(i, r * col_count + c) for i, (r, c)...  5.33 us
    pallas_call x1, Pallas kernels, shards(): pl.pallas_call(last_kernel, out_shape=shape(rows, cols), in_specs=[VMEM]...  4.03 us
  transfers between devices with their start and end apart: 7, of which 5 were waited for; matrix products, arithmetic and copies ran while one was open for 0% of the time, Pallas kernels for 17%

profile of v2, /device:TPU:0, one launch (start us, length us, event | category | flops | bytes accessed | tf_op | source)
XLA Modules:
  0.0 30.6 jit_solution(14960478705287110216)
XLA Ops:
  0.0 3.1 %load.1 = (f32[17,272,128]{2,1,0:T(8,128)S(1)}, bf16[16,256,128]{2,1,0:T(8,128)(2,1)S(1)}, f32[8,128]{1,0:T(8,128)S(1)}, f32[256,128]{1,0:T(8,128)S(1)}, f32[16,...) custom-call(s32[256,2048]{1,0:T(8,128)} %cov_ref.1, ...), custom_call_target="tpu_custom_call" | custom-call | flops 524288 | bytes 524288 | tf_op jit(solution)/shard_map/load/pallas_call | solution.py:440
  3.1 0.6 %collective-permute-start = (f32[256,128]{1,0:T(8,128)S(1)}, f32[256,128]{1,0:T(8,128)S(1)}, u32[]{:S(2)}, u32[]{:S(2)}) collective-permute-start(f32[256,128]{1,0:T(8,128)S(1)} %get-tuple-element.28), channel_id=1, source_target_pairs={{0,1},{1,0},{2,3},{3,2},{4,5},{5,4},{6,7},{7,6},{8,9},{9,8},{10,11... | collective-permute-start | bytes 393224 | tf_op jit(solution)/shard_map/ppermute | solution.py:434
  3.7 1.0 %collective-permute-done.side_ref = f32[256,128]{1,0:T(8,128)S(1)} collective-permute-done((f32[256,128]{1,0:T(8,128)S(1)}, f32[256,128]{1,0:T(8,128)S(1)}, u32[]{:S(2)}, u32[]{:S(2)}) %collective-permute-start) | collective-permute-done | bytes 131104 | tf_op jit(solution)/shard_map/ppermute | solution.py:434
  4.7 0.4 %collective-permute-start.2 = (f32[18,8,128]{2,1,0:T(8,128)S(1)}, f32[18,8,128]{2,1,0:T(8,128)S(1)}, u32[]{:S(2)}, u32[]{:S(2)}) collective-permute-start(f32[18,8,128]{2,1,0:T(8,128)S(1)} %get-tuple-element.51), channel_id=1, source_target_pairs={{0,1},{1,0},{2,4},{3,5},{4,2},{5,3},{6,8},{7,9},{8,6},{9,7},{10,12... | collective-permute-start | bytes 221192 | tf_op jit(solution)/shard_map/ppermute | solution.py:434
  5.1 4.0 %collective-permute-start.1 = (f32[18,8,128]{2,1,0:T(8,128)S(1)}, f32[18,8,128]{2,1,0:T(8,128)S(1)}, u32[]{:S(2)}, u32[]{:S(2)}) collective-permute-start(f32[18,8,128]{2,1,0:T(8,128)S(1)} %get-tuple-element.52), channel_id=1, source_target_pairs={{0,2},{1,3},{2,0},{3,1},{4,6},{5,7},{6,4},{7,5},{8,10},{9,11},{10,... | collective-permute-start | bytes 221192 | tf_op jit(solution)/shard_map/ppermute | solution.py:434
  9.2 2.5 %inner.1 = (f32[17,272,128]{2,1,0:T(8,128)S(1)}, f32[17,272,128]{2,1,0:T(8,128)S(1)}, f32[17,288,128]{2,1,0:T(8,128)S(1)}, f32[8,128]{1,0:T(8,128)S(1)}) custom-call(f32[256,128]{1,0:T(8,128)S(1)} %collective-permute-done.side_ref, bf16[256,256]{1,0:T(8,128)(2,1)S(1)} %get-tuple-element.30.band_ref, ...), custom_call_target="tpu_custom_call", output_to_operand_aliasing={{0}: (3, {})} | custom-call | flops 33554432 | bytes 33554432 | tf_op jit(solution)/shard_map/inner/pallas_call | solution.py:440
  11.6 0.0 collective-permute-done.2.second_ref
  11.6 0.3 %collective-permute-done.1.first_ref = f32[18,8,128]{2,1,0:T(8,128)S(1)} collective-permute-done((f32[18,8,128]{2,1,0:T(8,128)S(1)}, f32[18,8,128]{2,1,0:T(8,128)S(1)}, u32[]{:S(2)}, u32[]{:S(2)}) %collective-permute-start.1) | collective-permute-done | bytes 73760 | tf_op jit(solution)/shard_map/ppermute | solution.py:434
  12.0 0.8 %outer.1 = (f32[17,272,128]{2,1,0:T(8,128)S(1)}, f32[17,272,128]{2,1,0:T(8,128)S(1)}, f32[8,128]{1,0:T(8,128)S(1)}) custom-call(f32[18,8,128]{2,1,0:T(8,128)S(1)} %collective-permute-done.1.first_ref, f32[18,8,128]{2,1,0:T(8,128)S(1)} %collective-permute-done.2.second_ref, ...), custom_call_target="tpu_custom_call", output_to_operand_aliasing={{0}: (5, {}), {1}: (6, {})} | custom-call | flops 524288 | bytes 524288 | tf_op jit(solution)/shard_map/outer/pallas_call | solution.py:440
  12.8 2.2 %collective-permute-start.3 = (f32[8,128]{1,0:T(8,128)S(1)}, f32[8,128]{1,0:T(8,128)S(1)}, u32[]{:S(2)}, u32[]{:S(2)}) collective-permute-start(f32[8,128]{1,0:T(8,128)S(1)} %get-tuple-element.38), channel_id=1, source_target_pairs={{0,3},{1,2},{2,1},{3,0},{4,7},{5,6},{6,5},{7,4},{8,11},{9,10},{10,... | collective-permute-start | bytes 12296 | tf_op jit(solution)/shard_map/ppermute | solution.py:434
  15.0 1.3 %collective-permute-done.3 = f32[8,128]{1,0:T(8,128)S(1)} collective-permute-done((f32[8,128]{1,0:T(8,128)S(1)}, f32[8,128]{1,0:T(8,128)S(1)}, u32[]{:S(2)}, u32[]{:S(2)}) %collective-permute-start.3) | collective-permute-done | bytes 4128 | tf_op jit(solution)/shard_map/ppermute | solution.py:434
  16.3 1.9 %collective-permute-start.4 = (f32[16,128]{1,0:T(8,128)S(1)}, f32[16,128]{1,0:T(8,128)S(1)}, u32[]{:S(2)}, u32[]{:S(2)}) collective-permute-start(f32[16,128]{1,0:T(8,128)S(1)} %get-tuple-element.53.after_ref), channel_id=1, source_target_pairs={{0,5},{1,4},{2,7},{3,6},{4,1},{5,0},{6,3},{7,2},{8,13},{9,12},{10,... | collective-permute-start | bytes 24584 | tf_op jit(solution)/shard_map/ppermute | solution.py:434
  18.2 1.4 %spread.1 = (f32[17,256,128]{2,1,0:T(8,128)S(1)}, f32[17,8,8,128]{3,2,1,0:T(8,128)S(1)}, f32[17,8,8,128]{3,2,1,0:T(8,128)S(1)}) custom-call(f32[17,272,128]{2,1,0:T(8,128)S(1)} %get-tuple-element.42.cover_ref), custom_call_target="tpu_custom_call" | custom-call | flops 16777216 | bytes 16777216 | tf_op jit(solution)/shard_map/spread/pallas_call | solution.py:440
  19.5 1.5 %dose.1 = (f32[16,256,128]{2,1,0:T(8,128)S(1)}, f32[17,256,128]{2,1,0:T(8,128)S(1)}) custom-call(f32[17,272,128]{2,1,0:T(8,128)S(1)} %get-tuple-element.42.cover_ref, f32[17,272,128]{2,1,0:T(8,128)S(1)} %get-tuple-element.43.fine_ref, f32[16,128]{1,0:T(8,128)S(1)} %get-tuple-element.53.after_ref), custom_call_target="tpu_custom_call" | custom-call | flops 16777216 | bytes 16777216 | tf_op jit(solution)/shard_map/dose/pallas_call | solution.py:440
  21.0 0.0 collective-permute-done.4
  21.0 2.7 %collective-permute-start.5 = (f32[32,128]{1,0:T(8,128)S(1)}, f32[32,128]{1,0:T(8,128)S(1)}, u32[]{:S(2)}, u32[]{:S(2)}) collective-permute-start(f32[32,128]{1,0:T(8,128)S(1)} %pad_maximum_fusion.5), channel_id=1, source_target_pairs={{0,9},{1,8},{2,11},{3,10},{4,13},{5,12},{6,15},{7,14},{8,1},{9,0},... | collective-permute-start | bytes 49160 | tf_op jit(solution)/shard_map/ppermute | solution.py:434
  23.7 1.7 %collective-permute-done.5 = f32[32,128]{1,0:T(8,128)S(1)} collective-permute-done((f32[32,128]{1,0:T(8,128)S(1)}, f32[32,128]{1,0:T(8,128)S(1)}, u32[]{:S(2)}, u32[]{:S(2)}) %collective-permute-start.5) | collective-permute-done | bytes 16416 | tf_op jit(solution)/shard_map/ppermute | solution.py:434
  25.4 0.2 collective-permute-start.6
  25.6 1.0 %collective-permute-done.6 = f32[64,128]{1,0:T(8,128)S(1)} collective-permute-done((f32[64,128]{1,0:T(8,128)S(1)}, f32[64,128]{1,0:T(8,128)S(1)}, u32[]{:S(2)}, u32[]{:S(2)}) %collective-permute-start.6) | collective-permute-done | bytes 32800 | tf_op jit(solution)/shard_map/ppermute | solution.py:434
  26.6 4.0 %last.1 = f32[256,2048]{1,0:T(8,128)} custom-call(f32[128,128]{1,0:T(8,128)S(1)} %constant_dynamic-update-slice_fusion.2.gathered_ref, f32[64,128]{1,0:T(8,128)S(1)} %get-tuple-element.39.left_ref, f32[16,128]{1,0:T(8,128)S(1)} %get-tuple-element.40.own_ref, f32[128,256]{1,0:T(8,128)S(1)} %get-tuple-element.41.right_ref, ...), custom_call_target="tpu_custom_call" | custom-call | tf_op jit(solution)/shard_map/last/pallas_call | solution.py:548
  (9 shorter events, 0.0 us)
Async XLA Ops:
  3.1 1.5 %collective-permute-start = (f32[256,128]{1,0:T(8,128)S(1)}, f32[256,128]{1,0:T(8,128)S(1)}, u32[]{:S(2)}, u32[]{:S(2)}) collective-permute-start(f32[256,128]{1,0:T(8,128)S(1)} %get-tuple-element.28), channel_id=1, source_target_pairs={{0,1},{1,0},{2,3},{3,2},{4,5},{5,4},{6,7},{7,6},{8,9},{9,8},{10,11... | collective-permute-start | bytes 393224 | tf_op jit(solution)/shard_map/ppermute | solution.py:434
  4.7 6.9 %collective-permute-start.2 = (f32[18,8,128]{2,1,0:T(8,128)S(1)}, f32[18,8,128]{2,1,0:T(8,128)S(1)}, u32[]{:S(2)}, u32[]{:S(2)}) collective-permute-start(f32[18,8,128]{2,1,0:T(8,128)S(1)} %get-tuple-element.51), channel_id=1, source_target_pairs={{0,1},{1,0},{2,4},{3,5},{4,2},{5,3},{6,8},{7,9},{8,6},{9,7},{10,12... | collective-permute-start | bytes 221192 | tf_op jit(solution)/shard_map/ppermute | solution.py:434
  5.1 6.8 %collective-permute-start.1 = (f32[18,8,128]{2,1,0:T(8,128)S(1)}, f32[18,8,128]{2,1,0:T(8,128)S(1)}, u32[]{:S(2)}, u32[]{:S(2)}) collective-permute-start(f32[18,8,128]{2,1,0:T(8,128)S(1)} %get-tuple-element.52), channel_id=1, source_target_pairs={{0,2},{1,3},{2,0},{3,1},{4,6},{5,7},{6,4},{7,5},{8,10},{9,11},{10,... | collective-permute-start | bytes 221192 | tf_op jit(solution)/shard_map/ppermute | solution.py:434
  12.8 3.5 %collective-permute-start.3 = (f32[8,128]{1,0:T(8,128)S(1)}, f32[8,128]{1,0:T(8,128)S(1)}, u32[]{:S(2)}, u32[]{:S(2)}) collective-permute-start(f32[8,128]{1,0:T(8,128)S(1)} %get-tuple-element.38), channel_id=1, source_target_pairs={{0,3},{1,2},{2,1},{3,0},{4,7},{5,6},{6,5},{7,4},{8,11},{9,10},{10,... | collective-permute-start | bytes 12296 | tf_op jit(solution)/shard_map/ppermute | solution.py:434
  16.3 4.7 %collective-permute-start.4 = (f32[16,128]{1,0:T(8,128)S(1)}, f32[16,128]{1,0:T(8,128)S(1)}, u32[]{:S(2)}, u32[]{:S(2)}) collective-permute-start(f32[16,128]{1,0:T(8,128)S(1)} %get-tuple-element.53.after_ref), channel_id=1, source_target_pairs={{0,5},{1,4},{2,7},{3,6},{4,1},{5,0},{6,3},{7,2},{8,13},{9,12},{10,... | collective-permute-start | bytes 24584 | tf_op jit(solution)/shard_map/ppermute | solution.py:434
  21.0 4.3 %collective-permute-start.5 = (f32[32,128]{1,0:T(8,128)S(1)}, f32[32,128]{1,0:T(8,128)S(1)}, u32[]{:S(2)}, u32[]{:S(2)}) collective-permute-start(f32[32,128]{1,0:T(8,128)S(1)} %pad_maximum_fusion.5), channel_id=1, source_target_pairs={{0,9},{1,8},{2,11},{3,10},{4,13},{5,12},{6,15},{7,14},{8,1},{9,0},... | collective-permute-start | bytes 49160 | tf_op jit(solution)/shard_map/ppermute | solution.py:434
  25.4 1.2 %collective-permute-start.6 = (f32[64,128]{1,0:T(8,128)S(1)}, f32[64,128]{1,0:T(8,128)S(1)}, u32[]{:S(2)}, u32[]{:S(2)}) collective-permute-start(f32[64,128]{1,0:T(8,128)S(1)} %pad_maximum_fusion.4), channel_id=1, source_target_pairs={{0,1},{1,0},{2,3},{3,2},{4,5},{5,4},{6,7},{7,6},{8,9},{9,8},{10,11... | collective-permute-start | bytes 98312 | tf_op jit(solution)/shard_map/ppermute | solution.py:434

commit v3 on v2

--- a/solution.py
+++ b/solution.py
@@ -123,7 +123,26 @@
     return [(a, min(size, stop - a)) for a in range(start, stop, size)]
 
 
-def load_kernel(cov_ref, fog_rows_ref, fog_cols_ref, cover_ref, shifted, sums_ref, edge_ref, first_ref, second_ref, band_ref, left_ref, own_ref, right_ref, loaded, cells_of, fog_r, fog_c, sems):
+def edges_kernel(cov_ref, edge_ref, first_ref, second_ref, tile, strips, sems):
+    rows, cols = cov_ref.shape
+    tiles = cols // LANES
+    odd = lax.rem(lax.axis_index("row"), 2)
+    over = pl.ds(pl.multiple_of((1 - lax.axis_index("col")) * (cols - LANES), LANES), LANES)
+    copies = [pltpu.make_async_copy(cov_ref.at[:, over], tile, sems.at[0])]
+    for i, start in enumerate((1 - odd, odd)):
+        span = pl.ds(pl.multiple_of(start * (rows - EDGE), EDGE), EDGE)
+        copies.append(pltpu.make_async_copy(cov_ref.at[span], strips.at[i], sems.at[1 + i]))
+    for copy in copies:
+        copy.start()
+    for copy in copies:
+        copy.wait()
+    edge_ref[...] = tile[...].astype(F32)
+    for t in range(tiles):
+        first_ref[t] = strips[0, :, t * LANES : (t + 1) * LANES].astype(F32)
+        second_ref[t] = strips[1, :, t * LANES : (t + 1) * LANES].astype(F32)
+
+
+def load_kernel(cov_ref, fog_rows_ref, fog_cols_ref, side_ref, cover_ref, window, sums_ref, band_ref, left_ref, own_ref, right_ref, loaded, cells_of, fog_r, fog_c, sems):
     rows, cols = cov_ref.shape
     tiles = cols // LANES
     pieces = sems.shape[0] - 2
@@ -138,7 +157,8 @@
         pltpu.make_async_copy(fog_rows_ref, fog_r, sems.at[pieces]),
         pltpu.make_async_copy(fog_cols_ref, fog_c, sems.at[pieces + 1]),
     ]
-    for copy in fogs + copies[:2]:
+    ahead = 3
+    for copy in fogs + copies[:ahead]:
         copy.start()
     tap = tap_of(jnp.abs(iota((2 * LANES, LANES), 0) - HALF - iota((2 * LANES, LANES), 1)))
     band_ref[:, :LANES], band_ref[:, LANES:] = halves(tap)
@@ -148,60 +168,53 @@
     prep(place, fog_r[...], fog_c[...], left_ref, own_ref, right_ref)
     lane = iota((1, LANES), 1)
     per = LANES // BS
+    touches = (lane < HALF) == (lax.axis_index("col") == 0)
+
+    def put(t, at, value):
+        window[t, at, :LANES] = value
+        window[(t - 1) % (tiles + 1), at, LANES:] = value
+
     for p, copy in enumerate(copies):
         copy.wait()
-        if p + 2 < pieces:
-            copies[p + 2].start()
-        at = slice(EDGE + p * part, EDGE + (p + 1) * part)
-        before = None
+        if p + ahead < pieces:
+            copies[p + ahead].start()
+        at = slice(p * part, (p + 1) * part)
+        side = jnp.where(touches, side_ref[at, :], 0.0)
+        cover_ref[tiles, EDGE + p * part : EDGE + (p + 1) * part, :] = side
+        side = pltpu.roll(side, HALF, 1)
+        before = side
         for t in range(tiles):
-            value = loaded[p * part : (p + 1) * part, t * LANES : (t + 1) * LANES].astype(F32)
-            cover_ref[t, at, :] = value
+            value = loaded[at, t * LANES : (t + 1) * LANES].astype(F32)
+            cover_ref[t, EDGE + p * part : EDGE + (p + 1) * part, :] = value
             here = pltpu.roll(value, HALF, 1)
-            if t:
-                shifted[t, p * part : (p + 1) * part, :] = jnp.where(lane < HALF, before, here).astype(BF16)
+            put(t, at, jnp.where(lane < HALF, before, here).astype(BF16))
             before = here
             for i in range(part // BS):
                 cell = value[i * BS : (i + 1) * BS]
                 cells_of[t, p * (part // BS) + i] = sum(cell[b : b + 8] for b in range(8, BS, 8)) + cell[:8]
-    edge_ref[...] = cover_ref[(1 - lax.axis_index("col")) * (tiles - 1), EDGE : EDGE + rows, :]
-    even = lax.rem(lax.axis_index("row"), 2) == 0
+        put(tiles, at, jnp.where(lane < HALF, before, side).astype(BF16))
     spot = iota((8, LANES), 1)
     sums = jnp.zeros((8, LANES), F32)
     for t in range(tiles):
-        top = cover_ref[t, EDGE : 2 * EDGE, :]
-        low = cover_ref[t, rows : rows + EDGE, :]
-        first_ref[t] = jnp.where(even, low, top)
-        second_ref[t] = jnp.where(even, top, low)
         cell = fold([cells_of[t, i] for i in range(rows // BS)], (spot % per) * BS)
         sums = jnp.where(spot // per == t, cell, sums)
     sums_ref[...] = sums
 
 
-def inner_kernel(side_ref, band_ref, c_ref, cover_in, shifted, cover_ref, fine_ref, across, sums_ref, ends):
-    tiles = cover_ref.shape[0] - 1
-    rows = side_ref.shape[0]
-    lane = iota((1, LANES), 1)
+def inner_kernel(window, band_ref, c_ref, cover_in, fine_ref, across, sums_ref):
+    tiles = cover_in.shape[0] - 1
+    rows = window.shape[1]
     cells = rows // BS
     per = LANES // BS
     spot = iota((cells, LANES), 1)
     pick = (spot % per) * BS
-    own = slice(EDGE, EDGE + rows)
-    value = jnp.where((lane < HALF) == (lax.axis_index("col") == 0), side_ref[...], 0.0)
-    cover_ref[tiles, own, :] = value
-    side = pltpu.roll(value, HALF, 1)
-    ends[0] = jnp.where(lane < HALF, side, pltpu.roll(cover_in[0, own, :], HALF, 1)).astype(BF16)
-    ends[1] = jnp.where(lane < HALF, pltpu.roll(cover_in[tiles - 1, own, :], HALF, 1), side).astype(BF16)
-
-    def tile(t):
-        return ends.at[0] if t in (0, tiles + 1) else ends.at[1] if t == tiles else shifted.at[t]
-
-    def columns(t):
-        left, right = tile(t), tile(t + 1)
-        for a, n in chunks(0, rows, 128):
-            window = jnp.concatenate([left[a : a + n, :], right[a : a + n, :]], axis=1)
-            both = jnp.dot(window, band_ref[...], preferred_element_type=F32)
-            across[t, PAD + EDGE + a : PAD + EDGE + a + n, :] = both[:, :LANES] + both[:, LANES:]
+
+    def columns(t, count):
+        part = window[t : t + count].reshape(count * rows, 2 * LANES)
+        both = jnp.dot(part, band_ref[...], preferred_element_type=F32)
+        for i in range(count):
+            mine = both[i * rows : (i + 1) * rows]
+            across[t + i, PAD + EDGE : PAD + EDGE + rows, :] = mine[:, :LANES] + mine[:, LANES:]
 
     def down(t):
         parts = []
@@ -217,11 +230,13 @@
             sums_ref[...] = jnp.where(spot // per == t + tiles, f, sums_ref[...])
 
     sums_ref[...] = c_ref[...]
-    columns(0)
-    for t in range(tiles + 1):
-        if t < tiles:
-            columns(t + 1)
-        down(t)
+    groups = chunks(0, tiles + 1, 2)
+    columns(*groups[0])
+    for g, (start, count) in enumerate(groups):
+        if g + 1 < len(groups):
+            columns(*groups[g + 1])
+        for t in range(start, start + count):
+            down(t)
 
 
 def outer_kernel(first_ref, second_ref, band_ref, across_ref, part_ref, cover_in, fine_in, cover_ref, fine_ref, sums_ref, across, window):
@@ -287,7 +302,8 @@
     sums_ref[...] = part_ref[...] + total
 
 
-def spread_kernel(cover_ref, blurred_ref, above_ref, below_ref):
+def spread_kernel(cover_ref, after_ref, blurred_ref, above_ref, below_ref):
+    del after_ref
     tiles, ext = cover_ref.shape[0] - 1, cover_ref.shape[1]
     rows = ext - 2 * EDGE
     scale = 0.5 / 255.0
@@ -324,7 +340,7 @@
             )
 
 
-def last_kernel(gathered_ref, left_ref, own_ref, right_ref, band_ref, dose_ref, charge_ref, blurred_ref, above_ref, below_ref, out_ref, c_all, f_all, ring_ref, last_ref, upper, lower, turned, ends, staged, sems):
+def last_kernel(gathered_ref, left_ref, own_ref, right_ref, band_ref, dose_ref, charge_ref, blurred_ref, above_ref, below_ref, out_ref, c_all, f_all, ring_ref, last_ref, window, turned, ends, staged, sems):
     rows, cols = out_ref.shape
     tiles = cols // LANES
     n_rows, n_cols = c_all.shape
@@ -355,6 +371,7 @@
     coarse = dot(left_ref[...], spread)
     back = (1.5 - coarse) * c - 0.5 * f_all[...]
     last_ref[...] = dot(own_ref[...], both(back))
+
     ring = ring_ref.shape[0]
 
     def expand(ref, t):
@@ -379,40 +396,61 @@
             )
             turned[t % 2, at : at + BS, :] = pltpu.roll(some, HALF, 1)
 
-    def copy(g):
-        span = slice(2 * g * LANES, 2 * (g + 1) * LANES)
-        return pltpu.make_async_copy(staged.at[:, span], out_ref.at[:, span], sems.at[g])
-
-    def finish(t):
-        coarse = expand(ring_ref, t)[1 : 1 + cells] + expand(last_ref, t)[1 : 1 + cells]
-        for a, n in chunks(0, rows, 128):
-            at = slice(a, a + n)
-            window = jnp.concatenate([upper[t, at, :], upper[t + 1, at, :]], axis=1)
-            rest = jnp.concatenate([lower[t, at, :], lower[t + 1, at, :]], axis=1)
-            twice = jnp.dot(window, band_ref[...], preferred_element_type=F32)
-            once = jnp.dot(rest, band_ref[:, :LANES], preferred_element_type=F32)
-            fine = twice[:, :LANES] + twice[:, LANES:] + once
-            for i in range(n // BS):
-                cell = slice(a + i * BS, a + (i + 1) * BS)
-                value = dose_ref[t, cell, :] - fine[i * BS : (i + 1) * BS] - coarse[a // BS + i : a // BS + i + 1, :]
-                staged[cell, t * LANES : (t + 1) * LANES] = value
-        if t % 2:
-            copy(t // 2).start()
-
-    charge(tiles)
-    first = tiles % 2
-    for t in range(tiles + 1):
-        if t == 0:
-            ends[...] = turned[first]
+    def put(t, at, value):
+        for i, part in enumerate(halves(value)):
+            if t < tiles:
+                window[t, at, 2 * i * LANES : (2 * i + 1) * LANES] = part
+            if t:
+                window[t - 1, at, (2 * i + 1) * LANES : (2 * i + 2) * LANES] = part
+
+    def fill(t):
         if t < tiles:
             charge(t)
         for a, n in chunks(0, rows):
             at = slice(a, a + n)
             before = turned[(t - 1) % 2, at, :] if t else ends[at, :]
             here = turned[t % 2, at, :] if t < tiles else ends[at, :]
-            upper[t, at, :], lower[t, at, :] = halves(jnp.where(lane < HALF, before, here))
-        if t:
-            finish(t - 1)
+            put(t, at, jnp.where(lane < HALF, before, here))
+
+    def copy(g):
+        span = slice(2 * g * LANES, 2 * (g + 1) * LANES)
+        return pltpu.make_async_copy(staged.at[:, span], out_ref.at[:, span], sems.at[g])
+
+    def finish(g):
+        part = window[2 * g : 2 * g + 2].reshape(2 * rows, 4 * LANES)
+        band = band_ref[...]
+        both = jnp.dot(part, jnp.concatenate([band, band], axis=0), preferred_element_type=F32)
+        for t in (2 * g, 2 * g + 1):
+            fine = both[(t % 2) * rows : (t % 2 + 1) * rows]
+            coarse = expand(ring_ref, t)[1 : 1 + cells] + expand(last_ref, t)[1 : 1 + cells]
+            for i in range(cells):
+                at = slice(i * BS, (i + 1) * BS)
+                value = dose_ref[t, at, :] - fine[at, :LANES] - fine[at, LANES:] - coarse[i : i + 1, :]
+                staged[at, t * LANES : (t + 1) * LANES] = value
+        copy(g).start()
+
+    def stage(body):
+        pl.when(row >= 0)(body)
+
+    def start():
+        charge(tiles)
+        ends[...] = turned[tiles % 2]
+        for t in range(3):
+            fill(t)
+
+    stage(start)
+    for g in range(tiles // 2):
+
+        def step(g=g):
+            if g:
+                finish(g - 1)
+            for t in range(2 * g + 1, 2 * g + 3):
+                if t > 2:
+                    fill(t)
+
+        if g:
+            stage(step)
+    stage(lambda: finish(tiles // 2 - 1))
     for g in range(tiles // 2):
         copy(g).wait()
 
@@ -453,22 +491,42 @@
     own_tiles = shape(tiles + 1, rows, LANES)
     hbm = pl.BlockSpec(memory_space=pltpu.HBM)
     in_hbm = [pltpu.with_memory_space_constraint(x, pltpu.HBM) for x in (coverage, fog_rows, fog_cols)]
-    cover, shifted, c_sums, edge, first_rows, second_rows, band, left, own, right = call(
+    edge, first_rows, second_rows = call(
+        edges_kernel,
+        (shape(rows, LANES), shape(tiles, EDGE, LANES), shape(tiles, EDGE, LANES)),
+        [hbm],
+        in_hbm[0],
+        scratch=[
+            pltpu.VMEM((rows, LANES), jnp.int32),
+            pltpu.VMEM((2, EDGE, cols), jnp.int32),
+            pltpu.SemaphoreType.DMA((3,)),
+        ],
+        mib=2,
+        name="edges",
+    )
+
+    side = move(edge, lambda r, c: (r, 1 - c))
+    corners = [side[None, :EDGE], side[None, rows - EDGE :]]
+
+    first = move(jnp.concatenate([first_rows] + corners, axis=0), lambda r, c: (r ^ 1, c))
+    second = move(
+        jnp.concatenate([second_rows] + corners, axis=0),
+        lambda r, c: (r, 1 - c) if r in (0, row_count - 1) else ((r + 1, c) if r % 2 else (r - 1, c)),
+    )
+    cover, window, c_sums, band, left, own, right = call(
         load_kernel,
         (
             wide,
-            shape(tiles, rows, LANES, dtype=BF16),
+            shape(tiles + 1, rows, 2 * LANES, dtype=BF16),
             shape(back_rows, LANES),
-            shape(rows, LANES),
-            shape(tiles, EDGE, LANES),
-            shape(tiles, EDGE, LANES),
             shape(2 * LANES, 2 * LANES, dtype=BF16),
             shape(n_rows, 2 * n_rows),
             shape(16, 2 * n_rows),
             shape(n_cols, 2 * n_cols),
         ),
-        [hbm] * 3,
+        [hbm] * 3 + [VMEM],
         *in_hbm,
+        side,
         scratch=[
             pltpu.VMEM((rows, cols), jnp.int32),
             pltpu.VMEM((tiles, back_rows, 8, LANES), F32),
@@ -476,29 +534,18 @@
             pltpu.VMEM(fog_cols.shape, F32),
             pltpu.SemaphoreType.DMA((4 + 2,)),
         ],
+        mib=8,
         name="load",
     )
-
-    side = move(edge, lambda r, c: (r, 1 - c))
-    corners = [side[None, :EDGE], side[None, rows - EDGE :]]
-
-    first = move(jnp.concatenate([first_rows] + corners, axis=0), lambda r, c: (r ^ 1, c))
-    second = move(
-        jnp.concatenate([second_rows] + corners, axis=0),
-        lambda r, c: (r, 1 - c) if r in (0, row_count - 1) else ((r + 1, c) if r % 2 else (r - 1, c)),
-    )
-    cover, fine, across, part = call(
+    fine, across, part = call(
         inner_kernel,
-        (wide, wide, shape(tiles + 1, ext + 2 * PAD, LANES), shape(back_rows, LANES)),
-        [VMEM] * 5,
-        side,
+        (wide, shape(tiles + 1, ext + 2 * PAD, LANES), shape(back_rows, LANES)),
+        [VMEM] * 4,
+        window,
         band,
         c_sums,
         cover,
-        shifted,
-        scratch=[pltpu.VMEM((2, rows, LANES), BF16)],
-        aliases={3: 0},
-        ops=64,
+        mib=8,
         name="inner",
     )
     cover, fine, sums = call(
@@ -517,33 +564,46 @@
             pltpu.VMEM(((tiles + 1) * 2 * EDGE, 2 * LANES), BF16),
         ],
         aliases={5: 0, 6: 1},
+        mib=8,
         name="outer",
     )
 
     few = shape(tiles + 1, back_rows, 8, LANES)
-    blurred, above, below = call(
-        spread_kernel, (own_tiles, few, few), [VMEM], cover, mib=4, ops=32, name="spread"
-    )
+
+    def spread(after):
+        return call(
+            spread_kernel, (own_tiles, few, few), [VMEM] * 2, cover, after, mib=4, name="spread"
+        )
+
+    def first_dose(after):
+        return call(
+            first_dose_kernel,
+            (shape(tiles, rows, LANES), own_tiles),
+            [VMEM] * 3,
+            cover,
+            fine,
+            after,
+            scratch=[pltpu.VMEM((tiles + 1, ext, LANES), F32)],
+            mib=8,
+            name="dose",
+        )
+
+    pending = [spread, first_dose]
+    done = []
     gathered = sums
     bit = 1
     while bit < row_count:
         other = move(gathered, lambda r, c: (r ^ bit, 1 - c))
+        if bit > 1 and pending:
+            results = pending.pop(0)(gathered)
+            other, *results = lax.optimization_barrier((other, *results))
+            done += results
         gathered = jnp.concatenate([gathered, other], axis=0)
-        if bit == 1:
-            dose, charge = call(
-                first_dose_kernel,
-                (shape(tiles, rows, LANES), own_tiles),
-                [VMEM] * 3,
-                cover,
-                fine,
-                gathered,
-                scratch=[pltpu.VMEM((tiles + 1, ext, LANES), F32)],
-                mib=8,
-                ops=32,
-                name="dose",
-            )
         bit *= 2
     gathered = jnp.concatenate([gathered, move(gathered, lambda r, c: (r, 1 - c))], axis=0)
+    for work in pending:
+        done += work(gathered)
+    blurred, above, below, dose, charge = done
 
     return pl.pallas_call(
         last_kernel,
@@ -555,8 +615,7 @@
             pltpu.VMEM((n_rows, n_cols), F32),
             pltpu.VMEM((16, n_cols), F32),
             pltpu.VMEM((16, n_cols), F32),
-            pltpu.VMEM((tiles + 1, rows, LANES), BF16),
-            pltpu.VMEM((tiles + 1, rows, LANES), BF16),
+            pltpu.VMEM((tiles, rows, 4 * LANES), BF16),
             pltpu.VMEM((2, rows, LANES), F32),
             pltpu.VMEM((rows, LANES), F32),
             pltpu.VMEM((rows, cols), F32),

time: 30.8 us -> 28.2 us (0.916)
  starting transfers between devices: 11.9 us -> 7.83 us
  waiting for transfers between devices: 5.33 us -> 6.72 us
    ppermute x7, starting transfers between devices: 11.9 us -> 7.83 us  [move(): lax.ppermute(value, ('row', 'col'), [(i, r * col_count + c) for i, (r, c)...]
    ppermute x7, waiting for transfers between devices: 5.33 us -> 6.72 us  [move(): lax.ppermute(value, ('row', 'col'), [(i, r * col_count + c) for i, (r, c)...]
    pallas_call x5 -> x6, Pallas kernels: 9.3 us -> 9.85 us  [call(): pl.pallas_call(kernel, out_shape=outs, in_specs=ins, out_specs=(VMEM,) *...]
    pallas_call x1, Pallas kernels: 4.03 us -> 3.56 us  [shards(): pl.pallas_call(last_kernel, out_shape=shape(rows, cols), in_specs=[VMEM]...]
  transfers between devices with their start and end apart: 7 -> 7, of which waited for: 5 -> 5; matrix products, arithmetic and copies ran while one was open for 0% -> 0% of each run, Pallas kernels for 17% -> 29%
where the time goes in v3:
time: 28.2 us; the launch traced here: 28 us
  Pallas kernels  13.4 us (48%)
  starting transfers between devices  7.83 us (28%)
  waiting for transfers between devices  6.72 us (24%)
    pallas_call x6, Pallas kernels, call(): pl.pallas_call(kernel, out_shape=outs, in_specs=ins, out_specs=(VMEM,) *...  9.85 us
    ppermute x7, starting transfers between devices, move(): lax.ppermute(value, ('row', 'col'), [(i, r * col_count + c) for i, (r, c)...  7.83 us
    ppermute x7, waiting for transfers between devices, move(): lax.ppermute(value, ('row', 'col'), [(i, r * col_count + c) for i, (r, c)...  6.72 us
    pallas_call x1, Pallas kernels, shards(): pl.pallas_call(last_kernel, out_shape=shape(rows, cols), in_specs=[VMEM]...  3.56 us
  transfers between devices with their start and end apart: 7, of which 5 were waited for; matrix products, arithmetic and copies ran while one was open for 0% of the time, Pallas kernels for 29%

profile of v3, /device:TPU:0, one launch (start us, length us, event | category | flops | bytes accessed | tf_op | source)
XLA Modules:
  0.0 28.0 jit_solution(16149782158501367440)
XLA Ops:
  0.0 1.0 %edges.1 = (f32[256,128]{1,0:T(8,128)S(1)}, f32[16,8,128]{2,1,0:T(8,128)S(1)}, f32[16,8,128]{2,1,0:T(8,128)S(1)}) custom-call(s32[256,2048]{1,0:T(8,128)} %cov_ref.3), custom_call_target="tpu_custom_call" | custom-call | flops 524288 | bytes 524288 | tf_op jit(solution)/shard_map/edges/pallas_call | solution.py:478
  1.0 0.6 %collective-permute-start = (f32[256,128]{1,0:T(8,128)S(1)}, f32[256,128]{1,0:T(8,128)S(1)}, u32[]{:S(2)}, u32[]{:S(2)}) collective-permute-start(f32[256,128]{1,0:T(8,128)S(1)} %get-tuple-element.34), channel_id=1, source_target_pairs={{0,1},{1,0},{2,3},{3,2},{4,5},{5,4},{6,7},{7,6},{8,9},{9,8},{10,11... | collective-permute-start | bytes 393224 | tf_op jit(solution)/shard_map/ppermute | solution.py:472
  1.5 1.0 %collective-permute-done.side_ref = f32[256,128]{1,0:T(8,128)S(1)} collective-permute-done((f32[256,128]{1,0:T(8,128)S(1)}, f32[256,128]{1,0:T(8,128)S(1)}, u32[]{:S(2)}, u32[]{:S(2)}) %collective-permute-start) | collective-permute-done | bytes 131104 | tf_op jit(solution)/shard_map/ppermute | solution.py:472
  2.6 0.4 %collective-permute-start.2 = (f32[18,8,128]{2,1,0:T(8,128)S(1)}, f32[18,8,128]{2,1,0:T(8,128)S(1)}, u32[]{:S(2)}, u32[]{:S(2)}) collective-permute-start(f32[18,8,128]{2,1,0:T(8,128)S(1)} %get-tuple-element.65), channel_id=1, source_target_pairs={{0,1},{1,0},{2,4},{3,5},{4,2},{5,3},{6,8},{7,9},{8,6},{9,7},{10,12... | collective-permute-start | bytes 221192 | tf_op jit(solution)/shard_map/ppermute | solution.py:472
  3.0 4.0 %collective-permute-start.1 = (f32[18,8,128]{2,1,0:T(8,128)S(1)}, f32[18,8,128]{2,1,0:T(8,128)S(1)}, u32[]{:S(2)}, u32[]{:S(2)}) collective-permute-start(f32[18,8,128]{2,1,0:T(8,128)S(1)} %get-tuple-element.66), channel_id=1, source_target_pairs={{0,2},{1,3},{2,0},{3,1},{4,6},{5,7},{6,4},{7,5},{8,10},{9,11},{10,... | collective-permute-start | bytes 221192 | tf_op jit(solution)/shard_map/ppermute | solution.py:472
  7.0 3.0 %load.1 = (f32[17,272,128]{2,1,0:T(8,128)S(1)}, bf16[17,256,256]{2,1,0:T(8,128)(2,1)S(1)}, f32[8,128]{1,0:T(8,128)S(1)}, bf16[256,256]{1,0:T(8,128)(2,1)S(1)}, f...) custom-call(s32[256,2048]{1,0:T(8,128)} %cov_ref.3, f32[8,8]{1,0:T(8,128)} %fog_rows_ref.1, ...), custom_call_target="tpu_custom_call" | custom-call | flops 524288 | bytes 524288 | tf_op jit(solution)/shard_map/load/pallas_call | solution.py:478
  10.0 2.2 %inner.1 = (f32[17,272,128]{2,1,0:T(8,128)S(1)}, f32[17,288,128]{2,1,0:T(8,128)S(1)}, f32[8,128]{1,0:T(8,128)S(1)}) custom-call(bf16[17,256,256]{2,1,0:T(8,128)(2,1)S(1)} %get-tuple-element.37.window, bf16[256,256]{1,0:T(8,128)(2,1)S(1)} %get-tuple-element.36.band_ref, f32[8,128]{1,0:T(8,128)S(1)} %get-tuple-element.38.c_ref, ...), custom_call_target="tpu_custom_call" | custom-call | flops 524288 | bytes 524288 | tf_op jit(solution)/shard_map/inner/pallas_call | solution.py:478
  12.2 0.0 collective-permute-done.2.second_ref
  12.2 0.0 collective-permute-done.1.first_ref
  12.2 0.9 %outer.1 = (f32[17,272,128]{2,1,0:T(8,128)S(1)}, f32[17,272,128]{2,1,0:T(8,128)S(1)}, f32[8,128]{1,0:T(8,128)S(1)}) custom-call(f32[18,8,128]{2,1,0:T(8,128)S(1)} %collective-permute-done.1.first_ref, f32[18,8,128]{2,1,0:T(8,128)S(1)} %collective-permute-done.2.second_ref, ...), custom_call_target="tpu_custom_call", output_to_operand_aliasing={{0}: (5, {}), {1}: (6, {})} | custom-call | flops 524288 | bytes 524288 | tf_op jit(solution)/shard_map/outer/pallas_call | solution.py:478
  13.0 0.1 collective-permute-start.3
  13.1 3.0 %collective-permute-done.3 = f32[8,128]{1,0:T(8,128)S(1)} collective-permute-done((f32[8,128]{1,0:T(8,128)S(1)}, f32[8,128]{1,0:T(8,128)S(1)}, u32[]{:S(2)}, u32[]{:S(2)}) %collective-permute-start.3) | collective-permute-done | bytes 4128 | tf_op jit(solution)/shard_map/ppermute | solution.py:472
  16.1 0.8 %collective-permute-start.4 = (f32[16,128]{1,0:T(8,128)S(1)}, f32[16,128]{1,0:T(8,128)S(1)}, u32[]{:S(2)}, u32[]{:S(2)}) collective-permute-start(f32[16,128]{1,0:T(8,128)S(1)} %get-tuple-element.69.after_ref), channel_id=1, source_target_pairs={{0,5},{1,4},{2,7},{3,6},{4,1},{5,0},{6,3},{7,2},{8,13},{9,12},{10,... | collective-permute-start | bytes 24584 | tf_op jit(solution)/shard_map/ppermute | solution.py:472
  16.9 1.4 %spread.1 = (f32[17,256,128]{2,1,0:T(8,128)S(1)}, f32[17,8,8,128]{3,2,1,0:T(8,128)S(1)}, f32[17,8,8,128]{3,2,1,0:T(8,128)S(1)}) custom-call(f32[17,272,128]{2,1,0:T(8,128)S(1)} %get-tuple-element.44.cover_ref, f32[16,128]{1,0:T(8,128)S(1)} %get-tuple-element.69.after_ref), custom_call_target="tpu_custom_call" | custom-call | flops 524288 | bytes 524288 | tf_op jit(solution)/shard_map/spread/pallas_call | solution.py:478
  18.3 0.9 %collective-permute-done.4 = f32[16,128]{1,0:T(8,128)S(1)} collective-permute-done((f32[16,128]{1,0:T(8,128)S(1)}, f32[16,128]{1,0:T(8,128)S(1)}, u32[]{:S(2)}, u32[]{:S(2)}) %collective-permute-start.4) | collective-permute-done | bytes 8224 | tf_op jit(solution)/shard_map/ppermute | solution.py:472
  19.2 1.8 %collective-permute-start.5 = (f32[32,128]{1,0:T(8,128)S(1)}, f32[32,128]{1,0:T(8,128)S(1)}, u32[]{:S(2)}, u32[]{:S(2)}) collective-permute-start(f32[32,128]{1,0:T(8,128)S(1)} %get-tuple-element.63.after_ref), channel_id=1, source_target_pairs={{0,9},{1,8},{2,11},{3,10},{4,13},{5,12},{6,15},{7,14},{8,1},{9,0},... | collective-permute-start | bytes 49160 | tf_op jit(solution)/shard_map/ppermute | solution.py:472
  21.0 1.5 %dose.1 = (f32[16,256,128]{2,1,0:T(8,128)S(1)}, f32[17,256,128]{2,1,0:T(8,128)S(1)}) custom-call(f32[17,272,128]{2,1,0:T(8,128)S(1)} %get-tuple-element.44.cover_ref, f32[17,272,128]{2,1,0:T(8,128)S(1)} %get-tuple-element.49.fine_ref, f32[32,128]{1,0:T(8,128)S(1)} %get-tuple-element.63.after_ref), custom_call_target="tpu_custom_call" | custom-call | flops 524288 | bytes 524288 | tf_op jit(solution)/shard_map/dose/pallas_call | solution.py:478
  22.5 0.8 %collective-permute-done.5 = f32[32,128]{1,0:T(8,128)S(1)} collective-permute-done((f32[32,128]{1,0:T(8,128)S(1)}, f32[32,128]{1,0:T(8,128)S(1)}, u32[]{:S(2)}, u32[]{:S(2)}) %collective-permute-start.5) | collective-permute-done | bytes 16416 | tf_op jit(solution)/shard_map/ppermute | solution.py:472
  23.3 0.2 collective-permute-start.6
  23.5 1.0 %collective-permute-done.6 = f32[64,128]{1,0:T(8,128)S(1)} collective-permute-done((f32[64,128]{1,0:T(8,128)S(1)}, f32[64,128]{1,0:T(8,128)S(1)}, u32[]{:S(2)}, u32[]{:S(2)}) %collective-permute-start.6) | collective-permute-done | bytes 32800 | tf_op jit(solution)/shard_map/ppermute | solution.py:472
  24.5 3.6 %last.1 = f32[256,2048]{1,0:T(8,128)} custom-call(f32[128,128]{1,0:T(8,128)S(1)} %constant_dynamic-update-slice_fusion.5.gathered_ref, f32[64,128]{1,0:T(8,128)S(1)} %get-tuple-element.53.left_ref, f32[16,128]{1,0:T(8,128)S(1)} %get-tuple-element.54.own_ref, f32[128,256]{1,0:T(8,128)S(1)} %get-tuple-element.55.right_ref, ...), custom_call_target="tpu_custom_call" | custom-call | tf_op jit(solution)/shard_map/last/pallas_call | solution.py:608
  (8 shorter events, 0.0 us)
Async XLA Ops:
  1.0 1.5 %collective-permute-start = (f32[256,128]{1,0:T(8,128)S(1)}, f32[256,128]{1,0:T(8,128)S(1)}, u32[]{:S(2)}, u32[]{:S(2)}) collective-permute-start(f32[256,128]{1,0:T(8,128)S(1)} %get-tuple-element.34), channel_id=1, source_target_pairs={{0,1},{1,0},{2,3},{3,2},{4,5},{5,4},{6,7},{7,6},{8,9},{9,8},{10,11... | collective-permute-start | bytes 393224 | tf_op jit(solution)/shard_map/ppermute | solution.py:472
  2.6 9.6 %collective-permute-start.2 = (f32[18,8,128]{2,1,0:T(8,128)S(1)}, f32[18,8,128]{2,1,0:T(8,128)S(1)}, u32[]{:S(2)}, u32[]{:S(2)}) collective-permute-start(f32[18,8,128]{2,1,0:T(8,128)S(1)} %get-tuple-element.65), channel_id=1, source_target_pairs={{0,1},{1,0},{2,4},{3,5},{4,2},{5,3},{6,8},{7,9},{8,6},{9,7},{10,12... | collective-permute-start | bytes 221192 | tf_op jit(solution)/shard_map/ppermute | solution.py:472
  3.0 9.2 %collective-permute-start.1 = (f32[18,8,128]{2,1,0:T(8,128)S(1)}, f32[18,8,128]{2,1,0:T(8,128)S(1)}, u32[]{:S(2)}, u32[]{:S(2)}) collective-permute-start(f32[18,8,128]{2,1,0:T(8,128)S(1)} %get-tuple-element.66), channel_id=1, source_target_pairs={{0,2},{1,3},{2,0},{3,1},{4,6},{5,7},{6,4},{7,5},{8,10},{9,11},{10,... | collective-permute-start | bytes 221192 | tf_op jit(solution)/shard_map/ppermute | solution.py:472
  13.0 3.1 %collective-permute-start.3 = (f32[8,128]{1,0:T(8,128)S(1)}, f32[8,128]{1,0:T(8,128)S(1)}, u32[]{:S(2)}, u32[]{:S(2)}) collective-permute-start(f32[8,128]{1,0:T(8,128)S(1)} %get-tuple-element.43), channel_id=1, source_target_pairs={{0,3},{1,2},{2,1},{3,0},{4,7},{5,6},{6,5},{7,4},{8,11},{9,10},{10,... | collective-permute-start | bytes 12296 | tf_op jit(solution)/shard_map/ppermute | solution.py:472
  16.1 3.1 %collective-permute-start.4 = (f32[16,128]{1,0:T(8,128)S(1)}, f32[16,128]{1,0:T(8,128)S(1)}, u32[]{:S(2)}, u32[]{:S(2)}) collective-permute-start(f32[16,128]{1,0:T(8,128)S(1)} %get-tuple-element.69.after_ref), channel_id=1, source_target_pairs={{0,5},{1,4},{2,7},{3,6},{4,1},{5,0},{6,3},{7,2},{8,13},{9,12},{10,... | collective-permute-start | bytes 24584 | tf_op jit(solution)/shard_map/ppermute | solution.py:472
  19.2 4.1 %collective-permute-start.5 = (f32[32,128]{1,0:T(8,128)S(1)}, f32[32,128]{1,0:T(8,128)S(1)}, u32[]{:S(2)}, u32[]{:S(2)}) collective-permute-start(f32[32,128]{1,0:T(8,128)S(1)} %get-tuple-element.63.after_ref), channel_id=1, source_target_pairs={{0,9},{1,8},{2,11},{3,10},{4,13},{5,12},{6,15},{7,14},{8,1},{9,0},... | collective-permute-start | bytes 49160 | tf_op jit(solution)/shard_map/ppermute | solution.py:472
  23.3 1.2 %collective-permute-start.6 = (f32[64,128]{1,0:T(8,128)S(1)}, f32[64,128]{1,0:T(8,128)S(1)}, u32[]{:S(2)}, u32[]{:S(2)}) collective-permute-start(f32[64,128]{1,0:T(8,128)S(1)} %pad_maximum_fusion.4), channel_id=1, source_target_pairs={{0,1},{1,0},{2,3},{3,2},{4,5},{5,4},{6,7},{7,6},{8,9},{9,8},{10,11... | collective-permute-start | bytes 98312 | tf_op jit(solution)/shard_map/ppermute | solution.py:472

commit v4 on v3

--- a/solution.py
+++ b/solution.py
@@ -100,23 +100,14 @@
     return acc
 
 
-def fold(parts, pick):
-    row = iota((8, LANES), 0)
-    step = 4
-    while step:
-        keep = row % (2 * step) < step
-        half = len(parts) // 2
-        parts = [
-            jnp.where(keep, a + pltpu.roll(a, 8 - step, 0), b + pltpu.roll(b, step, 0))
-            for a, b in zip(parts[:half], parts[half:])
-        ]
-        step //= 2
-    x = parts[0]
-    step = BS // 2
-    while step:
-        x = x + pltpu.roll(x, LANES - step, 1)
-        step //= 2
-    return jnp.take_along_axis(x, pick, axis=1)
+def eights(x):
+    return sum((x[b : b + 8] for b in range(8, x.shape[0], 8)), x[:8])
+
+
+def sublane_sums(x):
+    half = x.shape[0] // 2
+    x = x[:half] + x[half:]
+    return x.reshape(half // 8, 8, LANES).sum(axis=1)
 
 
 def chunks(start, stop, size=64):
@@ -142,7 +133,7 @@
         second_ref[t] = strips[1, :, t * LANES : (t + 1) * LANES].astype(F32)
 
 
-def load_kernel(cov_ref, fog_rows_ref, fog_cols_ref, side_ref, cover_ref, window, sums_ref, band_ref, left_ref, own_ref, right_ref, loaded, cells_of, fog_r, fog_c, sems):
+def load_kernel(cov_ref, fog_rows_ref, fog_cols_ref, side_ref, cover_ref, window, parts_ref, band_ref, fold_ref, left_ref, own_ref, right_ref, loaded, fog_r, fog_c, sems):
     rows, cols = cov_ref.shape
     tiles = cols // LANES
     pieces = sems.shape[0] - 2
@@ -162,12 +153,14 @@
         copy.start()
     tap = tap_of(jnp.abs(iota((2 * LANES, LANES), 0) - HALF - iota((2 * LANES, LANES), 1)))
     band_ref[:, :LANES], band_ref[:, LANES:] = halves(tap)
+    for t in range(tiles):
+        group = (iota((LANES, LANES), 0) + t * LANES) // BS
+        fold_ref[t * LANES : (t + 1) * LANES, :] = (group == iota((LANES, LANES), 1)).astype(F32).astype(BF16)
     for copy in fogs:
         copy.wait()
     place = lax.axis_index("row") * (rows // BS)
     prep(place, fog_r[...], fog_c[...], left_ref, own_ref, right_ref)
     lane = iota((1, LANES), 1)
-    per = LANES // BS
     touches = (lane < HALF) == (lax.axis_index("col") == 0)
 
     def put(t, at, value):
@@ -189,25 +182,16 @@
             here = pltpu.roll(value, HALF, 1)
             put(t, at, jnp.where(lane < HALF, before, here).astype(BF16))
             before = here
-            for i in range(part // BS):
-                cell = value[i * BS : (i + 1) * BS]
-                cells_of[t, p * (part // BS) + i] = sum(cell[b : b + 8] for b in range(8, BS, 8)) + cell[:8]
+            some = jnp.concatenate([eights(value[i : i + BS]) for i in range(0, part, BS)], axis=0)
+            span = slice(t * LANES, (t + 1) * LANES)
+            for half, rest in zip(range(2), halves(some)):
+                low = half * (rows // 4) + p * (part // 4)
+                parts_ref[low : low + part // 4, span] = rest
         put(tiles, at, jnp.where(lane < HALF, before, side).astype(BF16))
-    spot = iota((8, LANES), 1)
-    sums = jnp.zeros((8, LANES), F32)
-    for t in range(tiles):
-        cell = fold([cells_of[t, i] for i in range(rows // BS)], (spot % per) * BS)
-        sums = jnp.where(spot // per == t, cell, sums)
-    sums_ref[...] = sums
-
-
-def inner_kernel(window, band_ref, c_ref, cover_in, fine_ref, across, sums_ref):
+
+def inner_kernel(window, band_ref, fold_ref, c_ref, cover_in, fine_ref, across, sums_ref, f_parts):
     tiles = cover_in.shape[0] - 1
     rows = window.shape[1]
-    cells = rows // BS
-    per = LANES // BS
-    spot = iota((cells, LANES), 1)
-    pick = (spot % per) * BS
 
     def columns(t, count):
         part = window[t : t + count].reshape(count * rows, 2 * LANES)
@@ -223,13 +207,14 @@
             base = PAD + EDGE + low
             fine = row_blur(lambda k: across[t, base + k : base + k + high - low, :])
             fine_ref[t, EDGE + low : EDGE + high, :] = fine
-            energy = cover_in[t, EDGE + low : EDGE + high, :] * fine
-            parts.append(sum(energy[b : b + 8] for b in range(8, high - low, 8)) + energy[:8])
+            parts.append(eights(cover_in[t, EDGE + low : EDGE + high, :] * fine))
         if t < tiles:
-            f = fold(parts, pick)
-            sums_ref[...] = jnp.where(spot // per == t + tiles, f, sums_ref[...])
-
-    sums_ref[...] = c_ref[...]
+            span = slice(t * LANES, (t + 1) * LANES)
+            for i in range(0, len(parts), 2):
+                upper, lower = halves(jnp.concatenate(parts[i : i + 2], axis=0))
+                f_parts[8 * i : 8 * i + 16, span] = upper
+                f_parts[rows // 4 + 8 * i : rows // 4 + 8 * i + 16, span] = lower
+
     groups = chunks(0, tiles + 1, 2)
     columns(*groups[0])
     for g, (start, count) in enumerate(groups):
@@ -237,18 +222,18 @@
             columns(*groups[g + 1])
         for t in range(start, start + count):
             down(t)
-
-
-def outer_kernel(first_ref, second_ref, band_ref, across_ref, part_ref, cover_in, fine_in, cover_ref, fine_ref, sums_ref, across, window):
+    c = sublane_sums(jnp.dot(c_ref[...], fold_ref[...], preferred_element_type=F32))
+    f = sublane_sums(jnp.dot(f_parts[...], fold_ref[...], preferred_element_type=F32))
+    sums_ref[...] = c + pltpu.roll(f, HALF, 1)
+
+
+def outer_kernel(first_ref, second_ref, band_ref, fold_ref, across_ref, part_ref, cover_in, fine_in, cover_ref, fine_ref, sums_ref, across, window, f_parts):
     tiles = cover_ref.shape[0] - 1
     ext = cover_ref.shape[1]
     rows = ext - 2 * EDGE
     even = lax.rem(lax.axis_index("row"), 2) == 0
     lane = iota((1, LANES), 1)
     cells = rows // BS
-    per = LANES // BS
-    spot = iota((cells, LANES), 1)
-    pick = (spot % per) * BS
     both = 2 * EDGE
     touches = (lane < HALF) == (lax.axis_index("col") == 0)
     place = lax.axis_index("row")
@@ -280,7 +265,6 @@
     twice = jnp.dot(window[...], band_ref[...], preferred_element_type=F32)
     once = twice[:, :LANES] + twice[:, LANES:]
     reach = 2 * PAD + 2 * EDGE
-    total = jnp.zeros((cells, LANES), F32)
     for t in range(tiles + 1):
         across[t, 0:PAD, :] = jnp.zeros((PAD, LANES), F32)
         across[t, PAD : PAD + EDGE, :] = once[t * both : t * both + EDGE]
@@ -295,11 +279,14 @@
         fine_ref[t, 0 : EDGE + 8, :] = top
         fine_ref[t, EDGE + rows - 8 :, :] = bot
         if t < tiles:
-            zero = jnp.zeros((8, LANES), F32)
             a = top[EDGE:] * cover_ref[t, EDGE : EDGE + 8, :]
             b = bot[:8] * cover_ref[t, EDGE + rows - 8 : EDGE + rows, :]
-            total = jnp.where(spot // per == t + tiles, fold([a] + [zero] * (cells - 2) + [b], pick), total)
-    sums_ref[...] = part_ref[...] + total
+            span = slice(t * LANES, (t + 1) * LANES)
+            f_parts[:16, span], f_parts[16:, span] = halves(jnp.concatenate([a, b], axis=0))
+    f = sublane_sums(jnp.dot(f_parts[...], fold_ref[...], preferred_element_type=F32))
+    row = iota((cells, LANES), 0)
+    total = jnp.where(row == 0, f[0:1], jnp.where(row == cells - 1, f[1:2], 0.0))
+    sums_ref[...] = part_ref[...] + pltpu.roll(total, HALF, 1)
 
 
 def spread_kernel(cover_ref, after_ref, blurred_ref, above_ref, below_ref):
@@ -430,7 +417,7 @@
         copy(g).start()
 
     def stage(body):
-        pl.when(row >= 0)(body)
+        body()
 
     def start():
         charge(tiles)
@@ -513,13 +500,14 @@
         jnp.concatenate([second_rows] + corners, axis=0),
         lambda r, c: (r, 1 - c) if r in (0, row_count - 1) else ((r + 1, c) if r % 2 else (r - 1, c)),
     )
-    cover, window, c_sums, band, left, own, right = call(
+    cover, window, c_parts, band, fold, left, own, right = call(
         load_kernel,
         (
             wide,
             shape(tiles + 1, rows, 2 * LANES, dtype=BF16),
-            shape(back_rows, LANES),
+            shape(rows // 2, cols, dtype=BF16),
             shape(2 * LANES, 2 * LANES, dtype=BF16),
+            shape(cols, LANES, dtype=BF16),
             shape(n_rows, 2 * n_rows),
             shape(16, 2 * n_rows),
             shape(n_cols, 2 * n_cols),
@@ -529,7 +517,6 @@
         side,
         scratch=[
             pltpu.VMEM((rows, cols), jnp.int32),
-            pltpu.VMEM((tiles, back_rows, 8, LANES), F32),
             pltpu.VMEM(fog_rows.shape, F32),
             pltpu.VMEM(fog_cols.shape, F32),
             pltpu.SemaphoreType.DMA((4 + 2,)),
@@ -540,21 +527,24 @@
     fine, across, part = call(
         inner_kernel,
         (wide, shape(tiles + 1, ext + 2 * PAD, LANES), shape(back_rows, LANES)),
-        [VMEM] * 4,
+        [VMEM] * 5,
         window,
         band,
-        c_sums,
+        fold,
+        c_parts,
         cover,
+        scratch=[pltpu.VMEM((rows // 2, cols), BF16)],
         mib=8,
         name="inner",
     )
     cover, fine, sums = call(
         outer_kernel,
         (wide, wide, shape(back_rows, LANES)),
-        [VMEM] * 7,
+        [VMEM] * 8,
         first,
         second,
         band,
+        fold,
         across,
         part,
         cover,
@@ -562,8 +552,9 @@
         scratch=[
             pltpu.VMEM((tiles + 1, 4 * PAD + 4 * EDGE, LANES), F32),
             pltpu.VMEM(((tiles + 1) * 2 * EDGE, 2 * LANES), BF16),
+            pltpu.VMEM((32, cols), BF16),
         ],
-        aliases={5: 0, 6: 1},
+        aliases={6: 0, 7: 1},
         mib=8,
         name="outer",
     )

time: 28.2 us -> 27.9 us (0.989)
  Pallas kernels: 13.4 us -> 13.1 us
where the time goes in v4:
time: 27.9 us; the launch traced here: 27.7 us
  Pallas kernels  13.1 us (47%)
  starting transfers between devices  7.78 us (28%)
  waiting for transfers between devices  6.73 us (24%)
    pallas_call x6, Pallas kernels, call(): pl.pallas_call(kernel, out_shape=outs, in_specs=ins, out_specs=(VMEM,) *...  9.77 us
    ppermute x7, starting transfers between devices, move(): lax.ppermute(value, ('row', 'col'), [(i, r * col_count + c) for i, (r, c)...  7.78 us
    ppermute x7, waiting for transfers between devices, move(): lax.ppermute(value, ('row', 'col'), [(i, r * col_count + c) for i, (r, c)...  6.73 us
    pallas_call x1, Pallas kernels, shards(): pl.pallas_call(last_kernel, out_shape=shape(rows, cols), in_specs=[VMEM]...  3.32 us
  transfers between devices with their start and end apart: 7, of which 5 were waited for; matrix products, arithmetic and copies ran while one was open for 0% of the time, Pallas kernels for 29%

profile of v4, /device:TPU:0, one launch (start us, length us, event | category | flops | bytes accessed | tf_op | source)
XLA Modules:
  0.0 27.7 jit_solution(10557514422300028632)
XLA Ops:
  0.0 1.0 %edges.1 = (f32[256,128]{1,0:T(8,128)S(1)}, f32[16,8,128]{2,1,0:T(8,128)S(1)}, f32[16,8,128]{2,1,0:T(8,128)S(1)}) custom-call(s32[256,2048]{1,0:T(8,128)} %cov_ref.3), custom_call_target="tpu_custom_call" | custom-call | flops 524288 | bytes 524288 | tf_op jit(solution)/shard_map/edges/pallas_call | solution.py:465
  1.0 0.6 %collective-permute-start = (f32[256,128]{1,0:T(8,128)S(1)}, f32[256,128]{1,0:T(8,128)S(1)}, u32[]{:S(2)}, u32[]{:S(2)}) collective-permute-start(f32[256,128]{1,0:T(8,128)S(1)} %get-tuple-element.35), channel_id=1, source_target_pairs={{0,1},{1,0},{2,3},{3,2},{4,5},{5,4},{6,7},{7,6},{8,9},{9,8},{10,11... | collective-permute-start | bytes 393224 | tf_op jit(solution)/shard_map/ppermute | solution.py:459
  1.5 1.0 %collective-permute-done.side_ref = f32[256,128]{1,0:T(8,128)S(1)} collective-permute-done((f32[256,128]{1,0:T(8,128)S(1)}, f32[256,128]{1,0:T(8,128)S(1)}, u32[]{:S(2)}, u32[]{:S(2)}) %collective-permute-start) | collective-permute-done | bytes 131104 | tf_op jit(solution)/shard_map/ppermute | solution.py:459
  2.6 0.4 %collective-permute-start.2 = (f32[18,8,128]{2,1,0:T(8,128)S(1)}, f32[18,8,128]{2,1,0:T(8,128)S(1)}, u32[]{:S(2)}, u32[]{:S(2)}) collective-permute-start(f32[18,8,128]{2,1,0:T(8,128)S(1)} %get-tuple-element.67), channel_id=1, source_target_pairs={{0,1},{1,0},{2,4},{3,5},{4,2},{5,3},{6,8},{7,9},{8,6},{9,7},{10,12... | collective-permute-start | bytes 221192 | tf_op jit(solution)/shard_map/ppermute | solution.py:459
  3.0 4.0 %collective-permute-start.1 = (f32[18,8,128]{2,1,0:T(8,128)S(1)}, f32[18,8,128]{2,1,0:T(8,128)S(1)}, u32[]{:S(2)}, u32[]{:S(2)}) collective-permute-start(f32[18,8,128]{2,1,0:T(8,128)S(1)} %get-tuple-element.68), channel_id=1, source_target_pairs={{0,2},{1,3},{2,0},{3,1},{4,6},{5,7},{6,4},{7,5},{8,10},{9,11},{10,... | collective-permute-start | bytes 221192 | tf_op jit(solution)/shard_map/ppermute | solution.py:459
  7.0 2.6 %load.1 = (f32[17,272,128]{2,1,0:T(8,128)S(1)}, bf16[17,256,256]{2,1,0:T(8,128)(2,1)S(1)}, bf16[128,2048]{1,0:T(8,128)(2,1)S(1)}, bf16[256,256]{1,0:T(8,128)(2,1...) custom-call(s32[256,2048]{1,0:T(8,128)} %cov_ref.3, ...), custom_call_target="tpu_custom_call" | custom-call | flops 524288 | bytes 524288 | tf_op jit(solution)/shard_map/load/pallas_call | solution.py:465
  9.6 2.7 %inner.1 = (f32[17,272,128]{2,1,0:T(8,128)S(1)}, f32[17,288,128]{2,1,0:T(8,128)S(1)}, f32[8,128]{1,0:T(8,128)S(1)}) custom-call(bf16[17,256,256]{2,1,0:T(8,128)(2,1)S(1)} %get-tuple-element.39.window, bf16[256,256]{1,0:T(8,128)(2,1)S(1)} %get-tuple-element.37.band_ref, bf16[2048,128]{1,0:T(8,128)(2,1)S(1)} %get-tuple-element.38.fold_ref, ...), custom_call_target="tpu_custom_call" | custom-call | flops 524288 | bytes 524288 | tf_op jit(solution)/shard_map/inner/pallas_call | solution.py:465
  12.3 0.0 collective-permute-done.2.second_ref
  12.3 0.0 collective-permute-done.1.first_ref
  12.3 0.7 %outer.1 = (f32[17,272,128]{2,1,0:T(8,128)S(1)}, f32[17,272,128]{2,1,0:T(8,128)S(1)}, f32[8,128]{1,0:T(8,128)S(1)}) custom-call(f32[18,8,128]{2,1,0:T(8,128)S(1)} %collective-permute-done.1.first_ref, f32[18,8,128]{2,1,0:T(8,128)S(1)} %collective-permute-done.2.second_ref, ...), custom_call_target="tpu_custom_call", output_to_operand_aliasing={{0}: (6, {}), {1}: (7, {})} | custom-call | flops 524288 | bytes 524288 | tf_op jit(solution)/shard_map/outer/pallas_call | solution.py:465
  13.0 0.0 collective-permute-start.3
  13.0 3.0 %collective-permute-done.3 = f32[8,128]{1,0:T(8,128)S(1)} collective-permute-done((f32[8,128]{1,0:T(8,128)S(1)}, f32[8,128]{1,0:T(8,128)S(1)}, u32[]{:S(2)}, u32[]{:S(2)}) %collective-permute-start.3) | collective-permute-done | bytes 4128 | tf_op jit(solution)/shard_map/ppermute | solution.py:459
  16.0 0.8 %collective-permute-start.4 = (f32[16,128]{1,0:T(8,128)S(1)}, f32[16,128]{1,0:T(8,128)S(1)}, u32[]{:S(2)}, u32[]{:S(2)}) collective-permute-start(f32[16,128]{1,0:T(8,128)S(1)} %get-tuple-element.71.after_ref), channel_id=1, source_target_pairs={{0,5},{1,4},{2,7},{3,6},{4,1},{5,0},{6,3},{7,2},{8,13},{9,12},{10,... | collective-permute-start | bytes 24584 | tf_op jit(solution)/shard_map/ppermute | solution.py:459
  16.8 1.4 %spread.1 = (f32[17,256,128]{2,1,0:T(8,128)S(1)}, f32[17,8,8,128]{3,2,1,0:T(8,128)S(1)}, f32[17,8,8,128]{3,2,1,0:T(8,128)S(1)}) custom-call(f32[17,272,128]{2,1,0:T(8,128)S(1)} %get-tuple-element.46.cover_ref, f32[16,128]{1,0:T(8,128)S(1)} %get-tuple-element.71.after_ref), custom_call_target="tpu_custom_call" | custom-call | flops 524288 | bytes 524288 | tf_op jit(solution)/shard_map/spread/pallas_call | solution.py:465
  18.1 0.9 %collective-permute-done.4 = f32[16,128]{1,0:T(8,128)S(1)} collective-permute-done((f32[16,128]{1,0:T(8,128)S(1)}, f32[16,128]{1,0:T(8,128)S(1)}, u32[]{:S(2)}, u32[]{:S(2)}) %collective-permute-start.4) | collective-permute-done | bytes 8224 | tf_op jit(solution)/shard_map/ppermute | solution.py:459
  19.1 1.8 %collective-permute-start.5 = (f32[32,128]{1,0:T(8,128)S(1)}, f32[32,128]{1,0:T(8,128)S(1)}, u32[]{:S(2)}, u32[]{:S(2)}) collective-permute-start(f32[32,128]{1,0:T(8,128)S(1)} %get-tuple-element.65.after_ref), channel_id=1, source_target_pairs={{0,9},{1,8},{2,11},{3,10},{4,13},{5,12},{6,15},{7,14},{8,1},{9,0},... | collective-permute-start | bytes 49160 | tf_op jit(solution)/shard_map/ppermute | solution.py:459
  20.9 1.5 %dose.1 = (f32[16,256,128]{2,1,0:T(8,128)S(1)}, f32[17,256,128]{2,1,0:T(8,128)S(1)}) custom-call(f32[17,272,128]{2,1,0:T(8,128)S(1)} %get-tuple-element.46.cover_ref, f32[17,272,128]{2,1,0:T(8,128)S(1)} %get-tuple-element.51.fine_ref, f32[32,128]{1,0:T(8,128)S(1)} %get-tuple-element.65.after_ref), custom_call_target="tpu_custom_call" | custom-call | flops 524288 | bytes 524288 | tf_op jit(solution)/shard_map/dose/pallas_call | solution.py:465
  22.4 0.8 %collective-permute-done.5 = f32[32,128]{1,0:T(8,128)S(1)} collective-permute-done((f32[32,128]{1,0:T(8,128)S(1)}, f32[32,128]{1,0:T(8,128)S(1)}, u32[]{:S(2)}, u32[]{:S(2)}) %collective-permute-start.5) | collective-permute-done | bytes 16416 | tf_op jit(solution)/shard_map/ppermute | solution.py:459
  23.2 0.2 collective-permute-start.6
  23.4 1.0 %collective-permute-done.6 = f32[64,128]{1,0:T(8,128)S(1)} collective-permute-done((f32[64,128]{1,0:T(8,128)S(1)}, f32[64,128]{1,0:T(8,128)S(1)}, u32[]{:S(2)}, u32[]{:S(2)}) %collective-permute-start.6) | collective-permute-done | bytes 32800 | tf_op jit(solution)/shard_map/ppermute | solution.py:459
  24.4 3.3 %last.1 = f32[256,2048]{1,0:T(8,128)} custom-call(f32[128,128]{1,0:T(8,128)S(1)} %constant_dynamic-update-slice_fusion.5.gathered_ref, f32[64,128]{1,0:T(8,128)S(1)} %get-tuple-element.55.left_ref, f32[16,128]{1,0:T(8,128)S(1)} %get-tuple-element.56.own_ref, f32[128,256]{1,0:T(8,128)S(1)} %get-tuple-element.57.right_ref, ...), custom_call_target="tpu_custom_call" | custom-call | tf_op jit(solution)/shard_map/last/pallas_call | solution.py:599
  (8 shorter events, 0.0 us)
Async XLA Ops:
  1.0 1.5 %collective-permute-start = (f32[256,128]{1,0:T(8,128)S(1)}, f32[256,128]{1,0:T(8,128)S(1)}, u32[]{:S(2)}, u32[]{:S(2)}) collective-permute-start(f32[256,128]{1,0:T(8,128)S(1)} %get-tuple-element.35), channel_id=1, source_target_pairs={{0,1},{1,0},{2,3},{3,2},{4,5},{5,4},{6,7},{7,6},{8,9},{9,8},{10,11... | collective-permute-start | bytes 393224 | tf_op jit(solution)/shard_map/ppermute | solution.py:459
  2.6 9.7 %collective-permute-start.2 = (f32[18,8,128]{2,1,0:T(8,128)S(1)}, f32[18,8,128]{2,1,0:T(8,128)S(1)}, u32[]{:S(2)}, u32[]{:S(2)}) collective-permute-start(f32[18,8,128]{2,1,0:T(8,128)S(1)} %get-tuple-element.67), channel_id=1, source_target_pairs={{0,1},{1,0},{2,4},{3,5},{4,2},{5,3},{6,8},{7,9},{8,6},{9,7},{10,12... | collective-permute-start | bytes 221192 | tf_op jit(solution)/shard_map/ppermute | solution.py:459
  3.0 9.3 %collective-permute-start.1 = (f32[18,8,128]{2,1,0:T(8,128)S(1)}, f32[18,8,128]{2,1,0:T(8,128)S(1)}, u32[]{:S(2)}, u32[]{:S(2)}) collective-permute-start(f32[18,8,128]{2,1,0:T(8,128)S(1)} %get-tuple-element.68), channel_id=1, source_target_pairs={{0,2},{1,3},{2,0},{3,1},{4,6},{5,7},{6,4},{7,5},{8,10},{9,11},{10,... | collective-permute-start | bytes 221192 | tf_op jit(solution)/shard_map/ppermute | solution.py:459
  13.0 3.0 %collective-permute-start.3 = (f32[8,128]{1,0:T(8,128)S(1)}, f32[8,128]{1,0:T(8,128)S(1)}, u32[]{:S(2)}, u32[]{:S(2)}) collective-permute-start(f32[8,128]{1,0:T(8,128)S(1)} %get-tuple-element.45), channel_id=1, source_target_pairs={{0,3},{1,2},{2,1},{3,0},{4,7},{5,6},{6,5},{7,4},{8,11},{9,10},{10,... | collective-permute-start | bytes 12296 | tf_op jit(solution)/shard_map/ppermute | solution.py:459
  16.0 3.1 %collective-permute-start.4 = (f32[16,128]{1,0:T(8,128)S(1)}, f32[16,128]{1,0:T(8,128)S(1)}, u32[]{:S(2)}, u32[]{:S(2)}) collective-permute-start(f32[16,128]{1,0:T(8,128)S(1)} %get-tuple-element.71.after_ref), channel_id=1, source_target_pairs={{0,5},{1,4},{2,7},{3,6},{4,1},{5,0},{6,3},{7,2},{8,13},{9,12},{10,... | collective-permute-start | bytes 24584 | tf_op jit(solution)/shard_map/ppermute | solution.py:459
  19.1 4.1 %collective-permute-start.5 = (f32[32,128]{1,0:T(8,128)S(1)}, f32[32,128]{1,0:T(8,128)S(1)}, u32[]{:S(2)}, u32[]{:S(2)}) collective-permute-start(f32[32,128]{1,0:T(8,128)S(1)} %get-tuple-element.65.after_ref), channel_id=1, source_target_pairs={{0,9},{1,8},{2,11},{3,10},{4,13},{5,12},{6,15},{7,14},{8,1},{9,0},... | collective-permute-start | bytes 49160 | tf_op jit(solution)/shard_map/ppermute | solution.py:459
  23.2 1.2 %collective-permute-start.6 = (f32[64,128]{1,0:T(8,128)S(1)}, f32[64,128]{1,0:T(8,128)S(1)}, u32[]{:S(2)}, u32[]{:S(2)}) collective-permute-start(f32[64,128]{1,0:T(8,128)S(1)} %pad_maximum_fusion.4), channel_id=1, source_target_pairs={{0,1},{1,0},{2,3},{3,2},{4,5},{5,4},{6,7},{7,6},{8,9},{9,8},{10,11... | collective-permute-start | bytes 98312 | tf_op jit(solution)/shard_map/ppermute | solution.py:459

commit v5 on v4

--- a/solution.py
+++ b/solution.py
@@ -114,7 +114,7 @@
     return [(a, min(size, stop - a)) for a in range(start, stop, size)]
 
 
-def edges_kernel(cov_ref, edge_ref, first_ref, second_ref, tile, strips, sems):
+def edges_kernel(cov_ref, fog_rows_ref, fog_cols_ref, edge_ref, first_ref, second_ref, fog_r, fog_c, tile, strips, sems):
     rows, cols = cov_ref.shape
     tiles = cols // LANES
     odd = lax.rem(lax.axis_index("row"), 2)
@@ -123,108 +123,99 @@
     for i, start in enumerate((1 - odd, odd)):
         span = pl.ds(pl.multiple_of(start * (rows - EDGE), EDGE), EDGE)
         copies.append(pltpu.make_async_copy(cov_ref.at[span], strips.at[i], sems.at[1 + i]))
+    copies.append(pltpu.make_async_copy(fog_rows_ref, fog_r, sems.at[3]))
+    copies.append(pltpu.make_async_copy(fog_cols_ref, fog_c, sems.at[4]))
     for copy in copies:
         copy.start()
     for copy in copies:
         copy.wait()
-    edge_ref[...] = tile[...].astype(F32)
+    edge_ref[:rows, :] = tile[...].astype(F32)
+    for i, start in enumerate((1 - odd, odd)):
+        span = pl.ds(pl.multiple_of(start * (rows - EDGE), EDGE), EDGE)
+        edge_ref[rows + i * EDGE : rows + (i + 1) * EDGE, :] = tile[span, :].astype(F32)
     for t in range(tiles):
         first_ref[t] = strips[0, :, t * LANES : (t + 1) * LANES].astype(F32)
         second_ref[t] = strips[1, :, t * LANES : (t + 1) * LANES].astype(F32)
 
 
-def load_kernel(cov_ref, fog_rows_ref, fog_cols_ref, side_ref, cover_ref, window, parts_ref, band_ref, fold_ref, left_ref, own_ref, right_ref, loaded, fog_r, fog_c, sems):
+def prep_kernel(fog_rows_ref, fog_cols_ref, band_ref, fold_ref, left_ref, own_ref, right_ref):
+    tap = tap_of(jnp.abs(iota((2 * LANES, LANES), 0) - HALF - iota((2 * LANES, LANES), 1)))
+    band_ref[:, :LANES], band_ref[:, LANES:] = halves(tap)
+    for t in range(0, fold_ref.shape[0], LANES):
+        group = (iota((LANES, LANES), 0) + t) // BS
+        fold_ref[t : t + LANES, :] = (group == iota((LANES, LANES), 1)).astype(F32).astype(BF16)
+    place = lax.axis_index("row") * (left_ref.shape[0] // lax.axis_size("row"))
+    prep(place, fog_rows_ref[...], fog_cols_ref[...], left_ref, own_ref, right_ref)
+
+
+def block_kernel(cov_ref, side_ref, band_ref, fold_ref, cover_ref, fine_ref, across, sums_ref, window, parts):
     rows, cols = cov_ref.shape
     tiles = cols // LANES
-    pieces = sems.shape[0] - 2
-    part = rows // pieces
-    copies = [
-        pltpu.make_async_copy(
-            cov_ref.at[p * part : (p + 1) * part], loaded.at[p * part : (p + 1) * part], sems.at[p]
-        )
-        for p in range(pieces)
-    ]
-    fogs = [
-        pltpu.make_async_copy(fog_rows_ref, fog_r, sems.at[pieces]),
-        pltpu.make_async_copy(fog_cols_ref, fog_c, sems.at[pieces + 1]),
-    ]
-    ahead = 3
-    for copy in fogs + copies[:ahead]:
-        copy.start()
-    tap = tap_of(jnp.abs(iota((2 * LANES, LANES), 0) - HALF - iota((2 * LANES, LANES), 1)))
-    band_ref[:, :LANES], band_ref[:, LANES:] = halves(tap)
-    for t in range(tiles):
-        group = (iota((LANES, LANES), 0) + t * LANES) // BS
-        fold_ref[t * LANES : (t + 1) * LANES, :] = (group == iota((LANES, LANES), 1)).astype(F32).astype(BF16)
-    for copy in fogs:
-        copy.wait()
-    place = lax.axis_index("row") * (rows // BS)
-    prep(place, fog_r[...], fog_c[...], left_ref, own_ref, right_ref)
+    part = 2 * BS
+    pieces = rows // part
+    cells = rows // BS
     lane = iota((1, LANES), 1)
     touches = (lane < HALF) == (lax.axis_index("col") == 0)
-
-    def put(t, at, value):
-        window[t, at, :LANES] = value
-        window[(t - 1) % (tiles + 1), at, LANES:] = value
-
-    for p, copy in enumerate(copies):
-        copy.wait()
-        if p + ahead < pieces:
-            copies[p + ahead].start()
-        at = slice(p * part, (p + 1) * part)
-        side = jnp.where(touches, side_ref[at, :], 0.0)
-        cover_ref[tiles, EDGE + p * part : EDGE + (p + 1) * part, :] = side
+    c_rows, f_rows = 8 * cells, 8 * (cells + 2)
+
+    def keep(base, height, low, span, values):
+        for half, value in zip(range(2), halves(jnp.concatenate(values, axis=0))):
+            at = base + half * height + low
+            parts[at : at + 8 * len(values), span] = value
+
+    for p in range(pieces):
+        first = p * part
+        at = slice(EDGE + first, EDGE + first + part)
+
+        def put(t, value):
+            window[t, :, :LANES] = value
+            window[(t - 1) % (tiles + 1), :, LANES:] = value
+
+        side = jnp.where(touches, side_ref[first : first + part, :], 0.0)
+        cover_ref[tiles, at, :] = side
         side = pltpu.roll(side, HALF, 1)
         before = side
         for t in range(tiles):
-            value = loaded[at, t * LANES : (t + 1) * LANES].astype(F32)
-            cover_ref[t, EDGE + p * part : EDGE + (p + 1) * part, :] = value
+            span = slice(t * LANES, (t + 1) * LANES)
+            value = cov_ref[first : first + part, span].astype(F32)
+            cover_ref[t, at, :] = value
             here = pltpu.roll(value, HALF, 1)
-            put(t, at, jnp.where(lane < HALF, before, here).astype(BF16))
+            put(t, jnp.where(lane < HALF, before, here).astype(BF16))
             before = here
-            some = jnp.concatenate([eights(value[i : i + BS]) for i in range(0, part, BS)], axis=0)
-            span = slice(t * LANES, (t + 1) * LANES)
-            for half, rest in zip(range(2), halves(some)):
-                low = half * (rows // 4) + p * (part // 4)
-                parts_ref[low : low + part // 4, span] = rest
-        put(tiles, at, jnp.where(lane < HALF, before, side).astype(BF16))
-
-def inner_kernel(window, band_ref, fold_ref, c_ref, cover_in, fine_ref, across, sums_ref, f_parts):
-    tiles = cover_in.shape[0] - 1
-    rows = window.shape[1]
-
-    def columns(t, count):
-        part = window[t : t + count].reshape(count * rows, 2 * LANES)
-        both = jnp.dot(part, band_ref[...], preferred_element_type=F32)
-        for i in range(count):
-            mine = both[i * rows : (i + 1) * rows]
-            across[t + i, PAD + EDGE : PAD + EDGE + rows, :] = mine[:, :LANES] + mine[:, LANES:]
-
-    def down(t):
-        parts = []
-        for a, n in chunks(0, rows, BS):
-            low, high = max(a, 8), min(a + n, rows - 8)
-            base = PAD + EDGE + low
-            fine = row_blur(lambda k: across[t, base + k : base + k + high - low, :])
-            fine_ref[t, EDGE + low : EDGE + high, :] = fine
-            parts.append(eights(cover_in[t, EDGE + low : EDGE + high, :] * fine))
-        if t < tiles:
-            span = slice(t * LANES, (t + 1) * LANES)
-            for i in range(0, len(parts), 2):
-                upper, lower = halves(jnp.concatenate(parts[i : i + 2], axis=0))
-                f_parts[8 * i : 8 * i + 16, span] = upper
-                f_parts[rows // 4 + 8 * i : rows // 4 + 8 * i + 16, span] = lower
-
-    groups = chunks(0, tiles + 1, 2)
-    columns(*groups[0])
-    for g, (start, count) in enumerate(groups):
-        if g + 1 < len(groups):
-            columns(*groups[g + 1])
-        for t in range(start, start + count):
-            down(t)
-    c = sublane_sums(jnp.dot(c_ref[...], fold_ref[...], preferred_element_type=F32))
-    f = sublane_sums(jnp.dot(f_parts[...], fold_ref[...], preferred_element_type=F32))
-    sums_ref[...] = c + pltpu.roll(f, HALF, 1)
+            keep(0, c_rows, 8 * (first // BS), span, [eights(value[i : i + BS]) for i in range(0, part, BS)])
+        put(tiles, jnp.where(lane < HALF, before, side).astype(BF16))
+        for t, count in chunks(0, tiles + 1, 6):
+            some = window[t : t + count].reshape(count * part, 2 * LANES)
+            both = jnp.dot(some, band_ref[...], preferred_element_type=F32)
+            for i in range(count):
+                mine = both[i * part : (i + 1) * part]
+                across[t + i, PAD + EDGE + first : PAD + EDGE + first + part, :] = mine[:, :LANES] + mine[:, LANES:]
+        ready = range(max(2 * p - 1, 0), 2 * p + 1 if p + 1 < pieces else cells)
+        for t in range(tiles + 1):
+            got = {}
+            for i in ready:
+                low, high = max(i * BS, 8), min((i + 1) * BS, rows - 8)
+                base = PAD + EDGE + low
+                fine = row_blur(lambda k: across[t, base + k : base + k + high - low, :])
+                fine_ref[t, EDGE + low : EDGE + high, :] = fine
+                if t < tiles:
+                    got[i] = eights(cover_ref[t, EDGE + low : EDGE + high, :] * fine)
+            if t < tiles:
+                span = slice(t * LANES, (t + 1) * LANES)
+                zero = jnp.zeros((8, LANES), F32)
+                for i in got:
+                    if i % 2 or i == 0:
+                        pair = [got[i], got.get(i + 1, zero)] if i else [got[0], zero]
+                        keep(2 * c_rows, f_rows, 8 * (i + 1) if i else 0, span, pair)
+    def folded(some, step):
+        return sum(
+            jnp.dot(parts[some, a : a + step], fold_ref[a : a + step, :], preferred_element_type=F32)
+            for a in range(0, cols, step)
+        )
+
+    c = sublane_sums(folded(slice(0, 2 * c_rows), cols))
+    f = sublane_sums(folded(slice(2 * c_rows, 2 * c_rows + 2 * f_rows), 4 * LANES))
+    sums_ref[...] = c + pltpu.roll(jnp.concatenate([f[:1], f[2 : cells + 1]], axis=0), HALF, 1)
 
 
 def outer_kernel(first_ref, second_ref, band_ref, fold_ref, across_ref, part_ref, cover_in, fine_in, cover_ref, fine_ref, sums_ref, across, window, f_parts):
@@ -240,11 +231,8 @@
     alone = (place == 0) | (place == lax.axis_size("row") - 1)
 
     def halo(t):
-        if t < tiles:
-            a, b = first_ref[t], second_ref[t]
-        else:
-            a = jnp.where(even, first_ref[t], first_ref[t + 1])
-            b = jnp.where(even, second_ref[t + 1], second_ref[t])
+        a, b = first_ref[t], second_ref[t]
+        if t == tiles:
             a, b = jnp.where(touches, a, 0.0), jnp.where(touches, b, 0.0)
         b = jnp.where(alone, 0.0, b)
         top = jnp.where(even, b, a)
@@ -477,65 +465,69 @@
     wide = shape(tiles + 1, ext, LANES)
     own_tiles = shape(tiles + 1, rows, LANES)
     hbm = pl.BlockSpec(memory_space=pltpu.HBM)
-    in_hbm = [pltpu.with_memory_space_constraint(x, pltpu.HBM) for x in (coverage, fog_rows, fog_cols)]
-    edge, first_rows, second_rows = call(
+    edge, first_rows, second_rows, fog_r, fog_c = call(
         edges_kernel,
-        (shape(rows, LANES), shape(tiles, EDGE, LANES), shape(tiles, EDGE, LANES)),
-        [hbm],
-        in_hbm[0],
+        (
+            shape(ext, LANES),
+            shape(tiles, EDGE, LANES),
+            shape(tiles, EDGE, LANES),
+            shape(*fog_rows.shape),
+            shape(*fog_cols.shape),
+        ),
+        [hbm] * 3,
+        *[pltpu.with_memory_space_constraint(x, pltpu.HBM) for x in (coverage, fog_rows, fog_cols)],
         scratch=[
             pltpu.VMEM((rows, LANES), jnp.int32),
             pltpu.VMEM((2, EDGE, cols), jnp.int32),
-            pltpu.SemaphoreType.DMA((3,)),
+            pltpu.SemaphoreType.DMA((5,)),
         ],
         mib=2,
         name="edges",
     )
 
     side = move(edge, lambda r, c: (r, 1 - c))
-    corners = [side[None, :EDGE], side[None, rows - EDGE :]]
-
-    first = move(jnp.concatenate([first_rows] + corners, axis=0), lambda r, c: (r ^ 1, c))
-    second = move(
-        jnp.concatenate([second_rows] + corners, axis=0),
-        lambda r, c: (r, 1 - c) if r in (0, row_count - 1) else ((r + 1, c) if r % 2 else (r - 1, c)),
-    )
-    cover, window, c_parts, band, fold, left, own, right = call(
-        load_kernel,
+    band, fold, left, own, right = call(
+        prep_kernel,
         (
-            wide,
-            shape(tiles + 1, rows, 2 * LANES, dtype=BF16),
-            shape(rows // 2, cols, dtype=BF16),
             shape(2 * LANES, 2 * LANES, dtype=BF16),
             shape(cols, LANES, dtype=BF16),
             shape(n_rows, 2 * n_rows),
             shape(16, 2 * n_rows),
             shape(n_cols, 2 * n_cols),
         ),
-        [hbm] * 3 + [VMEM],
-        *in_hbm,
+        [VMEM] * 2,
+        fog_r,
+        fog_c,
+        mib=4,
+        name="prep",
+    )
+    side, band = lax.optimization_barrier((side, band))
+    corners = side[rows:].reshape(2, EDGE, LANES)
+
+    first = move(jnp.concatenate([first_rows, corners[:1]], axis=0), lambda r, c: (r ^ 1, c))
+    second = move(
+        jnp.concatenate([second_rows, corners[1:]], axis=0),
+        lambda r, c: (r, 1 - c) if r in (0, row_count - 1) else ((r + 1, c) if r % 2 else (r - 1, c)),
+    )
+    cover, fine, across, part = call(
+        block_kernel,
+        (
+            wide,
+            wide,
+            shape(tiles + 1, ext + 2 * PAD, LANES),
+            shape(back_rows, LANES),
+        ),
+        [VMEM] * 4,
+        coverage,
         side,
+        band,
+        fold,
         scratch=[
-            pltpu.VMEM((rows, cols), jnp.int32),
-            pltpu.VMEM(fog_rows.shape, F32),
-            pltpu.VMEM(fog_cols.shape, F32),
-            pltpu.SemaphoreType.DMA((4 + 2,)),
+            pltpu.VMEM((tiles + 1, 2 * BS, 2 * LANES), BF16),
+            pltpu.VMEM((32 * (back_rows + 1), cols), BF16),
         ],
         mib=8,
-        name="load",
-    )
-    fine, across, part = call(
-        inner_kernel,
-        (wide, shape(tiles + 1, ext + 2 * PAD, LANES), shape(back_rows, LANES)),
-        [VMEM] * 5,
-        window,
-        band,
-        fold,
-        c_parts,
-        cover,
-        scratch=[pltpu.VMEM((rows // 2, cols), BF16)],
-        mib=8,
-        name="inner",
+        name="block",
     )
     cover, fine, sums = call(
         outer_kernel,

time: 27.9 us -> 26.3 us (0.943)
  waiting for transfers between devices: 6.73 us -> 2.77 us
  starting transfers between devices: 7.78 us -> 11.5 us
  Pallas kernels: 13.1 us -> 11.8 us
    ppermute x7, waiting for transfers between devices: 6.73 us -> 2.77 us  [move(): lax.ppermute(value, ('row', 'col'), [(i, r * col_count + c) for i, (r, c)...]
    ppermute x7, starting transfers between devices: 7.78 us -> 11.5 us  [move(): lax.ppermute(value, ('row', 'col'), [(i, r * col_count + c) for i, (r, c)...]
    pallas_call x6, Pallas kernels: 9.77 us -> 8.42 us  [call(): pl.pallas_call(kernel, out_shape=outs, in_specs=ins, out_specs=(VMEM,) *...]
  transfers between devices with their start and end apart: 7 -> 7, of which waited for: 5 -> 4; matrix products, arithmetic and copies ran while one was open for 0% -> 0% of each run, Pallas kernels for 29% -> 25%
where the time goes in v5:
time: 26.3 us; the launch traced here: 26.2 us
  Pallas kernels  11.8 us (45%)
  starting transfers between devices  11.5 us (44%)
  waiting for transfers between devices  2.77 us (11%)
    ppermute x7, starting transfers between devices, move(): lax.ppermute(value, ('row', 'col'), [(i, r * col_count + c) for i, (r, c)...  11.5 us
    pallas_call x6, Pallas kernels, call(): pl.pallas_call(kernel, out_shape=outs, in_specs=ins, out_specs=(VMEM,) *...  8.42 us
    pallas_call x1, Pallas kernels, shards(): pl.pallas_call(last_kernel, out_shape=shape(rows, cols), in_specs=[VMEM]...  3.35 us
    ppermute x7, waiting for transfers between devices, move(): lax.ppermute(value, ('row', 'col'), [(i, r * col_count + c) for i, (r, c)...  2.77 us
  transfers between devices with their start and end apart: 7, of which 4 were waited for; matrix products, arithmetic and copies ran while one was open for 0% of the time, Pallas kernels for 25%

profile of v5, /device:TPU:0, one launch (start us, length us, event | category | flops | bytes accessed | tf_op | source)
XLA Modules:
  0.0 26.2 jit_solution(3790800965962076791)
XLA Ops:
  0.0 0.0 copy-start
  0.0 1.1 %edges.1 = (f32[272,128]{1,0:T(8,128)S(1)}, f32[16,8,128]{2,1,0:T(8,128)S(1)}, f32[16,8,128]{2,1,0:T(8,128)S(1)}, f32[8,8]{1,0:T(8,128)S(1)}, f32[16,16]{1,0:T(8,128)S(1)}) custom-call(s32[256,2048]{1,0:T(8,128)} %cov_ref.3, f32[8,8]{1,0:T(8,128)} %fog_rows_ref.1, f32[16,16]{1,0:T(8,128)} %fog_cols_ref.1), custom_call_target="tpu_custom_call" | custom-call | flops 524288 | bytes 524288 | tf_op jit(solution)/shard_map/edges/pallas_call | solution.py:453
  1.2 0.6 %collective-permute-start = (f32[272,128]{1,0:T(8,128)S(1)}, f32[272,128]{1,0:T(8,128)S(1)}, u32[]{:S(2)}, u32[]{:S(2)}) collective-permute-start(f32[272,128]{1,0:T(8,128)S(1)} %get-tuple-element.37), channel_id=1, source_target_pairs={{0,1},{1,0},{2,3},{3,2},{4,5},{5,4},{6,7},{7,6},{8,9},{9,8},{10,11... | collective-permute-start | bytes 417800 | tf_op jit(solution)/shard_map/ppermute | solution.py:447
  1.7 0.6 %prep.1 = (bf16[256,256]{1,0:T(8,128)(2,1)S(1)}, bf16[2048,128]{1,0:T(8,128)(2,1)S(1)}, f32[64,128]{1,0:T(8,128)S(1)}, f32[16,128]{1,0:T(8,128)S(1)}, f32[128,256]{1,0:T(8,128)S(1)}) custom-call(f32[8,8]{1,0:T(8,128)S(1)} %get-tuple-element.38.fog_rows_ref, f32[16,16]{1,0:T(8,128)S(1)} %get-tuple-element.39.fog_cols_ref), custom_call_target="tpu_custom_call" | custom-call | flops 524288 | bytes 524288 | tf_op jit(solution)/shard_map/prep/pallas_call | solution.py:453
  2.3 0.4 %collective-permute-done.side_ref = f32[272,128]{1,0:T(8,128)S(1)} collective-permute-done((f32[272,128]{1,0:T(8,128)S(1)}, f32[272,128]{1,0:T(8,128)S(1)}, u32[]{:S(2)}, u32[]{:S(2)}) %collective-permute-start) | collective-permute-done | bytes 139296 | tf_op jit(solution)/shard_map/ppermute | solution.py:447
  2.7 2.9 %collective-permute-start.1 = (f32[17,8,128]{2,1,0:T(8,128)S(1)}, f32[17,8,128]{2,1,0:T(8,128)S(1)}, u32[]{:S(2)}, u32[]{:S(2)}) collective-permute-start(f32[17,8,128]{2,1,0:T(8,128)S(1)} %pad_maximum_fusion), channel_id=1, source_target_pairs={{0,2},{1,3},{2,0},{3,1},{4,6},{5,7},{6,4},{7,5},{8,10},{9,11},{10,... | collective-permute-start | bytes 208904 | tf_op jit(solution)/shard_map/ppermute | solution.py:447
  5.7 0.0 collective-permute-start.2
  5.7 0.0 copy-done
  5.7 3.1 %block.1 = (f32[17,272,128]{2,1,0:T(8,128)S(1)}, f32[17,272,128]{2,1,0:T(8,128)S(1)}, f32[17,288,128]{2,1,0:T(8,128)S(1)}, f32[8,128]{1,0:T(8,128)S(1)}) custom-call(s32[256,2048]{1,0:T(8,128)S(1)} %copy-done, f32[272,128]{1,0:T(8,128)S(1)} %collective-permute-done.side_ref, bf16[256,256]{1,0:T(8,128)(2,1)S(1)} %get-tuple-element.43.band_ref, ...), custom_call_target="tpu_custom_call" | custom-call | flops 524288 | bytes 524288 | tf_op jit(solution)/shard_map/block/pallas_call | solution.py:453
  8.8 0.2 collective-permute-done.1.first_ref
  9.0 0.0 collective-permute-done.2.second_ref
  9.0 0.7 %outer.1 = (f32[17,272,128]{2,1,0:T(8,128)S(1)}, f32[17,272,128]{2,1,0:T(8,128)S(1)}, f32[8,128]{1,0:T(8,128)S(1)}) custom-call(f32[17,8,128]{2,1,0:T(8,128)S(1)} %collective-permute-done.1.first_ref, f32[17,8,128]{2,1,0:T(8,128)S(1)} %collective-permute-done.2.second_ref, ...), custom_call_target="tpu_custom_call", output_to_operand_aliasing={{0}: (6, {}), {1}: (7, {})} | custom-call | flops 524288 | bytes 524288 | tf_op jit(solution)/shard_map/outer/pallas_call | solution.py:453
  9.7 2.0 %collective-permute-start.3 = (f32[8,128]{1,0:T(8,128)S(1)}, f32[8,128]{1,0:T(8,128)S(1)}, u32[]{:S(2)}, u32[]{:S(2)}) collective-permute-start(f32[8,128]{1,0:T(8,128)S(1)} %get-tuple-element.49), channel_id=1, source_target_pairs={{0,3},{1,2},{2,1},{3,0},{4,7},{5,6},{6,5},{7,4},{8,11},{9,10},{10,... | collective-permute-start | bytes 12296 | tf_op jit(solution)/shard_map/ppermute | solution.py:447
  11.7 1.3 %collective-permute-done.3 = f32[8,128]{1,0:T(8,128)S(1)} collective-permute-done((f32[8,128]{1,0:T(8,128)S(1)}, f32[8,128]{1,0:T(8,128)S(1)}, u32[]{:S(2)}, u32[]{:S(2)}) %collective-permute-start.3) | collective-permute-done | bytes 4128 | tf_op jit(solution)/shard_map/ppermute | solution.py:447
  13.1 2.1 %collective-permute-start.4 = (f32[16,128]{1,0:T(8,128)S(1)}, f32[16,128]{1,0:T(8,128)S(1)}, u32[]{:S(2)}, u32[]{:S(2)}) collective-permute-start(f32[16,128]{1,0:T(8,128)S(1)} %get-tuple-element.73.after_ref), channel_id=1, source_target_pairs={{0,5},{1,4},{2,7},{3,6},{4,1},{5,0},{6,3},{7,2},{8,13},{9,12},{10,... | collective-permute-start | bytes 24584 | tf_op jit(solution)/shard_map/ppermute | solution.py:447
  15.1 1.4 %spread.1 = (f32[17,256,128]{2,1,0:T(8,128)S(1)}, f32[17,8,8,128]{3,2,1,0:T(8,128)S(1)}, f32[17,8,8,128]{3,2,1,0:T(8,128)S(1)}) custom-call(f32[17,272,128]{2,1,0:T(8,128)S(1)} %get-tuple-element.50.cover_ref, f32[16,128]{1,0:T(8,128)S(1)} %get-tuple-element.73.after_ref), custom_call_target="tpu_custom_call" | custom-call | flops 524288 | bytes 524288 | tf_op jit(solution)/shard_map/spread/pallas_call | solution.py:453
  16.5 0.0 collective-permute-done.4
  16.5 3.5 %collective-permute-start.5 = (f32[32,128]{1,0:T(8,128)S(1)}, f32[32,128]{1,0:T(8,128)S(1)}, u32[]{:S(2)}, u32[]{:S(2)}) collective-permute-start(f32[32,128]{1,0:T(8,128)S(1)} %get-tuple-element.69.after_ref), channel_id=1, source_target_pairs={{0,9},{1,8},{2,11},{3,10},{4,13},{5,12},{6,15},{7,14},{8,1},{9,0},... | collective-permute-start | bytes 49160 | tf_op jit(solution)/shard_map/ppermute | solution.py:447
  20.0 1.5 %dose.1 = (f32[16,256,128]{2,1,0:T(8,128)S(1)}, f32[17,256,128]{2,1,0:T(8,128)S(1)}) custom-call(f32[17,272,128]{2,1,0:T(8,128)S(1)} %get-tuple-element.50.cover_ref, f32[17,272,128]{2,1,0:T(8,128)S(1)} %get-tuple-element.55.fine_ref, f32[32,128]{1,0:T(8,128)S(1)} %get-tuple-element.69.after_ref), custom_call_target="tpu_custom_call" | custom-call | flops 524288 | bytes 524288 | tf_op jit(solution)/shard_map/dose/pallas_call | solution.py:453
  21.5 0.0 collective-permute-done.5
  21.5 0.5 %collective-permute-start.6 = (f32[64,128]{1,0:T(8,128)S(1)}, f32[64,128]{1,0:T(8,128)S(1)}, u32[]{:S(2)}, u32[]{:S(2)}) collective-permute-start(f32[64,128]{1,0:T(8,128)S(1)} %pad_maximum_fusion.2), channel_id=1, source_target_pairs={{0,1},{1,0},{2,3},{3,2},{4,5},{5,4},{6,7},{7,6},{8,9},{9,8},{10,11... | collective-permute-start | bytes 98312 | tf_op jit(solution)/shard_map/ppermute | solution.py:447
  22.0 0.9 %collective-permute-done.6 = f32[64,128]{1,0:T(8,128)S(1)} collective-permute-done((f32[64,128]{1,0:T(8,128)S(1)}, f32[64,128]{1,0:T(8,128)S(1)}, u32[]{:S(2)}, u32[]{:S(2)}) %collective-permute-start.6) | collective-permute-done | bytes 32800 | tf_op jit(solution)/shard_map/ppermute | solution.py:447
  22.8 3.4 %last.1 = f32[256,2048]{1,0:T(8,128)} custom-call(f32[128,128]{1,0:T(8,128)S(1)} %constant_dynamic-update-slice_fusion.5.gathered_ref, f32[64,128]{1,0:T(8,128)S(1)} %get-tuple-element.59.left_ref, f32[16,128]{1,0:T(8,128)S(1)} %get-tuple-element.60.own_ref, f32[128,256]{1,0:T(8,128)S(1)} %get-tuple-element.61.right_ref, ...), custom_call_target="tpu_custom_call" | custom-call | tf_op jit(solution)/shard_map/last/pallas_call | solution.py:591
  (9 shorter events, 0.0 us)
Async XLA Ops:
  0.0 5.7 %copy-start = (s32[256,2048]{1,0:T(8,128)S(1)}, s32[256,2048]{1,0:T(8,128)}, u32[]{:S(2)}) copy-start(s32[256,2048]{1,0:T(8,128)} %cov_ref.3) | copy-start | bytes 6291460
  1.2 1.6 %collective-permute-start = (f32[272,128]{1,0:T(8,128)S(1)}, f32[272,128]{1,0:T(8,128)S(1)}, u32[]{:S(2)}, u32[]{:S(2)}) collective-permute-start(f32[272,128]{1,0:T(8,128)S(1)} %get-tuple-element.37), channel_id=1, source_target_pairs={{0,1},{1,0},{2,3},{3,2},{4,5},{5,4},{6,7},{7,6},{8,9},{9,8},{10,11... | collective-permute-start | bytes 417800 | tf_op jit(solution)/shard_map/ppermute | solution.py:447
  2.7 6.3 %collective-permute-start.1 = (f32[17,8,128]{2,1,0:T(8,128)S(1)}, f32[17,8,128]{2,1,0:T(8,128)S(1)}, u32[]{:S(2)}, u32[]{:S(2)}) collective-permute-start(f32[17,8,128]{2,1,0:T(8,128)S(1)} %pad_maximum_fusion), channel_id=1, source_target_pairs={{0,2},{1,3},{2,0},{3,1},{4,6},{5,7},{6,4},{7,5},{8,10},{9,11},{10,... | collective-permute-start | bytes 208904 | tf_op jit(solution)/shard_map/ppermute | solution.py:447
  5.7 3.4 %collective-permute-start.2 = (f32[17,8,128]{2,1,0:T(8,128)S(1)}, f32[17,8,128]{2,1,0:T(8,128)S(1)}, u32[]{:S(2)}, u32[]{:S(2)}) collective-permute-start(f32[17,8,128]{2,1,0:T(8,128)S(1)} %pad_maximum_fusion.1), channel_id=1, source_target_pairs={{0,1},{1,0},{2,4},{3,5},{4,2},{5,3},{6,8},{7,9},{8,6},{9,7},{10,12... | collective-permute-start | bytes 208904 | tf_op jit(solution)/shard_map/ppermute | solution.py:447
  9.7 3.4 %collective-permute-start.3 = (f32[8,128]{1,0:T(8,128)S(1)}, f32[8,128]{1,0:T(8,128)S(1)}, u32[]{:S(2)}, u32[]{:S(2)}) collective-permute-start(f32[8,128]{1,0:T(8,128)S(1)} %get-tuple-element.49), channel_id=1, source_target_pairs={{0,3},{1,2},{2,1},{3,0},{4,7},{5,6},{6,5},{7,4},{8,11},{9,10},{10,... | collective-permute-start | bytes 12296 | tf_op jit(solution)/shard_map/ppermute | solution.py:447
  13.1 3.4 %collective-permute-start.4 = (f32[16,128]{1,0:T(8,128)S(1)}, f32[16,128]{1,0:T(8,128)S(1)}, u32[]{:S(2)}, u32[]{:S(2)}) collective-permute-start(f32[16,128]{1,0:T(8,128)S(1)} %get-tuple-element.73.after_ref), channel_id=1, source_target_pairs={{0,5},{1,4},{2,7},{3,6},{4,1},{5,0},{6,3},{7,2},{8,13},{9,12},{10,... | collective-permute-start | bytes 24584 | tf_op jit(solution)/shard_map/ppermute | solution.py:447
  16.5 5.0 %collective-permute-start.5 = (f32[32,128]{1,0:T(8,128)S(1)}, f32[32,128]{1,0:T(8,128)S(1)}, u32[]{:S(2)}, u32[]{:S(2)}) collective-permute-start(f32[32,128]{1,0:T(8,128)S(1)} %get-tuple-element.69.after_ref), channel_id=1, source_target_pairs={{0,9},{1,8},{2,11},{3,10},{4,13},{5,12},{6,15},{7,14},{8,1},{9,0},... | collective-permute-start | bytes 49160 | tf_op jit(solution)/shard_map/ppermute | solution.py:447
  21.5 1.3 %collective-permute-start.6 = (f32[64,128]{1,0:T(8,128)S(1)}, f32[64,128]{1,0:T(8,128)S(1)}, u32[]{:S(2)}, u32[]{:S(2)}) collective-permute-start(f32[64,128]{1,0:T(8,128)S(1)} %pad_maximum_fusion.2), channel_id=1, source_target_pairs={{0,1},{1,0},{2,3},{3,2},{4,5},{5,4},{6,7},{7,6},{8,9},{9,8},{10,11... | collective-permute-start | bytes 98312 | tf_op jit(solution)/shard_map/ppermute | solution.py:447

commit v6 on v5

--- a/solution.py
+++ b/solution.py
@@ -168,8 +168,9 @@
         at = slice(EDGE + first, EDGE + first + part)
 
         def put(t, value):
-            window[t, :, :LANES] = value
-            window[(t - 1) % (tiles + 1), :, LANES:] = value
+            window[t] = value
+            if t == 0:
+                window[tiles + 1] = value
 
         side = jnp.where(touches, side_ref[first : first + part, :], 0.0)
         cover_ref[tiles, at, :] = side
@@ -185,8 +186,8 @@
             keep(0, c_rows, 8 * (first // BS), span, [eights(value[i : i + BS]) for i in range(0, part, BS)])
         put(tiles, jnp.where(lane < HALF, before, side).astype(BF16))
         for t, count in chunks(0, tiles + 1, 6):
-            some = window[t : t + count].reshape(count * part, 2 * LANES)
-            both = jnp.dot(some, band_ref[...], preferred_element_type=F32)
+            some = [jnp.concatenate([window[t + i], window[t + i + 1]], axis=1) for i in range(count)]
+            both = jnp.dot(jnp.concatenate(some, axis=0), band_ref[...], preferred_element_type=F32)
             for i in range(count):
                 mine = both[i * part : (i + 1) * part]
                 across[t + i, PAD + EDGE + first : PAD + EDGE + first + part, :] = mine[:, :LANES] + mine[:, LANES:]
@@ -523,7 +524,7 @@
         band,
         fold,
         scratch=[
-            pltpu.VMEM((tiles + 1, 2 * BS, 2 * LANES), BF16),
+            pltpu.VMEM((tiles + 2, 2 * BS, LANES), BF16),
             pltpu.VMEM((32 * (back_rows + 1), cols), BF16),
         ],
         mib=8,
@@ -577,7 +578,7 @@
     bit = 1
     while bit < row_count:
         other = move(gathered, lambda r, c: (r ^ bit, 1 - c))
-        if bit > 1 and pending:
+        if pending:
             results = pending.pop(0)(gathered)
             other, *results = lax.optimization_barrier((other, *results))
             done += results

time: 26.3 us -> 26.3 us (level)
  no operation moved by 1% of the time
where the time goes in v6:
time: 26.3 us; the launch traced here: 26.1 us
  Pallas kernels  11.7 us (44%)
  starting transfers between devices  11.4 us (43%)
  waiting for transfers between devices  2.99 us (11%)
    ppermute x7, starting transfers between devices, move(): lax.ppermute(value, ('row', 'col'), [(i, r * col_count + c) for i, (r, c)...  11.4 us
    pallas_call x6, Pallas kernels, call(): pl.pallas_call(kernel, out_shape=outs, in_specs=ins, out_specs=(VMEM,) *...  8.31 us
    pallas_call x1, Pallas kernels, shards(): pl.pallas_call(last_kernel, out_shape=shape(rows, cols), in_specs=[VMEM]...  3.35 us
    ppermute x7, waiting for transfers between devices, move(): lax.ppermute(value, ('row', 'col'), [(i, r * col_count + c) for i, (r, c)...  2.99 us
  transfers between devices with their start and end apart: 7, of which 4 were waited for; matrix products, arithmetic and copies ran while one was open for 0% of the time, Pallas kernels for 25%

profile of v6, /device:TPU:0, one launch (start us, length us, event | category | flops | bytes accessed | tf_op | source)
XLA Modules:
  0.0 26.1 jit_solution(17957095461001562188)
XLA Ops:
  0.0 0.0 copy-start
  0.0 1.1 %edges.1 = (f32[272,128]{1,0:T(8,128)S(1)}, f32[16,8,128]{2,1,0:T(8,128)S(1)}, f32[16,8,128]{2,1,0:T(8,128)S(1)}, f32[8,8]{1,0:T(8,128)S(1)}, f32[16,16]{1,0:T(8,128)S(1)}) custom-call(s32[256,2048]{1,0:T(8,128)} %cov_ref.3, f32[8,8]{1,0:T(8,128)} %fog_rows_ref.1, f32[16,16]{1,0:T(8,128)} %fog_cols_ref.1), custom_call_target="tpu_custom_call" | custom-call | flops 524288 | bytes 524288 | tf_op jit(solution)/shard_map/edges/pallas_call | solution.py:454
  1.2 0.6 %collective-permute-start = (f32[272,128]{1,0:T(8,128)S(1)}, f32[272,128]{1,0:T(8,128)S(1)}, u32[]{:S(2)}, u32[]{:S(2)}) collective-permute-start(f32[272,128]{1,0:T(8,128)S(1)} %get-tuple-element.37), channel_id=1, source_target_pairs={{0,1},{1,0},{2,3},{3,2},{4,5},{5,4},{6,7},{7,6},{8,9},{9,8},{10,11... | collective-permute-start | bytes 417800 | tf_op jit(solution)/shard_map/ppermute | solution.py:448
  1.7 0.6 %prep.1 = (bf16[256,256]{1,0:T(8,128)(2,1)S(1)}, bf16[2048,128]{1,0:T(8,128)(2,1)S(1)}, f32[64,128]{1,0:T(8,128)S(1)}, f32[16,128]{1,0:T(8,128)S(1)}, f32[128,256]{1,0:T(8,128)S(1)}) custom-call(f32[8,8]{1,0:T(8,128)S(1)} %get-tuple-element.38.fog_rows_ref, f32[16,16]{1,0:T(8,128)S(1)} %get-tuple-element.39.fog_cols_ref), custom_call_target="tpu_custom_call" | custom-call | flops 524288 | bytes 524288 | tf_op jit(solution)/shard_map/prep/pallas_call | solution.py:454
  2.3 0.4 %collective-permute-done.side_ref = f32[272,128]{1,0:T(8,128)S(1)} collective-permute-done((f32[272,128]{1,0:T(8,128)S(1)}, f32[272,128]{1,0:T(8,128)S(1)}, u32[]{:S(2)}, u32[]{:S(2)}) %collective-permute-start) | collective-permute-done | bytes 139296 | tf_op jit(solution)/shard_map/ppermute | solution.py:448
  2.7 2.9 %collective-permute-start.1 = (f32[17,8,128]{2,1,0:T(8,128)S(1)}, f32[17,8,128]{2,1,0:T(8,128)S(1)}, u32[]{:S(2)}, u32[]{:S(2)}) collective-permute-start(f32[17,8,128]{2,1,0:T(8,128)S(1)} %pad_maximum_fusion), channel_id=1, source_target_pairs={{0,2},{1,3},{2,0},{3,1},{4,6},{5,7},{6,4},{7,5},{8,10},{9,11},{10,... | collective-permute-start | bytes 208904 | tf_op jit(solution)/shard_map/ppermute | solution.py:448
  5.7 0.0 collective-permute-start.2
  5.7 0.0 copy-done
  5.7 3.0 %block.1 = (f32[17,272,128]{2,1,0:T(8,128)S(1)}, f32[17,272,128]{2,1,0:T(8,128)S(1)}, f32[17,288,128]{2,1,0:T(8,128)S(1)}, f32[8,128]{1,0:T(8,128)S(1)}) custom-call(s32[256,2048]{1,0:T(8,128)S(1)} %copy-done, f32[272,128]{1,0:T(8,128)S(1)} %collective-permute-done.side_ref, bf16[256,256]{1,0:T(8,128)(2,1)S(1)} %get-tuple-element.43.band_ref, ...), custom_call_target="tpu_custom_call" | custom-call | flops 524288 | bytes 524288 | tf_op jit(solution)/shard_map/block/pallas_call | solution.py:454
  8.7 0.3 %collective-permute-done.1.first_ref = f32[17,8,128]{2,1,0:T(8,128)S(1)} collective-permute-done((f32[17,8,128]{2,1,0:T(8,128)S(1)}, f32[17,8,128]{2,1,0:T(8,128)S(1)}, u32[]{:S(2)}, u32[]{:S(2)}) %collective-permute-start.1) | collective-permute-done | bytes 69664 | tf_op jit(solution)/shard_map/ppermute | solution.py:448
  9.0 0.0 collective-permute-done.2.second_ref
  9.0 0.7 %outer.1 = (f32[17,272,128]{2,1,0:T(8,128)S(1)}, f32[17,272,128]{2,1,0:T(8,128)S(1)}, f32[8,128]{1,0:T(8,128)S(1)}) custom-call(f32[17,8,128]{2,1,0:T(8,128)S(1)} %collective-permute-done.1.first_ref, f32[17,8,128]{2,1,0:T(8,128)S(1)} %collective-permute-done.2.second_ref, ...), custom_call_target="tpu_custom_call", output_to_operand_aliasing={{0}: (6, {}), {1}: (7, {})} | custom-call | flops 524288 | bytes 524288 | tf_op jit(solution)/shard_map/outer/pallas_call | solution.py:454
  9.7 1.9 %collective-permute-start.3 = (f32[8,128]{1,0:T(8,128)S(1)}, f32[8,128]{1,0:T(8,128)S(1)}, u32[]{:S(2)}, u32[]{:S(2)}) collective-permute-start(f32[8,128]{1,0:T(8,128)S(1)} %get-tuple-element.49.after_ref), channel_id=1, source_target_pairs={{0,3},{1,2},{2,1},{3,0},{4,7},{5,6},{6,5},{7,4},{8,11},{9,10},{10,... | collective-permute-start | bytes 12296 | tf_op jit(solution)/shard_map/ppermute | solution.py:448
  11.6 1.4 %spread.1 = (f32[17,256,128]{2,1,0:T(8,128)S(1)}, f32[17,8,8,128]{3,2,1,0:T(8,128)S(1)}, f32[17,8,8,128]{3,2,1,0:T(8,128)S(1)}) custom-call(f32[17,272,128]{2,1,0:T(8,128)S(1)} %get-tuple-element.50.cover_ref, f32[8,128]{1,0:T(8,128)S(1)} %get-tuple-element.49.after_ref), custom_call_target="tpu_custom_call" | custom-call | flops 524288 | bytes 524288 | tf_op jit(solution)/shard_map/spread/pallas_call | solution.py:454
  13.0 0.0 collective-permute-done.3
  13.0 2.2 %collective-permute-start.4 = (f32[16,128]{1,0:T(8,128)S(1)}, f32[16,128]{1,0:T(8,128)S(1)}, u32[]{:S(2)}, u32[]{:S(2)}) collective-permute-start(f32[16,128]{1,0:T(8,128)S(1)} %get-tuple-element.69.after_ref), channel_id=1, source_target_pairs={{0,5},{1,4},{2,7},{3,6},{4,1},{5,0},{6,3},{7,2},{8,13},{9,12},{10,... | collective-permute-start | bytes 24584 | tf_op jit(solution)/shard_map/ppermute | solution.py:448
  15.2 1.5 %dose.1 = (f32[16,256,128]{2,1,0:T(8,128)S(1)}, f32[17,256,128]{2,1,0:T(8,128)S(1)}) custom-call(f32[17,272,128]{2,1,0:T(8,128)S(1)} %get-tuple-element.50.cover_ref, f32[17,272,128]{2,1,0:T(8,128)S(1)} %get-tuple-element.55.fine_ref, f32[16,128]{1,0:T(8,128)S(1)} %get-tuple-element.69.after_ref), custom_call_target="tpu_custom_call" | custom-call | flops 524288 | bytes 524288 | tf_op jit(solution)/shard_map/dose/pallas_call | solution.py:454
  16.7 0.0 collective-permute-done.4
  16.7 3.3 %collective-permute-start.5 = (f32[32,128]{1,0:T(8,128)S(1)}, f32[32,128]{1,0:T(8,128)S(1)}, u32[]{:S(2)}, u32[]{:S(2)}) collective-permute-start(f32[32,128]{1,0:T(8,128)S(1)} %pad_maximum_fusion.3), channel_id=1, source_target_pairs={{0,9},{1,8},{2,11},{3,10},{4,13},{5,12},{6,15},{7,14},{8,1},{9,0},... | collective-permute-start | bytes 49160 | tf_op jit(solution)/shard_map/ppermute | solution.py:448
  20.1 1.4 %collective-permute-done.5 = f32[32,128]{1,0:T(8,128)S(1)} collective-permute-done((f32[32,128]{1,0:T(8,128)S(1)}, f32[32,128]{1,0:T(8,128)S(1)}, u32[]{:S(2)}, u32[]{:S(2)}) %collective-permute-start.5) | collective-permute-done | bytes 16416 | tf_op jit(solution)/shard_map/ppermute | solution.py:448
  21.5 0.4 %collective-permute-start.6 = (f32[64,128]{1,0:T(8,128)S(1)}, f32[64,128]{1,0:T(8,128)S(1)}, u32[]{:S(2)}, u32[]{:S(2)}) collective-permute-start(f32[64,128]{1,0:T(8,128)S(1)} %pad_maximum_fusion.2), channel_id=1, source_target_pairs={{0,1},{1,0},{2,3},{3,2},{4,5},{5,4},{6,7},{7,6},{8,9},{9,8},{10,11... | collective-permute-start | bytes 98312 | tf_op jit(solution)/shard_map/ppermute | solution.py:448
  21.9 0.9 %collective-permute-done.6 = f32[64,128]{1,0:T(8,128)S(1)} collective-permute-done((f32[64,128]{1,0:T(8,128)S(1)}, f32[64,128]{1,0:T(8,128)S(1)}, u32[]{:S(2)}, u32[]{:S(2)}) %collective-permute-start.6) | collective-permute-done | bytes 32800 | tf_op jit(solution)/shard_map/ppermute | solution.py:448
  22.8 3.3 %last.1 = f32[256,2048]{1,0:T(8,128)} custom-call(f32[128,128]{1,0:T(8,128)S(1)} %constant_dynamic-update-slice_fusion.2.gathered_ref, f32[64,128]{1,0:T(8,128)S(1)} %get-tuple-element.59.left_ref, f32[16,128]{1,0:T(8,128)S(1)} %get-tuple-element.60.own_ref, f32[128,256]{1,0:T(8,128)S(1)} %get-tuple-element.61.right_ref, ...), custom_call_target="tpu_custom_call" | custom-call | tf_op jit(solution)/shard_map/last/pallas_call | solution.py:592
  (10 shorter events, 0.0 us)
Async XLA Ops:
  0.0 5.7 %copy-start = (s32[256,2048]{1,0:T(8,128)S(1)}, s32[256,2048]{1,0:T(8,128)}, u32[]{:S(2)}) copy-start(s32[256,2048]{1,0:T(8,128)} %cov_ref.3) | copy-start | bytes 6291460
  1.2 1.6 %collective-permute-start = (f32[272,128]{1,0:T(8,128)S(1)}, f32[272,128]{1,0:T(8,128)S(1)}, u32[]{:S(2)}, u32[]{:S(2)}) collective-permute-start(f32[272,128]{1,0:T(8,128)S(1)} %get-tuple-element.37), channel_id=1, source_target_pairs={{0,1},{1,0},{2,3},{3,2},{4,5},{5,4},{6,7},{7,6},{8,9},{9,8},{10,11... | collective-permute-start | bytes 417800 | tf_op jit(solution)/shard_map/ppermute | solution.py:448
  2.7 6.3 %collective-permute-start.1 = (f32[17,8,128]{2,1,0:T(8,128)S(1)}, f32[17,8,128]{2,1,0:T(8,128)S(1)}, u32[]{:S(2)}, u32[]{:S(2)}) collective-permute-start(f32[17,8,128]{2,1,0:T(8,128)S(1)} %pad_maximum_fusion), channel_id=1, source_target_pairs={{0,2},{1,3},{2,0},{3,1},{4,6},{5,7},{6,4},{7,5},{8,10},{9,11},{10,... | collective-permute-start | bytes 208904 | tf_op jit(solution)/shard_map/ppermute | solution.py:448
  5.7 3.4 %collective-permute-start.2 = (f32[17,8,128]{2,1,0:T(8,128)S(1)}, f32[17,8,128]{2,1,0:T(8,128)S(1)}, u32[]{:S(2)}, u32[]{:S(2)}) collective-permute-start(f32[17,8,128]{2,1,0:T(8,128)S(1)} %pad_maximum_fusion.1), channel_id=1, source_target_pairs={{0,1},{1,0},{2,4},{3,5},{4,2},{5,3},{6,8},{7,9},{8,6},{9,7},{10,12... | collective-permute-start | bytes 208904 | tf_op jit(solution)/shard_map/ppermute | solution.py:448
  9.7 3.3 %collective-permute-start.3 = (f32[8,128]{1,0:T(8,128)S(1)}, f32[8,128]{1,0:T(8,128)S(1)}, u32[]{:S(2)}, u32[]{:S(2)}) collective-permute-start(f32[8,128]{1,0:T(8,128)S(1)} %get-tuple-element.49.after_ref), channel_id=1, source_target_pairs={{0,3},{1,2},{2,1},{3,0},{4,7},{5,6},{6,5},{7,4},{8,11},{9,10},{10,... | collective-permute-start | bytes 12296 | tf_op jit(solution)/shard_map/ppermute | solution.py:448
  13.0 3.7 %collective-permute-start.4 = (f32[16,128]{1,0:T(8,128)S(1)}, f32[16,128]{1,0:T(8,128)S(1)}, u32[]{:S(2)}, u32[]{:S(2)}) collective-permute-start(f32[16,128]{1,0:T(8,128)S(1)} %get-tuple-element.69.after_ref), channel_id=1, source_target_pairs={{0,5},{1,4},{2,7},{3,6},{4,1},{5,0},{6,3},{7,2},{8,13},{9,12},{10,... | collective-permute-start | bytes 24584 | tf_op jit(solution)/shard_map/ppermute | solution.py:448
  16.7 4.8 %collective-permute-start.5 = (f32[32,128]{1,0:T(8,128)S(1)}, f32[32,128]{1,0:T(8,128)S(1)}, u32[]{:S(2)}, u32[]{:S(2)}) collective-permute-start(f32[32,128]{1,0:T(8,128)S(1)} %pad_maximum_fusion.3), channel_id=1, source_target_pairs={{0,9},{1,8},{2,11},{3,10},{4,13},{5,12},{6,15},{7,14},{8,1},{9,0},... | collective-permute-start | bytes 49160 | tf_op jit(solution)/shard_map/ppermute | solution.py:448
  21.5 1.3 %collective-permute-start.6 = (f32[64,128]{1,0:T(8,128)S(1)}, f32[64,128]{1,0:T(8,128)S(1)}, u32[]{:S(2)}, u32[]{:S(2)}) collective-permute-start(f32[64,128]{1,0:T(8,128)S(1)} %pad_maximum_fusion.2), channel_id=1, source_target_pairs={{0,1},{1,0},{2,3},{3,2},{4,5},{5,4},{6,7},{7,6},{8,9},{9,8},{10,11... | collective-permute-start | bytes 98312 | tf_op jit(solution)/shard_map/ppermute | solution.py:448

commit v7 on v6

--- a/solution.py
+++ b/solution.py
@@ -327,12 +327,13 @@
     lane = iota((1, LANES), 1)
     count = n_rows // cells
     for j in range(count):
+        far = sum(count // 2 >> i for i in range(count.bit_length() - 1) if j >> i & 1)
         mine = gathered_ref[j * cells : (j + 1) * cells, :]
         other = gathered_ref[(count + j) * cells : (count + j + 1) * cells, :]
         here = col == bin(j).count("1") % 2
         low = jnp.where(here, mine, other)
         high = jnp.where(here, other, mine)
-        at = pl.ds(pl.multiple_of((row ^ j) * cells, cells), cells)
+        at = pl.ds(pl.multiple_of((row ^ far) * cells, cells), cells)
         c_all[at, :] = jnp.where(lane8 < HALF, low, pltpu.roll(high, HALF, 1)) * F32(1.0 / (255.0 * BS * BS))
         f_all[at, :] = jnp.where(lane8 < HALF, pltpu.roll(low, HALF, 1), high) * F32(1.0 / (255.0 * 255.0 * BS * BS))
     right = right_ref[...]
@@ -575,15 +576,15 @@
     pending = [spread, first_dose]
     done = []
     gathered = sums
-    bit = 1
-    while bit < row_count:
+    bit = row_count // 2
+    while bit:
         other = move(gathered, lambda r, c: (r ^ bit, 1 - c))
         if pending:
             results = pending.pop(0)(gathered)
             other, *results = lax.optimization_barrier((other, *results))
             done += results
         gathered = jnp.concatenate([gathered, other], axis=0)
-        bit *= 2
+        bit //= 2
     gathered = jnp.concatenate([gathered, move(gathered, lambda r, c: (r, 1 - c))], axis=0)
     for work in pending:
         done += work(gathered)

time: 26.3 us -> 26.4 us (level)
  waiting for transfers between devices: 2.99 us -> 3.95 us
  starting transfers between devices: 11.4 us -> 10.5 us
    ppermute x7, waiting for transfers between devices: 2.99 us -> 3.95 us  [move(): lax.ppermute(value, ('row', 'col'), [(i, r * col_count + c) for i, (r, c)...]
    ppermute x7, starting transfers between devices: 11.4 us -> 10.5 us  [move(): lax.ppermute(value, ('row', 'col'), [(i, r * col_count + c) for i, (r, c)...]
where the time goes in v7:
time: 26.4 us; the launch traced here: 26.2 us
  Pallas kernels  11.7 us (44%)
  starting transfers between devices  10.5 us (40%)
  waiting for transfers between devices  3.95 us (15%)
    ppermute x7, starting transfers between devices, move(): lax.ppermute(value, ('row', 'col'), [(i, r * col_count + c) for i, (r, c)...  10.5 us
    pallas_call x6, Pallas kernels, call(): pl.pallas_call(kernel, out_shape=outs, in_specs=ins, out_specs=(VMEM,) *...  8.31 us
    ppermute x7, waiting for transfers between devices, move(): lax.ppermute(value, ('row', 'col'), [(i, r * col_count + c) for i, (r, c)...  3.95 us
    pallas_call x1, Pallas kernels, shards(): pl.pallas_call(last_kernel, out_shape=shape(rows, cols), in_specs=[VMEM]...  3.35 us
  transfers between devices with their start and end apart: 7, of which 4 were waited for; matrix products, arithmetic and copies ran while one was open for 0% of the time, Pallas kernels for 25%

profile of v7, /device:TPU:0, one launch (start us, length us, event | category | flops | bytes accessed | tf_op | source)
XLA Modules:
  0.0 26.2 jit_solution(5223896082631390491)
XLA Ops:
  0.0 0.0 copy-start
  0.0 1.1 %edges.1 = (f32[272,128]{1,0:T(8,128)S(1)}, f32[16,8,128]{2,1,0:T(8,128)S(1)}, f32[16,8,128]{2,1,0:T(8,128)S(1)}, f32[8,8]{1,0:T(8,128)S(1)}, f32[16,16]{1,0:T(8,128)S(1)}) custom-call(s32[256,2048]{1,0:T(8,128)} %cov_ref.3, f32[8,8]{1,0:T(8,128)} %fog_rows_ref.1, f32[16,16]{1,0:T(8,128)} %fog_cols_ref.1), custom_call_target="tpu_custom_call" | custom-call | flops 524288 | bytes 524288 | tf_op jit(solution)/shard_map/edges/pallas_call | solution.py:455
  1.2 0.6 %collective-permute-start = (f32[272,128]{1,0:T(8,128)S(1)}, f32[272,128]{1,0:T(8,128)S(1)}, u32[]{:S(2)}, u32[]{:S(2)}) collective-permute-start(f32[272,128]{1,0:T(8,128)S(1)} %get-tuple-element.37), channel_id=1, source_target_pairs={{0,1},{1,0},{2,3},{3,2},{4,5},{5,4},{6,7},{7,6},{8,9},{9,8},{10,11... | collective-permute-start | bytes 417800 | tf_op jit(solution)/shard_map/ppermute | solution.py:449
  1.7 0.6 %prep.1 = (bf16[256,256]{1,0:T(8,128)(2,1)S(1)}, bf16[2048,128]{1,0:T(8,128)(2,1)S(1)}, f32[64,128]{1,0:T(8,128)S(1)}, f32[16,128]{1,0:T(8,128)S(1)}, f32[128,256]{1,0:T(8,128)S(1)}) custom-call(f32[8,8]{1,0:T(8,128)S(1)} %get-tuple-element.38.fog_rows_ref, f32[16,16]{1,0:T(8,128)S(1)} %get-tuple-element.39.fog_cols_ref), custom_call_target="tpu_custom_call" | custom-call | flops 524288 | bytes 524288 | tf_op jit(solution)/shard_map/prep/pallas_call | solution.py:455
  2.3 0.4 %collective-permute-done.side_ref = f32[272,128]{1,0:T(8,128)S(1)} collective-permute-done((f32[272,128]{1,0:T(8,128)S(1)}, f32[272,128]{1,0:T(8,128)S(1)}, u32[]{:S(2)}, u32[]{:S(2)}) %collective-permute-start) | collective-permute-done | bytes 139296 | tf_op jit(solution)/shard_map/ppermute | solution.py:449
  2.7 2.9 %collective-permute-start.1 = (f32[17,8,128]{2,1,0:T(8,128)S(1)}, f32[17,8,128]{2,1,0:T(8,128)S(1)}, u32[]{:S(2)}, u32[]{:S(2)}) collective-permute-start(f32[17,8,128]{2,1,0:T(8,128)S(1)} %pad_maximum_fusion), channel_id=1, source_target_pairs={{0,2},{1,3},{2,0},{3,1},{4,6},{5,7},{6,4},{7,5},{8,10},{9,11},{10,... | collective-permute-start | bytes 208904 | tf_op jit(solution)/shard_map/ppermute | solution.py:449
  5.7 0.0 collective-permute-start.2
  5.7 0.0 copy-done
  5.7 3.0 %block.1 = (f32[17,272,128]{2,1,0:T(8,128)S(1)}, f32[17,272,128]{2,1,0:T(8,128)S(1)}, f32[17,288,128]{2,1,0:T(8,128)S(1)}, f32[8,128]{1,0:T(8,128)S(1)}) custom-call(s32[256,2048]{1,0:T(8,128)S(1)} %copy-done, f32[272,128]{1,0:T(8,128)S(1)} %collective-permute-done.side_ref, bf16[256,256]{1,0:T(8,128)(2,1)S(1)} %get-tuple-element.43.band_ref, ...), custom_call_target="tpu_custom_call" | custom-call | flops 524288 | bytes 524288 | tf_op jit(solution)/shard_map/block/pallas_call | solution.py:455
  8.7 0.3 %collective-permute-done.1.first_ref = f32[17,8,128]{2,1,0:T(8,128)S(1)} collective-permute-done((f32[17,8,128]{2,1,0:T(8,128)S(1)}, f32[17,8,128]{2,1,0:T(8,128)S(1)}, u32[]{:S(2)}, u32[]{:S(2)}) %collective-permute-start.1) | collective-permute-done | bytes 69664 | tf_op jit(solution)/shard_map/ppermute | solution.py:449
  9.0 0.0 collective-permute-done.2.second_ref
  9.0 0.7 %outer.1 = (f32[17,272,128]{2,1,0:T(8,128)S(1)}, f32[17,272,128]{2,1,0:T(8,128)S(1)}, f32[8,128]{1,0:T(8,128)S(1)}) custom-call(f32[17,8,128]{2,1,0:T(8,128)S(1)} %collective-permute-done.1.first_ref, f32[17,8,128]{2,1,0:T(8,128)S(1)} %collective-permute-done.2.second_ref, ...), custom_call_target="tpu_custom_call", output_to_operand_aliasing={{0}: (6, {}), {1}: (7, {})} | custom-call | flops 524288 | bytes 524288 | tf_op jit(solution)/shard_map/outer/pallas_call | solution.py:455
  9.7 2.8 %collective-permute-start.3 = (f32[8,128]{1,0:T(8,128)S(1)}, f32[8,128]{1,0:T(8,128)S(1)}, u32[]{:S(2)}, u32[]{:S(2)}) collective-permute-start(f32[8,128]{1,0:T(8,128)S(1)} %get-tuple-element.49.after_ref), channel_id=1, source_target_pairs={{0,9},{1,8},{2,11},{3,10},{4,13},{5,12},{6,15},{7,14},{8,1},{9,0},... | collective-permute-start | bytes 12296 | tf_op jit(solution)/shard_map/ppermute | solution.py:449
  12.5 1.4 %spread.1 = (f32[17,256,128]{2,1,0:T(8,128)S(1)}, f32[17,8,8,128]{3,2,1,0:T(8,128)S(1)}, f32[17,8,8,128]{3,2,1,0:T(8,128)S(1)}) custom-call(f32[17,272,128]{2,1,0:T(8,128)S(1)} %get-tuple-element.50.cover_ref, f32[8,128]{1,0:T(8,128)S(1)} %get-tuple-element.49.after_ref), custom_call_target="tpu_custom_call" | custom-call | flops 524288 | bytes 524288 | tf_op jit(solution)/shard_map/spread/pallas_call | solution.py:455
  13.8 0.0 collective-permute-done.3
  13.8 3.0 %collective-permute-start.4 = (f32[16,128]{1,0:T(8,128)S(1)}, f32[16,128]{1,0:T(8,128)S(1)}, u32[]{:S(2)}, u32[]{:S(2)}) collective-permute-start(f32[16,128]{1,0:T(8,128)S(1)} %get-tuple-element.69.after_ref), channel_id=1, source_target_pairs={{0,5},{1,4},{2,7},{3,6},{4,1},{5,0},{6,3},{7,2},{8,13},{9,12},{10,... | collective-permute-start | bytes 24584 | tf_op jit(solution)/shard_map/ppermute | solution.py:449
  16.9 1.5 %dose.1 = (f32[16,256,128]{2,1,0:T(8,128)S(1)}, f32[17,256,128]{2,1,0:T(8,128)S(1)}) custom-call(f32[17,272,128]{2,1,0:T(8,128)S(1)} %get-tuple-element.50.cover_ref, f32[17,272,128]{2,1,0:T(8,128)S(1)} %get-tuple-element.55.fine_ref, f32[16,128]{1,0:T(8,128)S(1)} %get-tuple-element.69.after_ref), custom_call_target="tpu_custom_call" | custom-call | flops 524288 | bytes 524288 | tf_op jit(solution)/shard_map/dose/pallas_call | solution.py:455
  18.4 0.0 collective-permute-done.4
  18.4 0.9 %collective-permute-start.5 = (f32[32,128]{1,0:T(8,128)S(1)}, f32[32,128]{1,0:T(8,128)S(1)}, u32[]{:S(2)}, u32[]{:S(2)}) collective-permute-start(f32[32,128]{1,0:T(8,128)S(1)} %pad_maximum_fusion.3), channel_id=1, source_target_pairs={{0,3},{1,2},{2,1},{3,0},{4,7},{5,6},{6,5},{7,4},{8,11},{9,10},{10,... | collective-permute-start | bytes 49160 | tf_op jit(solution)/shard_map/ppermute | solution.py:449
  19.3 2.4 %collective-permute-done.5 = f32[32,128]{1,0:T(8,128)S(1)} collective-permute-done((f32[32,128]{1,0:T(8,128)S(1)}, f32[32,128]{1,0:T(8,128)S(1)}, u32[]{:S(2)}, u32[]{:S(2)}) %collective-permute-start.5) | collective-permute-done | bytes 16416 | tf_op jit(solution)/shard_map/ppermute | solution.py:449
  21.7 0.3 %collective-permute-start.6 = (f32[64,128]{1,0:T(8,128)S(1)}, f32[64,128]{1,0:T(8,128)S(1)}, u32[]{:S(2)}, u32[]{:S(2)}) collective-permute-start(f32[64,128]{1,0:T(8,128)S(1)} %pad_maximum_fusion.2), channel_id=1, source_target_pairs={{0,1},{1,0},{2,3},{3,2},{4,5},{5,4},{6,7},{7,6},{8,9},{9,8},{10,11... | collective-permute-start | bytes 98312 | tf_op jit(solution)/shard_map/ppermute | solution.py:449
  22.0 0.9 %collective-permute-done.6 = f32[64,128]{1,0:T(8,128)S(1)} collective-permute-done((f32[64,128]{1,0:T(8,128)S(1)}, f32[64,128]{1,0:T(8,128)S(1)}, u32[]{:S(2)}, u32[]{:S(2)}) %collective-permute-start.6) | collective-permute-done | bytes 32800 | tf_op jit(solution)/shard_map/ppermute | solution.py:449
  22.9 3.4 %last.1 = f32[256,2048]{1,0:T(8,128)} custom-call(f32[128,128]{1,0:T(8,128)S(1)} %constant_dynamic-update-slice_fusion.2.gathered_ref, f32[64,128]{1,0:T(8,128)S(1)} %get-tuple-element.59.left_ref, f32[16,128]{1,0:T(8,128)S(1)} %get-tuple-element.60.own_ref, f32[128,256]{1,0:T(8,128)S(1)} %get-tuple-element.61.right_ref, ...), custom_call_target="tpu_custom_call" | custom-call | tf_op jit(solution)/shard_map/last/pallas_call | solution.py:593
  (10 shorter events, 0.0 us)
Async XLA Ops:
  0.0 5.7 %copy-start = (s32[256,2048]{1,0:T(8,128)S(1)}, s32[256,2048]{1,0:T(8,128)}, u32[]{:S(2)}) copy-start(s32[256,2048]{1,0:T(8,128)} %cov_ref.3) | copy-start | bytes 6291460
  1.2 1.6 %collective-permute-start = (f32[272,128]{1,0:T(8,128)S(1)}, f32[272,128]{1,0:T(8,128)S(1)}, u32[]{:S(2)}, u32[]{:S(2)}) collective-permute-start(f32[272,128]{1,0:T(8,128)S(1)} %get-tuple-element.37), channel_id=1, source_target_pairs={{0,1},{1,0},{2,3},{3,2},{4,5},{5,4},{6,7},{7,6},{8,9},{9,8},{10,11... | collective-permute-start | bytes 417800 | tf_op jit(solution)/shard_map/ppermute | solution.py:449
  2.7 6.3 %collective-permute-start.1 = (f32[17,8,128]{2,1,0:T(8,128)S(1)}, f32[17,8,128]{2,1,0:T(8,128)S(1)}, u32[]{:S(2)}, u32[]{:S(2)}) collective-permute-start(f32[17,8,128]{2,1,0:T(8,128)S(1)} %pad_maximum_fusion), channel_id=1, source_target_pairs={{0,2},{1,3},{2,0},{3,1},{4,6},{5,7},{6,4},{7,5},{8,10},{9,11},{10,... | collective-permute-start | bytes 208904 | tf_op jit(solution)/shard_map/ppermute | solution.py:449
  5.7 3.4 %collective-permute-start.2 = (f32[17,8,128]{2,1,0:T(8,128)S(1)}, f32[17,8,128]{2,1,0:T(8,128)S(1)}, u32[]{:S(2)}, u32[]{:S(2)}) collective-permute-start(f32[17,8,128]{2,1,0:T(8,128)S(1)} %pad_maximum_fusion.1), channel_id=1, source_target_pairs={{0,1},{1,0},{2,4},{3,5},{4,2},{5,3},{6,8},{7,9},{8,6},{9,7},{10,12... | collective-permute-start | bytes 208904 | tf_op jit(solution)/shard_map/ppermute | solution.py:449
  9.7 4.1 %collective-permute-start.3 = (f32[8,128]{1,0:T(8,128)S(1)}, f32[8,128]{1,0:T(8,128)S(1)}, u32[]{:S(2)}, u32[]{:S(2)}) collective-permute-start(f32[8,128]{1,0:T(8,128)S(1)} %get-tuple-element.49.after_ref), channel_id=1, source_target_pairs={{0,9},{1,8},{2,11},{3,10},{4,13},{5,12},{6,15},{7,14},{8,1},{9,0},... | collective-permute-start | bytes 12296 | tf_op jit(solution)/shard_map/ppermute | solution.py:449
  13.8 4.5 %collective-permute-start.4 = (f32[16,128]{1,0:T(8,128)S(1)}, f32[16,128]{1,0:T(8,128)S(1)}, u32[]{:S(2)}, u32[]{:S(2)}) collective-permute-start(f32[16,128]{1,0:T(8,128)S(1)} %get-tuple-element.69.after_ref), channel_id=1, source_target_pairs={{0,5},{1,4},{2,7},{3,6},{4,1},{5,0},{6,3},{7,2},{8,13},{9,12},{10,... | collective-permute-start | bytes 24584 | tf_op jit(solution)/shard_map/ppermute | solution.py:449
  18.4 3.2 %collective-permute-start.5 = (f32[32,128]{1,0:T(8,128)S(1)}, f32[32,128]{1,0:T(8,128)S(1)}, u32[]{:S(2)}, u32[]{:S(2)}) collective-permute-start(f32[32,128]{1,0:T(8,128)S(1)} %pad_maximum_fusion.3), channel_id=1, source_target_pairs={{0,3},{1,2},{2,1},{3,0},{4,7},{5,6},{6,5},{7,4},{8,11},{9,10},{10,... | collective-permute-start | bytes 49160 | tf_op jit(solution)/shard_map/ppermute | solution.py:449
  21.7 1.2 %collective-permute-start.6 = (f32[64,128]{1,0:T(8,128)S(1)}, f32[64,128]{1,0:T(8,128)S(1)}, u32[]{:S(2)}, u32[]{:S(2)}) collective-permute-start(f32[64,128]{1,0:T(8,128)S(1)} %pad_maximum_fusion.2), channel_id=1, source_target_pairs={{0,1},{1,0},{2,3},{3,2},{4,5},{5,4},{6,7},{7,6},{8,9},{9,8},{10,11... | collective-permute-start | bytes 98312 | tf_op jit(solution)/shard_map/ppermute | solution.py:449

commit v8 on v6

--- a/solution.py
+++ b/solution.py
@@ -393,17 +393,18 @@
         return pltpu.make_async_copy(staged.at[:, span], out_ref.at[:, span], sems.at[g])
 
     def finish(g):
-        part = window[2 * g : 2 * g + 2].reshape(2 * rows, 4 * LANES)
+        part = window[4 * g : 4 * g + 4].reshape(4 * rows, 4 * LANES)
         band = band_ref[...]
         both = jnp.dot(part, jnp.concatenate([band, band], axis=0), preferred_element_type=F32)
-        for t in (2 * g, 2 * g + 1):
-            fine = both[(t % 2) * rows : (t % 2 + 1) * rows]
+        for t in range(4 * g, 4 * g + 4):
+            fine = both[(t % 4) * rows : (t % 4 + 1) * rows]
             coarse = expand(ring_ref, t)[1 : 1 + cells] + expand(last_ref, t)[1 : 1 + cells]
             for i in range(cells):
                 at = slice(i * BS, (i + 1) * BS)
                 value = dose_ref[t, at, :] - fine[at, :LANES] - fine[at, LANES:] - coarse[i : i + 1, :]
                 staged[at, t * LANES : (t + 1) * LANES] = value
-        copy(g).start()
+            if t % 2:
+                copy(t // 2).start()
 
     def stage(body):
         body()
@@ -415,18 +416,12 @@
             fill(t)
 
     stage(start)
-    for g in range(tiles // 2):
-
-        def step(g=g):
-            if g:
-                finish(g - 1)
-            for t in range(2 * g + 1, 2 * g + 3):
-                if t > 2:
-                    fill(t)
-
-        if g:
-            stage(step)
-    stage(lambda: finish(tiles // 2 - 1))
+    for t in range(3, 5):
+        fill(t)
+    for g in range(tiles // 4):
+        for t in range(4 * g + 5, min(4 * g + 9, tiles + 1)):
+            fill(t)
+        finish(g)
     for g in range(tiles // 2):
         copy(g).wait()
 

time: 26.3 us -> 26.3 us (level)
  no operation moved by 1% of the time
where the time goes in v8:
time: 26.3 us; the launch traced here: 26.1 us
  Pallas kernels  11.6 us (44%)
  starting transfers between devices  11.4 us (43%)
  waiting for transfers between devices  2.99 us (11%)
    ppermute x7, starting transfers between devices, move(): lax.ppermute(value, ('row', 'col'), [(i, r * col_count + c) for i, (r, c)...  11.4 us
    pallas_call x6, Pallas kernels, call(): pl.pallas_call(kernel, out_shape=outs, in_specs=ins, out_specs=(VMEM,) *...  8.31 us
    pallas_call x1, Pallas kernels, shards(): pl.pallas_call(last_kernel, out_shape=shape(rows, cols), in_specs=[VMEM]...  3.33 us
    ppermute x7, waiting for transfers between devices, move(): lax.ppermute(value, ('row', 'col'), [(i, r * col_count + c) for i, (r, c)...  2.99 us
  transfers between devices with their start and end apart: 7, of which 4 were waited for; matrix products, arithmetic and copies ran while one was open for 0% of the time, Pallas kernels for 25%

profile of v8, /device:TPU:0, one launch (start us, length us, event | category | flops | bytes accessed | tf_op | source)
XLA Modules:
  0.0 26.1 jit_solution(7988381064191888797)
XLA Ops:
  0.0 0.0 copy-start
  0.0 1.1 %edges.1 = (f32[272,128]{1,0:T(8,128)S(1)}, f32[16,8,128]{2,1,0:T(8,128)S(1)}, f32[16,8,128]{2,1,0:T(8,128)S(1)}, f32[8,8]{1,0:T(8,128)S(1)}, f32[16,16]{1,0:T(8,128)S(1)}) custom-call(s32[256,2048]{1,0:T(8,128)} %cov_ref.3, f32[8,8]{1,0:T(8,128)} %fog_rows_ref.1, f32[16,16]{1,0:T(8,128)} %fog_cols_ref.1), custom_call_target="tpu_custom_call" | custom-call | flops 524288 | bytes 524288 | tf_op jit(solution)/shard_map/edges/pallas_call | solution.py:449
  1.2 0.6 %collective-permute-start = (f32[272,128]{1,0:T(8,128)S(1)}, f32[272,128]{1,0:T(8,128)S(1)}, u32[]{:S(2)}, u32[]{:S(2)}) collective-permute-start(f32[272,128]{1,0:T(8,128)S(1)} %get-tuple-element.37), channel_id=1, source_target_pairs={{0,1},{1,0},{2,3},{3,2},{4,5},{5,4},{6,7},{7,6},{8,9},{9,8},{10,11... | collective-permute-start | bytes 417800 | tf_op jit(solution)/shard_map/ppermute | solution.py:443
  1.7 0.6 %prep.1 = (bf16[256,256]{1,0:T(8,128)(2,1)S(1)}, bf16[2048,128]{1,0:T(8,128)(2,1)S(1)}, f32[64,128]{1,0:T(8,128)S(1)}, f32[16,128]{1,0:T(8,128)S(1)}, f32[128,256]{1,0:T(8,128)S(1)}) custom-call(f32[8,8]{1,0:T(8,128)S(1)} %get-tuple-element.38.fog_rows_ref, f32[16,16]{1,0:T(8,128)S(1)} %get-tuple-element.39.fog_cols_ref), custom_call_target="tpu_custom_call" | custom-call | flops 524288 | bytes 524288 | tf_op jit(solution)/shard_map/prep/pallas_call | solution.py:449
  2.3 0.4 %collective-permute-done.side_ref = f32[272,128]{1,0:T(8,128)S(1)} collective-permute-done((f32[272,128]{1,0:T(8,128)S(1)}, f32[272,128]{1,0:T(8,128)S(1)}, u32[]{:S(2)}, u32[]{:S(2)}) %collective-permute-start) | collective-permute-done | bytes 139296 | tf_op jit(solution)/shard_map/ppermute | solution.py:443
  2.7 2.9 %collective-permute-start.1 = (f32[17,8,128]{2,1,0:T(8,128)S(1)}, f32[17,8,128]{2,1,0:T(8,128)S(1)}, u32[]{:S(2)}, u32[]{:S(2)}) collective-permute-start(f32[17,8,128]{2,1,0:T(8,128)S(1)} %pad_maximum_fusion), channel_id=1, source_target_pairs={{0,2},{1,3},{2,0},{3,1},{4,6},{5,7},{6,4},{7,5},{8,10},{9,11},{10,... | collective-permute-start | bytes 208904 | tf_op jit(solution)/shard_map/ppermute | solution.py:443
  5.7 0.0 collective-permute-start.2
  5.7 0.0 copy-done
  5.7 3.0 %block.1 = (f32[17,272,128]{2,1,0:T(8,128)S(1)}, f32[17,272,128]{2,1,0:T(8,128)S(1)}, f32[17,288,128]{2,1,0:T(8,128)S(1)}, f32[8,128]{1,0:T(8,128)S(1)}) custom-call(s32[256,2048]{1,0:T(8,128)S(1)} %copy-done, f32[272,128]{1,0:T(8,128)S(1)} %collective-permute-done.side_ref, bf16[256,256]{1,0:T(8,128)(2,1)S(1)} %get-tuple-element.43.band_ref, ...), custom_call_target="tpu_custom_call" | custom-call | flops 524288 | bytes 524288 | tf_op jit(solution)/shard_map/block/pallas_call | solution.py:449
  8.7 0.3 %collective-permute-done.1.first_ref = f32[17,8,128]{2,1,0:T(8,128)S(1)} collective-permute-done((f32[17,8,128]{2,1,0:T(8,128)S(1)}, f32[17,8,128]{2,1,0:T(8,128)S(1)}, u32[]{:S(2)}, u32[]{:S(2)}) %collective-permute-start.1) | collective-permute-done | bytes 69664 | tf_op jit(solution)/shard_map/ppermute | solution.py:443
  9.0 0.0 collective-permute-done.2.second_ref
  9.0 0.7 %outer.1 = (f32[17,272,128]{2,1,0:T(8,128)S(1)}, f32[17,272,128]{2,1,0:T(8,128)S(1)}, f32[8,128]{1,0:T(8,128)S(1)}) custom-call(f32[17,8,128]{2,1,0:T(8,128)S(1)} %collective-permute-done.1.first_ref, f32[17,8,128]{2,1,0:T(8,128)S(1)} %collective-permute-done.2.second_ref, ...), custom_call_target="tpu_custom_call", output_to_operand_aliasing={{0}: (6, {}), {1}: (7, {})} | custom-call | flops 524288 | bytes 524288 | tf_op jit(solution)/shard_map/outer/pallas_call | solution.py:449
  9.7 1.9 %collective-permute-start.3 = (f32[8,128]{1,0:T(8,128)S(1)}, f32[8,128]{1,0:T(8,128)S(1)}, u32[]{:S(2)}, u32[]{:S(2)}) collective-permute-start(f32[8,128]{1,0:T(8,128)S(1)} %get-tuple-element.49.after_ref), channel_id=1, source_target_pairs={{0,3},{1,2},{2,1},{3,0},{4,7},{5,6},{6,5},{7,4},{8,11},{9,10},{10,... | collective-permute-start | bytes 12296 | tf_op jit(solution)/shard_map/ppermute | solution.py:443
  11.6 1.4 %spread.1 = (f32[17,256,128]{2,1,0:T(8,128)S(1)}, f32[17,8,8,128]{3,2,1,0:T(8,128)S(1)}, f32[17,8,8,128]{3,2,1,0:T(8,128)S(1)}) custom-call(f32[17,272,128]{2,1,0:T(8,128)S(1)} %get-tuple-element.50.cover_ref, f32[8,128]{1,0:T(8,128)S(1)} %get-tuple-element.49.after_ref), custom_call_target="tpu_custom_call" | custom-call | flops 524288 | bytes 524288 | tf_op jit(solution)/shard_map/spread/pallas_call | solution.py:449
  13.0 0.0 collective-permute-done.3
  13.0 2.2 %collective-permute-start.4 = (f32[16,128]{1,0:T(8,128)S(1)}, f32[16,128]{1,0:T(8,128)S(1)}, u32[]{:S(2)}, u32[]{:S(2)}) collective-permute-start(f32[16,128]{1,0:T(8,128)S(1)} %get-tuple-element.69.after_ref), channel_id=1, source_target_pairs={{0,5},{1,4},{2,7},{3,6},{4,1},{5,0},{6,3},{7,2},{8,13},{9,12},{10,... | collective-permute-start | bytes 24584 | tf_op jit(solution)/shard_map/ppermute | solution.py:443
  15.2 1.5 %dose.1 = (f32[16,256,128]{2,1,0:T(8,128)S(1)}, f32[17,256,128]{2,1,0:T(8,128)S(1)}) custom-call(f32[17,272,128]{2,1,0:T(8,128)S(1)} %get-tuple-element.50.cover_ref, f32[17,272,128]{2,1,0:T(8,128)S(1)} %get-tuple-element.55.fine_ref, f32[16,128]{1,0:T(8,128)S(1)} %get-tuple-element.69.after_ref), custom_call_target="tpu_custom_call" | custom-call | flops 524288 | bytes 524288 | tf_op jit(solution)/shard_map/dose/pallas_call | solution.py:449
  16.7 0.0 collective-permute-done.4
  16.7 3.3 %collective-permute-start.5 = (f32[32,128]{1,0:T(8,128)S(1)}, f32[32,128]{1,0:T(8,128)S(1)}, u32[]{:S(2)}, u32[]{:S(2)}) collective-permute-start(f32[32,128]{1,0:T(8,128)S(1)} %pad_maximum_fusion.3), channel_id=1, source_target_pairs={{0,9},{1,8},{2,11},{3,10},{4,13},{5,12},{6,15},{7,14},{8,1},{9,0},... | collective-permute-start | bytes 49160 | tf_op jit(solution)/shard_map/ppermute | solution.py:443
  20.1 1.4 %collective-permute-done.5 = f32[32,128]{1,0:T(8,128)S(1)} collective-permute-done((f32[32,128]{1,0:T(8,128)S(1)}, f32[32,128]{1,0:T(8,128)S(1)}, u32[]{:S(2)}, u32[]{:S(2)}) %collective-permute-start.5) | collective-permute-done | bytes 16416 | tf_op jit(solution)/shard_map/ppermute | solution.py:443
  21.5 0.4 %collective-permute-start.6 = (f32[64,128]{1,0:T(8,128)S(1)}, f32[64,128]{1,0:T(8,128)S(1)}, u32[]{:S(2)}, u32[]{:S(2)}) collective-permute-start(f32[64,128]{1,0:T(8,128)S(1)} %pad_maximum_fusion.2), channel_id=1, source_target_pairs={{0,1},{1,0},{2,3},{3,2},{4,5},{5,4},{6,7},{7,6},{8,9},{9,8},{10,11... | collective-permute-start | bytes 98312 | tf_op jit(solution)/shard_map/ppermute | solution.py:443
  21.9 0.9 %collective-permute-done.6 = f32[64,128]{1,0:T(8,128)S(1)} collective-permute-done((f32[64,128]{1,0:T(8,128)S(1)}, f32[64,128]{1,0:T(8,128)S(1)}, u32[]{:S(2)}, u32[]{:S(2)}) %collective-permute-start.6) | collective-permute-done | bytes 32800 | tf_op jit(solution)/shard_map/ppermute | solution.py:443
  22.8 3.3 %last.1 = f32[256,2048]{1,0:T(8,128)} custom-call(f32[128,128]{1,0:T(8,128)S(1)} %constant_dynamic-update-slice_fusion.2.gathered_ref, f32[64,128]{1,0:T(8,128)S(1)} %get-tuple-element.59.left_ref, f32[16,128]{1,0:T(8,128)S(1)} %get-tuple-element.60.own_ref, f32[128,256]{1,0:T(8,128)S(1)} %get-tuple-element.61.right_ref, ...), custom_call_target="tpu_custom_call" | custom-call | tf_op jit(solution)/shard_map/last/pallas_call | solution.py:587
  (10 shorter events, 0.0 us)
Async XLA Ops:
  0.0 5.7 %copy-start = (s32[256,2048]{1,0:T(8,128)S(1)}, s32[256,2048]{1,0:T(8,128)}, u32[]{:S(2)}) copy-start(s32[256,2048]{1,0:T(8,128)} %cov_ref.3) | copy-start | bytes 6291460
  1.2 1.6 %collective-permute-start = (f32[272,128]{1,0:T(8,128)S(1)}, f32[272,128]{1,0:T(8,128)S(1)}, u32[]{:S(2)}, u32[]{:S(2)}) collective-permute-start(f32[272,128]{1,0:T(8,128)S(1)} %get-tuple-element.37), channel_id=1, source_target_pairs={{0,1},{1,0},{2,3},{3,2},{4,5},{5,4},{6,7},{7,6},{8,9},{9,8},{10,11... | collective-permute-start | bytes 417800 | tf_op jit(solution)/shard_map/ppermute | solution.py:443
  2.7 6.3 %collective-permute-start.1 = (f32[17,8,128]{2,1,0:T(8,128)S(1)}, f32[17,8,128]{2,1,0:T(8,128)S(1)}, u32[]{:S(2)}, u32[]{:S(2)}) collective-permute-start(f32[17,8,128]{2,1,0:T(8,128)S(1)} %pad_maximum_fusion), channel_id=1, source_target_pairs={{0,2},{1,3},{2,0},{3,1},{4,6},{5,7},{6,4},{7,5},{8,10},{9,11},{10,... | collective-permute-start | bytes 208904 | tf_op jit(solution)/shard_map/ppermute | solution.py:443
  5.7 3.4 %collective-permute-start.2 = (f32[17,8,128]{2,1,0:T(8,128)S(1)}, f32[17,8,128]{2,1,0:T(8,128)S(1)}, u32[]{:S(2)}, u32[]{:S(2)}) collective-permute-start(f32[17,8,128]{2,1,0:T(8,128)S(1)} %pad_maximum_fusion.1), channel_id=1, source_target_pairs={{0,1},{1,0},{2,4},{3,5},{4,2},{5,3},{6,8},{7,9},{8,6},{9,7},{10,12... | collective-permute-start | bytes 208904 | tf_op jit(solution)/shard_map/ppermute | solution.py:443
  9.7 3.3 %collective-permute-start.3 = (f32[8,128]{1,0:T(8,128)S(1)}, f32[8,128]{1,0:T(8,128)S(1)}, u32[]{:S(2)}, u32[]{:S(2)}) collective-permute-start(f32[8,128]{1,0:T(8,128)S(1)} %get-tuple-element.49.after_ref), channel_id=1, source_target_pairs={{0,3},{1,2},{2,1},{3,0},{4,7},{5,6},{6,5},{7,4},{8,11},{9,10},{10,... | collective-permute-start | bytes 12296 | tf_op jit(solution)/shard_map/ppermute | solution.py:443
  13.0 3.7 %collective-permute-start.4 = (f32[16,128]{1,0:T(8,128)S(1)}, f32[16,128]{1,0:T(8,128)S(1)}, u32[]{:S(2)}, u32[]{:S(2)}) collective-permute-start(f32[16,128]{1,0:T(8,128)S(1)} %get-tuple-element.69.after_ref), channel_id=1, source_target_pairs={{0,5},{1,4},{2,7},{3,6},{4,1},{5,0},{6,3},{7,2},{8,13},{9,12},{10,... | collective-permute-start | bytes 24584 | tf_op jit(solution)/shard_map/ppermute | solution.py:443
  16.7 4.8 %collective-permute-start.5 = (f32[32,128]{1,0:T(8,128)S(1)}, f32[32,128]{1,0:T(8,128)S(1)}, u32[]{:S(2)}, u32[]{:S(2)}) collective-permute-start(f32[32,128]{1,0:T(8,128)S(1)} %pad_maximum_fusion.3), channel_id=1, source_target_pairs={{0,9},{1,8},{2,11},{3,10},{4,13},{5,12},{6,15},{7,14},{8,1},{9,0},... | collective-permute-start | bytes 49160 | tf_op jit(solution)/shard_map/ppermute | solution.py:443
  21.5 1.3 %collective-permute-start.6 = (f32[64,128]{1,0:T(8,128)S(1)}, f32[64,128]{1,0:T(8,128)S(1)}, u32[]{:S(2)}, u32[]{:S(2)}) collective-permute-start(f32[64,128]{1,0:T(8,128)S(1)} %pad_maximum_fusion.2), channel_id=1, source_target_pairs={{0,1},{1,0},{2,3},{3,2},{4,5},{5,4},{6,7},{7,6},{8,9},{9,8},{10,11... | collective-permute-start | bytes 98312 | tf_op jit(solution)/shard_map/ppermute | solution.py:443
